TPU v7x, 32 devices: a whole 2x2x4 slice. The times are simulated.
32 devices in a mesh: shard: 2 (over x), ctx: 4 (over z), tensor: 4 (over y, core).
Axes of the slice: x: 2, y: 2, z: 4, core: 2. Of those that a mesh axis runs over, the one named last changes fastest.
Arguments:
- inputs: bfloat16 [1024, 8, 1024], P('ctx', 'shard'), may hold values from -6 to 6
- time_features: bfloat16 [8, 256], P('shard'), may hold values from -1 to 1
- valid_mask: int32 [1024, 8], P('ctx', 'shard'), may hold values from 0 to 1, as said below
- teacher: bfloat16 [1024, 8, 1024], P('ctx', 'shard'), may hold values from -6 to 6
- w_time: bfloat16 [256, 1024], replicated, may hold values from -0.375 to 0.375
- b_time: float32 [1024], replicated, may hold values from -2 to 2
- w_query: bfloat16 [1024, 1024], P('shard', 'tensor'), may hold values from -0.1875 to 0.1875
- b_query: float32 [1024], P('tensor'), may hold values from -2 to 2
- w_key: bfloat16 [1024, 1024], P('shard', 'tensor'), may hold values from -0.1875 to 0.1875
- w_value: bfloat16 [1024, 1024], P('shard', 'tensor'), may hold values from -0.1875 to 0.1875
- b_value: float32 [1024], P('tensor'), may hold values from -0.3 to 0.3
- w_output: bfloat16 [1024, 1024], P('shard', 'tensor'), may hold values from -1.5 to 1.5
- b_output: float32 [1024], replicated, may hold values from -2 to 2
- gain_one: float32 [1024], replicated, may hold values from 0.5 to 1.5
- shift_one: float32 [1024], replicated, may hold values from -2 to 2
- w_hidden: bfloat16 [1024, 4096], P('shard', 'tensor'), may hold values from -0.1875 to 0.1875
- b_hidden: float32 [4096], P('tensor'), may hold values from -2 to 2
- w_down: bfloat16 [1024, 4096], P('shard', 'tensor'), may hold values from -0.09375 to 0.09375
- b_down: float32 [1024], replicated, may hold values from -2 to 2
- gain_two: float32 [1024], replicated, may hold values from 0.5 to 1.5
- shift_two: float32 [1024], replicated, may hold values from -2 to 2
Outputs:
- layer_out: bfloat16 [1024, 8, 1024], P('ctx', 'shard')
- loss: float32 [], replicated
- grad_inputs: float32 [1024, 8, 1024], P('ctx', 'shard')
- grad_w_time: float32 [256, 1024], replicated
- grad_b_time: float32 [1024], replicated
- grad_w_query: float32 [1024, 1024], P(('shard', 'ctx'), 'tensor')
- grad_b_query: float32 [1024], P('tensor')
- grad_w_key: float32 [1024, 1024], P(('shard', 'ctx'), 'tensor')
- grad_w_value: float32 [1024, 1024], P(('shard', 'ctx'), 'tensor')
- grad_b_value: float32 [1024], P('tensor')
- grad_w_output: float32 [1024, 1024], P(('shard', 'ctx'), 'tensor')
- grad_b_output: float32 [1024], replicated
- grad_gain_one: float32 [1024], replicated
- grad_shift_one: float32 [1024], replicated
- grad_w_hidden: float32 [1024, 4096], P(('shard', 'ctx'), 'tensor')
- grad_b_hidden: float32 [4096], P('tensor')
- grad_w_down: float32 [1024, 4096], P(('shard', 'ctx'), 'tensor')
- grad_b_down: float32 [1024], replicated
- grad_gain_two: float32 [1024], replicated
- grad_shift_two: float32 [1024], replicated
Inputs may be any that keep to these rules, and one draw needn't show every extreme that they name: `valid_mask`: 0 or 1; the last token of every sequence is valid.
All inputs are finite; a program needn't handle non-finite values.
Results may differ from a plain program's by a relative error of at most 0.018.
Values may be sent and summed in bfloat16 or wider, within the bound.
No kernel may reach another device: no remote copies, remote signals or barrier semaphores. Data moves between devices by JAX's collectives and lax.ppermute only.
A program may use at most 256 MiB of HBM per device.

v0:
```python
from functools import partial
import math

import jax
import jax.numpy as jnp
from jax import lax
from jax.sharding import PartitionSpec as P

D = 1024
HEADS = 16


def layer_norm(value, gain, shift):
    center = jnp.mean(value, axis=-1, keepdims=True)
    offset = value - center
    spread = jnp.mean(offset * offset, axis=-1, keepdims=True)
    return offset * lax.rsqrt(spread + 1e-05) * gain + shift


def contract(left, right, left_dim, right_dim):
    return lax.dot_general(
        left, right, (((left_dim,), (right_dim,)), ((), ())), preferred_element_type=jnp.float32
    )


def block_rows(length):
    return math.gcd(length, 512)


def score_block(queries, keys, scale):
    return jnp.einsum("qshd,kshd->qshk", queries, keys, preferred_element_type=jnp.float32) * scale


def fold_block(carry, keys, values, queries, scale):
    peak, total, summed = carry
    scores = score_block(queries, keys, scale)
    new_peak = jnp.maximum(peak, jnp.max(scores, axis=-1))
    fade = jnp.exp(peak - new_peak)
    weights = jnp.exp(scores - new_peak[..., None])
    total = total * fade + jnp.sum(weights, axis=-1)
    summed = summed * fade[..., None] + jnp.einsum(
        "qshk,kshd->qshd", weights.astype(jnp.bfloat16), values, preferred_element_type=jnp.float32
    )
    return (new_peak, total, summed)


def fold_keys(carry, piece, start, queries, scale):
    keys, values = piece
    length, seqs, width = keys.shape
    heads = queries.shape[2]
    head_size = width // heads
    block = block_rows(length)
    blocks = length // block
    keys = keys.reshape(blocks, block, seqs, heads, head_size)
    values = values.reshape(blocks, block, seqs, heads, head_size)

    def step(inner, pair):
        return (fold_block(inner, pair[0], pair[1], queries, scale), None)

    carry, unused = lax.scan(step, carry, (keys, values))
    return carry


def score_grads(keys, values, queries, out_grad, logsum, delta, scale):
    scores = score_block(queries, keys, scale)
    weights = jnp.exp(scores - logsum[..., None])
    weight_grad = jnp.einsum(
        "qshd,kshd->qshk", out_grad, values, preferred_element_type=jnp.float32
    )
    score_grad = (weights * (weight_grad - delta[..., None])).astype(jnp.bfloat16)
    return (weights, score_grad)


def pair_grads(keys, values, queries, out_grad, logsum, delta, scale):
    block, seqs = (keys.shape[0], keys.shape[1])
    weights, score_grad = score_grads(keys, values, queries, out_grad, logsum, delta, scale)
    value_grad = jnp.einsum(
        "qshk,qshd->kshd",
        weights.astype(jnp.bfloat16),
        out_grad,
        preferred_element_type=jnp.float32,
    )
    key_grad = (
        jnp.einsum("qshk,qshd->kshd", score_grad, queries, preferred_element_type=jnp.float32)
        * scale
    )
    joined = jnp.concatenate(
        [key_grad.reshape(block, seqs, -1), value_grad.reshape(block, seqs, -1)], axis=-1
    )
    return (score_grad, joined)


def back_block(query_grad, pair, queries, out_grad, logsum, delta, scale):
    keys, values = pair
    score_grad, joined = pair_grads(keys, values, queries, out_grad, logsum, delta, scale)
    query_grad = (
        query_grad
        + jnp.einsum("qshk,kshd->qshd", score_grad, keys, preferred_element_type=jnp.float32)
        * scale
    )
    return (query_grad, joined)


def body(
    inputs,
    time_features,
    valid_mask,
    teacher,
    w_time,
    b_time,
    w_query,
    b_query,
    w_key,
    w_value,
    b_value,
    w_output,
    b_output,
    gain_one,
    shift_one,
    w_hidden,
    b_hidden,
    w_down,
    b_down,
    gain_two,
    shift_two,
):
    positions, seqs, width = inputs.shape
    rows_local = positions * seqs
    head_size = D // HEADS
    scale = 1.0 / math.sqrt(head_size)
    embed = jnp.dot(time_features, w_time, preferred_element_type=jnp.float32) + b_time
    start = (inputs.astype(jnp.float32) + embed[None]).reshape(rows_local, width)
    start_low = start.astype(jnp.bfloat16)
    full_query, full_key, full_value, full_output = (
        lax.all_gather(w_query, "shard", axis=0, tiled=True),
        lax.all_gather(w_key, "shard", axis=0, tiled=True),
        lax.all_gather(w_value, "shard", axis=0, tiled=True),
        lax.all_gather(w_output, "shard", axis=0, tiled=True),
    )
    columns = full_query.shape[1]
    heads = columns // head_size
    query_low = (
        jnp.dot(start_low, full_query, preferred_element_type=jnp.float32) + b_query
    ).astype(jnp.bfloat16)
    key_low = jnp.dot(start_low, full_key, preferred_element_type=jnp.float32).astype(jnp.bfloat16)
    value_low = (
        jnp.dot(start_low, full_value, preferred_element_type=jnp.float32) + b_value
    ).astype(jnp.bfloat16)
    queries = query_low.reshape(positions, seqs, heads, head_size)
    key_local = key_low.reshape(positions, seqs, columns)
    value_local = value_low.reshape(positions, seqs, columns)
    initial = (
        jnp.full((positions, seqs, heads), -1e30, jnp.float32),
        jnp.zeros((positions, seqs, heads), jnp.float32),
        jnp.zeros((positions, seqs, heads, head_size), jnp.float32),
    )
    folder = partial(fold_keys, queries=queries, scale=scale)
    peak, total, summed = folder(
        initial,
        (
            lax.all_gather(key_local, "ctx", axis=0, tiled=True),
            lax.all_gather(value_local, "ctx", axis=0, tiled=True),
        ),
        jnp.int32(0),
    )
    attended = summed / total[..., None]
    logsum = peak + jnp.log(total)
    mixed_low = attended.reshape(rows_local, columns).astype(jnp.bfloat16)
    branch_part = contract(mixed_low, full_output, 1, 1)
    branch = lax.psum(branch_part.astype(jnp.bfloat16), "tensor").astype(jnp.float32) + b_output
    normed, norm_back_one = jax.vjp(layer_norm, start + branch, gain_one, shift_one)
    normed_low = normed.astype(jnp.bfloat16)
    full_hidden, full_down = (
        lax.all_gather(w_hidden, "shard", axis=0, tiled=True),
        lax.all_gather(w_down, "shard", axis=0, tiled=True),
    )
    pre_act = jnp.dot(normed_low, full_hidden, preferred_element_type=jnp.float32) + b_hidden
    hidden, gelu_back = jax.vjp(partial(jax.nn.gelu, approximate=False), pre_act)
    hidden_low = hidden.astype(jnp.bfloat16)
    feed_part = contract(hidden_low, full_down, 1, 1)
    feed = lax.psum(feed_part.astype(jnp.bfloat16), "tensor").astype(jnp.float32) + b_down
    result, norm_back_two = jax.vjp(layer_norm, normed + feed, gain_two, shift_two)
    layer_out = result.astype(jnp.bfloat16).reshape(positions, seqs, width)
    valid = valid_mask.astype(jnp.float32).reshape(rows_local)
    error = result - teacher.reshape(rows_local, width).astype(jnp.float32)
    squares_local = jnp.sum(valid[:, None] * error * error)
    squares_total, count = lax.psum((squares_local, jnp.sum(valid)), ("shard", "ctx"))
    loss = squares_total / (D * count)
    tokens_all = rows_local * lax.axis_size("ctx") * lax.axis_size("shard")
    result_grad = 2.0 * tokens_all / count * valid[:, None] * error
    sum_grad, grad_gain_two, grad_shift_two = norm_back_two(result_grad)
    feed_low = sum_grad.astype(jnp.bfloat16)
    grad_down = contract(feed_low, hidden_low, 0, 0)
    hidden_grad = jnp.dot(feed_low, full_down, preferred_element_type=jnp.float32)
    pre_grad = gelu_back(hidden_grad)[0].astype(jnp.bfloat16)
    grad_hidden = contract(normed_low, pre_grad, 0, 0)
    normed_part = contract(pre_grad, full_hidden, 1, 1)
    normed_grad = sum_grad + lax.psum(normed_part.astype(jnp.bfloat16), "tensor").astype(
        jnp.float32
    )
    first_grad, grad_gain_one, grad_shift_one = norm_back_one(normed_grad)
    branch_low = first_grad.astype(jnp.bfloat16)
    grad_output = contract(branch_low, mixed_low, 0, 0)
    mixed_grad = jnp.dot(branch_low, full_output, preferred_element_type=jnp.float32).astype(
        jnp.bfloat16
    )
    out_grad = mixed_grad.reshape(positions, seqs, heads, head_size)
    delta = jnp.sum(out_grad.astype(jnp.float32) * attended, axis=-1)
    all_keys, all_values = (
        lax.all_gather(key_local, "ctx", axis=0, tiled=True),
        lax.all_gather(value_local, "ctx", axis=0, tiled=True),
    )
    length = all_keys.shape[0]
    block = block_rows(length)
    key_blocks = all_keys.reshape(length // block, block, seqs, heads, head_size)
    value_blocks = all_values.reshape(length // block, block, seqs, heads, head_size)
    query_zero = jnp.zeros((positions, seqs, heads, head_size), jnp.float32)
    back_step = partial(
        back_block, queries=queries, out_grad=out_grad, logsum=logsum, delta=delta, scale=scale
    )
    query_grad, joined = lax.scan(back_step, query_zero, (key_blocks, value_blocks))
    joined = joined.reshape(length, seqs, 2 * columns)
    owned = lax.psum_scatter(
        joined.astype(jnp.bfloat16), "ctx", scatter_dimension=0, tiled=True
    ).astype(jnp.float32)
    key_grad_low = owned[:, :, :columns].reshape(rows_local, columns).astype(jnp.bfloat16)
    value_grad_low = owned[:, :, columns:].reshape(rows_local, columns).astype(jnp.bfloat16)
    query_grad_low = query_grad.reshape(rows_local, columns).astype(jnp.bfloat16)
    grad_query = contract(start_low, query_grad_low, 0, 0)
    grad_key = contract(start_low, key_grad_low, 0, 0)
    grad_value = contract(start_low, value_grad_low, 0, 0)
    start_part = (
        contract(query_grad_low, full_query, 1, 1)
        + contract(key_grad_low, full_key, 1, 1)
        + contract(value_grad_low, full_value, 1, 1)
    )
    start_grad = first_grad + lax.psum(start_part.astype(jnp.bfloat16), "tensor").astype(
        jnp.float32
    )
    grad_inputs = start_grad.reshape(positions, seqs, width)
    embed_grad = jnp.sum(grad_inputs, axis=0)
    time_grad = jnp.dot(
        time_features.astype(jnp.float32).T, embed_grad, precision=lax.Precision.HIGHEST
    )
    (
        grad_w_time,
        grad_b_time,
        grad_b_query,
        grad_b_value,
        grad_b_output,
        grad_gain_one,
        grad_shift_one,
        grad_b_hidden,
        grad_b_down,
        grad_gain_two,
        grad_shift_two,
    ) = lax.psum(
        (
            time_grad,
            jnp.sum(embed_grad, axis=0),
            jnp.sum(query_grad_low.astype(jnp.float32), axis=0),
            jnp.sum(value_grad_low.astype(jnp.float32), axis=0),
            jnp.sum(branch_low.astype(jnp.float32), axis=0),
            grad_gain_one,
            grad_shift_one,
            jnp.sum(pre_grad.astype(jnp.float32), axis=0),
            jnp.sum(feed_low.astype(jnp.float32), axis=0),
            grad_gain_two,
            grad_shift_two,
        ),
        ("shard", "ctx"),
    )
    grad_w_query, grad_w_key, grad_w_value, grad_w_output, grad_w_hidden, grad_w_down = (
        lax.psum_scatter(grad_query, ("shard", "ctx"), scatter_dimension=0, tiled=True),
        lax.psum_scatter(grad_key, ("shard", "ctx"), scatter_dimension=0, tiled=True),
        lax.psum_scatter(grad_value, ("shard", "ctx"), scatter_dimension=0, tiled=True),
        lax.psum_scatter(grad_output, ("shard", "ctx"), scatter_dimension=0, tiled=True),
        lax.psum_scatter(grad_hidden, ("shard", "ctx"), scatter_dimension=0, tiled=True),
        lax.psum_scatter(grad_down, ("shard", "ctx"), scatter_dimension=0, tiled=True),
    )
    return (
        layer_out,
        loss,
        grad_inputs,
        grad_w_time,
        grad_b_time,
        grad_w_query,
        grad_b_query,
        grad_w_key,
        grad_w_value,
        grad_b_value,
        grad_w_output,
        grad_b_output,
        grad_gain_one,
        grad_shift_one,
        grad_w_hidden,
        grad_b_hidden,
        grad_w_down,
        grad_b_down,
        grad_gain_two,
        grad_shift_two,
    )


def solution(mesh):
    placed = (
        P("ctx", "shard", None),
        P("shard", None),
        P("ctx", "shard"),
        P("ctx", "shard", None),
        P(),
        P(),
        P("shard", "tensor"),
        P("tensor"),
        P("shard", "tensor"),
        P("shard", "tensor"),
        P("tensor"),
        P("shard", "tensor"),
        P(),
        P(),
        P(),
        P("shard", "tensor"),
        P("tensor"),
        P("shard", "tensor"),
        P(),
        P(),
        P(),
    )
    return jax.shard_map(
        body,
        mesh=mesh,
        in_specs=placed,
        out_specs=(
            P("ctx", "shard", None),
            P(),
            P("ctx", "shard", None),
            P(),
            P(),
            P(("shard", "ctx"), "tensor"),
            P("tensor"),
            P(("shard", "ctx"), "tensor"),
            P(("shard", "ctx"), "tensor"),
            P("tensor"),
            P(("shard", "ctx"), "tensor"),
            P(),
            P(),
            P(),
            P(("shard", "ctx"), "tensor"),
            P("tensor"),
            P(("shard", "ctx"), "tensor"),
            P(),
            P(),
            P(),
        ),
        check_vma=False,
    )
```

profile of v0, /device:TPU:0, one launch (start us, length us, event | category | flops | bytes accessed | tf_op | source)
XLA Modules:
  0.0 1141.1 jit_solution(9354903953610810085)
XLA Ops:
  10.0 5.7 fusion.56
  15.6 5.3 reshape.180
  21.0 10.0 all_gather.26
  31.0 3.1 convolution_convert_fusion.4
  35.5 8.2 all_gather.29
  44.4 3.0 fusion.55
  48.8 7.4 all_gather.28
  56.2 3.1 fusion.54
  60.6 7.3 all_gather.31
  67.9 15.4 %all-gather.5.cloned.1.call-done = bf16[1024,4,256]{0,2,1:T(8,128)(2,1)} async-done(((bf16[256,4,256]{0,2,1:T(8,128)(2,1)}), bf16[1024,4,256]{0,2,1:T(8,128)(2,1)}) %all-gather.5.cloned.1.call-update) | async-done | bytes 2097168 | tf_op jit(solution)/shard_map/all_gather | solution.py:161
  83.3 4.5 reshape.182
  89.8 40.1 %all-gather.7.cloned.1.call-done = bf16[1024,4,256]{0,2,1:T(8,128)(2,1)} async-done(((bf16[256,4,256]{0,2,1:T(8,128)(2,1)}), bf16[1024,4,256]{0,2,1:T(8,128)(2,1)}) %all-gather.7.cloned.1.call-update) | async-done | bytes 2097168 | tf_op jit(solution)/shard_map/all_gather | solution.py:162
  130.0 4.5 reshape.185
  134.4 3.4 copy.84
  137.8 28.7 %while.28 = (s32[]{:T(128)}, f32[256,4,4]{0,2,1:T(4,128)S(1)}, f32[256,4,4]{0,2,1:T(4,128)S(1)}, f32[256,4,4,64]{0,3,2,1:T(8,128)}, bf16[2,512,4,4,64]{1,4,3,2,0...) while((s32[]{:T(128)}, f32[256,4,4]{0,2,1:T(4,128)S(1)}, ...), condition=%wide.region_3.4_spmd.clone, body=%wide.region_0.3_spmd.clone.sunk | while | flops 554455040 | bytes 63701640 | solution.py:60
  137.8 4.5 bitcast_reduce_fusion.2
  142.3 5.0 fusion.146
  148.1 3.9 fusion.148
  152.0 4.5 bitcast_reduce_fusion.2
  156.5 5.0 fusion.146
  162.3 4.2 fusion.148
  166.7 2.9 copy.86
  169.6 3.3 fusion.62
  172.8 2.8 convert_element_type.150
  175.6 3.3 convolution_convert_fusion.2
  180.3 48.4 %all-reduce.7.cloned.1.call-done = bf16[1024,1024]{1,0:T(8,128)(2,1)} async-done(((bf16[1024,1024]{1,0:T(8,128)(2,1)}), bf16[1024,1024]{1,0:T(8,128)(2,1)}) %all-reduce.7.cloned.1.call-update) | async-done | bytes 2097168 | tf_op jit(solution)/shard_map/psum | solution.py:170
  228.7 3.5 fusion.74
  234.7 15.7 %multiply_convert_fusion = (bf16[1024,1024]{1,0:T(8,128)(2,1)}, f32[1024,1024]{1,0:T(8,128)}, f32[1024,1024]{1,0:T(8,128)}) fusion(f32[1024]{0:T(1024)S(1)} %copy-done.47, bf16[1024,1024]{1,0:T(8,128)(2,1)} %all-gather.9.cloned.1.call-done, f32[1024,1024]{1,0:T(8,128)} %copy-done.4, f32[1024]{0:T(1024)S(1)} %copy-done.42, f32[1024]{0:T(1024)S(1)} %copy-done.32, ...), kind=kOutput, calls=%fused_computation.69 | convolution fusion | flops 2221932544 | bytes 16797696 | tf_op jit(solution)/shard_map/dot_general | solution.py:177
  250.4 5.9 convolution_convert_fusion.1
  257.0 22.5 %psum.122 = f32[]{:T(128)} all-reduce(f32[]{:T(128)} %convert_reduce_fusion.5), channel_id=1, replica_groups=mesh['shard'=2,'ctx'=4,'tensor'=4] {'shard','ctx'}, use_global_device_ids=true, to_apply=%region_13.14 | all-reduce | flops 1 | bytes 8 | tf_op jit(solution)/shard_map/psum | solution.py:187
  279.8 4.3 reshape.189
  284.8 23.2 %all-reduce.9.cloned.1.call-done = bf16[1024,1024]{1,0:T(8,128)(2,1)} async-done(((bf16[1024,1024]{1,0:T(8,128)(2,1)}), bf16[1024,1024]{1,0:T(8,128)(2,1)}) %all-reduce.9.cloned.1.call-update) | async-done | bytes 2097168 | tf_op jit(solution)/shard_map/psum | solution.py:181
  308.0 3.7 fusion.72
  313.9 5.5 multiply_reduce_fusion
  326.5 3.6 convert_reduce_fusion.1
  331.4 3.7 convolution_convert_fusion
  335.4 51.3 %all-reduce.11.cloned.1.call-done = bf16[1024,1024]{1,0:T(8,128)(2,1)} async-done(((bf16[1024,1024]{1,0:T(8,128)(2,1)}), bf16[1024,1024]{1,0:T(8,128)(2,1)}) %all-reduce.11.cloned.1.call-update) | async-done | bytes 2097168 | tf_op jit(solution)/shard_map/psum | solution.py:198
  386.8 5.2 multiply_reduce_fusion.1
  401.3 2.8 reshape.187
  404.0 7.8 multiply_reduce_fusion.7
  414.7 25.0 %while.29 = (s32[]{:T(128)}, f32[256,4,4,64]{0,3,2,1:T(8,128)}, bf16[2,512,4,512]{1,3,2,0:T(8,128)(2,1)}, bf16[2,512,4,4,64]{1,4,3,2,0:T(8,128)(2,1)S(1)}, bf16[...) while((s32[]{:T(128)}, f32[256,4,4,64]{0,3,2,1:T(8,128)}, ...), condition=%wide.region_21.22_spmd.clone, body=%wide.region_20.21_spmd.clone.sunk | while | flops 1364983808 | bytes 76595896 | solution.py:221
  423.1 4.0 fusion.161
  435.5 4.3 fusion.161
  439.7 7.3 copy.94
  450.1 2.8 fusion.76
  452.8 71.2 %reduce-scatter.8.cloned.1.call-done = bf16[256,4,512]{2,0,1:T(8,128)(2,1)} async-done(((bf16[1024,4,512]{2,0,1:T(8,128)(2,1)}), bf16[256,4,512]{2,0,1:T(8,128)(2,1)}) %reduce-scatter.8.cloned.1.call-update) | async-done | bytes 1048592 | tf_op jit(solution)/shard_map/reduce_scatter | solution.py:223
  530.0 5.5 add_convert_fusion
  535.6 52.0 %all-reduce.13.cloned.1.call-done = bf16[1024,1024]{1,0:T(8,128)(2,1)} async-done(((bf16[1024,1024]{1,0:T(8,128)(2,1)}), bf16[1024,1024]{1,0:T(8,128)(2,1)}) %all-reduce.13.cloned.1.call-update) | async-done | bytes 2097168 | tf_op jit(solution)/shard_map/psum | solution.py:237
  587.6 5.4 fusion.68
  593.0 5.2 reshape.188
  598.2 2.9 reduce_sum.252
  602.8 3.3 fusion.79
  608.2 3.4 fusion.78
  611.7 7.5 fusion.63
  619.5 6.6 fusion.80
  628.8 3.3 convolution_bitcast_fusion
  632.3 3.5 convolution_bitcast_fusion.1
  638.8 38.8 %all-reduce = (f32[]{:T(128)}, f32[1024]{0:T(1024)}, f32[256]{0:T(256)}, f32[256]{0:T(256)}, f32[1024]{0:T(1024)}, /*index=5*/f32[1024]{0:T(1024)}, f32[1024]{0:...) all-reduce(f32[]{:T(128)} %get-tuple-element.280, ...), channel_id=1, replica_groups=mesh['shard'=2,'ctx'=4,'tensor'=4] {'shard','ctx'}, use_global_device_ids=true, to_apply=%region_11.12 | all-reduce | flops 8705 | bytes 69640 | tf_op jit(solution)/shard_map/psum | solution.py:187
  683.5 64.4 %reduce-scatter.16.cloned.1.call-done = f32[128,256]{1,0:T(8,128)} async-done(((f32[1024,256]{1,0:T(8,128)}), f32[128,256]{1,0:T(8,128)}) %reduce-scatter.16.cloned.1.call-update) | async-done | bytes 131088 | tf_op jit(solution)/shard_map/reduce_scatter | solution.py:277
  747.9 67.0 %reduce-scatter.10.cloned.1.call-done = f32[128,256]{1,0:T(8,128)} async-done(((f32[1024,256]{1,0:T(8,128)}), f32[128,256]{1,0:T(8,128)}) %reduce-scatter.10.cloned.1.call-update) | async-done | bytes 131088 | tf_op jit(solution)/shard_map/reduce_scatter | solution.py:274
  815.0 91.1 %reduce-scatter.18.cloned.1.call-done = f32[128,1024]{1,0:T(8,128)} async-done(((f32[1024,1024]{1,0:T(8,128)}), f32[128,1024]{1,0:T(8,128)}) %reduce-scatter.18.cloned.1.call-update) | async-done | bytes 524304 | tf_op jit(solution)/shard_map/reduce_scatter | solution.py:278
  906.1 92.1 %reduce-scatter.20.cloned.1.call-done = f32[128,1024]{1,0:T(8,128)} async-done(((f32[1024,1024]{1,0:T(8,128)}), f32[128,1024]{1,0:T(8,128)}) %reduce-scatter.20.cloned.1.call-update) | async-done | bytes 524304 | tf_op jit(solution)/shard_map/reduce_scatter | solution.py:279
  998.2 67.1 %reduce-scatter.14.cloned.1.call-done = f32[128,256]{1,0:T(8,128)} async-done(((f32[1024,256]{1,0:T(8,128)}), f32[128,256]{1,0:T(8,128)}) %reduce-scatter.14.cloned.1.call-update) | async-done | bytes 131088 | tf_op jit(solution)/shard_map/reduce_scatter | solution.py:276
  1065.3 66.8 %reduce-scatter.12.cloned.1.call-done = f32[128,256]{1,0:T(8,128)} async-done(((f32[1024,256]{1,0:T(8,128)}), f32[128,256]{1,0:T(8,128)}) %reduce-scatter.12.cloned.1.call-update) | async-done | bytes 131088 | tf_op jit(solution)/shard_map/reduce_scatter | solution.py:275
  (212 shorter events, 78.3 us)
Async XLA Ops:
  8.0 75.3 %all-gather.5.cloned.1.call-start = ((), (), s32[]{:S(2)}) async-start(), calls=%async_computation.7 | async-start | bytes 2621440 | tf_op jit(solution)/shard_map/all_gather | solution.py:161
  15.6 5.3 copy-start.28
  21.0 14.5 %copy-start.29 = (bf16[512,256]{1,0:T(8,128)(2,1)S(1)}, bf16[512,256]{1,0:T(8,128)(2,1)}, u32[]{:S(2)}) copy-start(bf16[512,256]{1,0:T(8,128)(2,1)} %param.34) | copy-start | bytes 786436
  31.0 12.6 %copy-start.15 = (bf16[1024,256]{1,0:T(8,128)(2,1)}, bf16[1024,256]{1,0:T(8,128)(2,1)S(1)}, u32[]{:S(2)}) copy-start(bf16[1024,256]{1,0:T(8,128)(2,1)S(1)} %all_gather.26) | copy-start | bytes 1572868
  31.0 13.4 %copy-start.43 = (f32[256]{0:T(256)S(1)}, f32[256]{0:T(256)}, u32[]{:S(2)}) copy-start(f32[256]{0:T(256)} %param.35) | copy-start | bytes 3076
  35.4 13.4 %copy-start.30 = (bf16[512,256]{1,0:T(8,128)(2,1)S(1)}, bf16[512,256]{1,0:T(8,128)(2,1)}, u32[]{:S(2)}) copy-start(bf16[512,256]{1,0:T(8,128)(2,1)} %param.31) | copy-start | bytes 786436
  35.4 94.5 %all-gather.7.cloned.1.call-start = ((), (), s32[]{:S(2)}) async-start(), calls=%async_computation.8 | async-start | bytes 2621440 | tf_op jit(solution)/shard_map/all_gather | solution.py:162
  44.4 11.8 %copy-start.44 = (f32[256]{0:T(256)S(1)}, f32[256]{0:T(256)}, u32[]{:S(2)}) copy-start(f32[256]{0:T(256)} %param.32) | copy-start | bytes 3076
  48.7 179.9 %all-reduce.7.cloned.1.call-start = ((), (), s32[]{:S(2)}) async-start(), calls=%async_computation.9 | async-start | bytes 4194304 | tf_op jit(solution)/shard_map/psum | solution.py:170
  56.2 3.1 copy-start.19
  56.2 4.4 copy-start.31
  142.3 5.8 copy-start.2
  156.5 5.8 copy-start.2
  172.8 55.9 %copy-start.39 = (f32[1024]{0:T(1024)S(1)}, f32[1024]{0:T(1024)}, u32[]{:S(2)}) copy-start(f32[1024]{0:T(1024)} %param.37) | copy-start | bytes 12292
  178.9 55.8 %all-gather.9.cloned.1.call-start = ((), (), s32[]{:S(2)}) async-start(), calls=%async_computation.10 | async-start | bytes 3145728 | tf_op jit(solution)/shard_map/all_gather | solution.py:174
  179.4 71.0 %all-gather.11.cloned.1.call-start = ((), (), s32[]{:S(2)}) async-start(), calls=%async_computation.11 | async-start | bytes 3145728 | tf_op jit(solution)/shard_map/all_gather | solution.py:175
  180.0 128.0 %all-reduce.9.cloned.1.call-start = ((), (), s32[]{:S(2)}) async-start(), calls=%async_computation.12 | async-start | bytes 4194304 | tf_op jit(solution)/shard_map/psum | solution.py:181
  232.2 1.9 copy-start.4
  232.2 2.5 copy-start.32
  232.2 2.5 copy-start.42
  232.2 2.5 copy-start.47
  250.4 6.0 copy-start.37
  256.4 51.6 %copy-start.40 = (f32[1024]{0:T(1024)S(1)}, f32[1024]{0:T(1024)}, u32[]{:S(2)}) copy-start(f32[1024]{0:T(1024)} %param.43) | copy-start | bytes 12292
  256.4 130.4 %all-reduce.11.cloned.1.call-start = ((), (), s32[]{:S(2)}) async-start(), calls=%async_computation.13 | async-start | bytes 4194304 | tf_op jit(solution)/shard_map/psum | solution.py:198
  311.7 2.2 copy-start.12
  311.8 2.2 copy-start.33
  311.8 2.2 copy-start.41
  319.5 3.0 copy-start.50
  321.4 8.7 copy-start.7
  321.4 3.2 copy-start.46
  321.4 5.1 copy-start.49
  322.4 7.7 copy-start.23
  326.5 5.0 copy-start.45
  335.2 188.8 %reduce-scatter.8.cloned.1.call-start = ((), (), s32[]{:S(2)}) async-start(), calls=%async_computation.14 | async-start | bytes 5242880 | tf_op jit(solution)/shard_map/reduce_scatter | solution.py:223
  386.8 5.2 copy-start.5
  386.8 6.5 copy-start.8
  386.8 7.1 copy-start.14
  396.0 2.0 copy-start.9
  396.0 3.7 copy-start.26
  414.7 1.6 copy-start.6
  418.7 3.0 copy-start.3
  427.1 1.6 copy-start.6
  431.1 3.0 copy-start.3
  447.0 3.0 copy-start.20
  447.0 140.6 %all-reduce.13.cloned.1.call-start = ((), (), s32[]{:S(2)}) async-start(), calls=%async_computation.15 | async-start | bytes 4194304 | tf_op jit(solution)/shard_map/psum | solution.py:237
  450.1 75.7 %copy-start.16 = (bf16[1024,256]{1,0:T(8,128)(2,1)S(1)}, bf16[1024,256]{1,0:T(8,128)(2,1)}, u32[]{:S(2)}) copy-start(bf16[1024,256]{1,0:T(8,128)(2,1)} %copy-done.15) | copy-start | bytes 1572868
  524.0 4.4 copy-start.27
  525.7 4.2 copy-start.18
  535.5 145.5 %all-reduce.15.cloned.1.call-start = ((), (), s32[]{:S(2)}) async-start(), calls=%async_computation.16 | async-start | bytes 2097152 | tf_op jit(solution)/shard_map/psum | solution.py:257
  598.2 2.9 copy-start.38
  598.2 4.6 copy-start.25
  601.1 5.1 copy-start.11
  602.7 145.2 %reduce-scatter.16.cloned.1.call-start = ((), (), s32[]{:S(2)}) async-start(), calls=%async_computation.20 | async-start | bytes 1179648 | tf_op jit(solution)/shard_map/reduce_scatter | solution.py:277
  606.1 208.8 %reduce-scatter.10.cloned.1.call-start = ((), (), s32[]{:S(2)}) async-start(), calls=%async_computation.17 | async-start | bytes 1179648 | tf_op jit(solution)/shard_map/reduce_scatter | solution.py:274
  611.6 294.5 %reduce-scatter.18.cloned.1.call-start = ((), (), s32[]{:S(2)}) async-start(), calls=%async_computation.21 | async-start | bytes 4718592 | tf_op jit(solution)/shard_map/reduce_scatter | solution.py:278
  619.2 379.0 %reduce-scatter.20.cloned.1.call-start = ((), (), s32[]{:S(2)}) async-start(), calls=%async_computation.22 | async-start | bytes 4718592 | tf_op jit(solution)/shard_map/reduce_scatter | solution.py:279
  626.0 2.8 copy-start.22
  626.0 439.2 %reduce-scatter.14.cloned.1.call-start = ((), (), s32[]{:S(2)}) async-start(), calls=%async_computation.19 | async-start | bytes 1179648 | tf_op jit(solution)/shard_map/reduce_scatter | solution.py:276
  632.2 4.3 copy-start.13
  632.2 6.6 copy-start.34
  632.2 6.6 copy-start.35
  632.2 6.6 copy-start.36
  632.2 499.9 %reduce-scatter.12.cloned.1.call-start = ((), (), s32[]{:S(2)}) async-start(), calls=%async_computation.18 | async-start | bytes 1179648 | tf_op jit(solution)/shard_map/reduce_scatter | solution.py:275
  632.3 499.8 %copy-start.1 = (bf16[256,1024]{1,0:T(8,128)(2,1)S(1)}, bf16[256,1024]{1,0:T(8,128)(2,1)}, u32[]{:S(2)}) copy-start(bf16[256,1024]{1,0:T(8,128)(2,1)} %param.29) | copy-start | bytes 1572868
  (6 other events, 6.5 us)
Sparse Core Ops, SparseCore 0:
  35.5 47.7 all-gather.4
  85.5 44.4 all-gather.6
  179.0 49.6 all-reduce.6
  256.5 51.4 all-reduce.8
  335.3 51.4 all-reduce.10
  447.2 76.8 reduce-scatter.7
  535.7 51.9 all-reduce.12
Sparse Core Ops, SparseCore 1:
  180.9 31.2 all-gather.8
  213.7 33.0 all-gather.10
  602.8 78.2 all-reduce.14
  685.0 62.9 reduce-scatter.15
  752.3 62.6 reduce-scatter.9
  819.2 86.9 reduce-scatter.17
  910.6 87.5 reduce-scatter.19
  1002.0 63.2 reduce-scatter.13
  1069.5 62.5 reduce-scatter.11
where the time goes:
time: 1150 us; the launch traced here: 1140 us
  waiting for transfers between devices  754 us (66%)
  matrix products  123 us (11%)
  blocking collectives  94.3 us (8%)
  local copies, waits for them, and re-layouts  85 us (7%)
  other arithmetic  63.5 us (6%)
  between operations  19.9 us (2%)
    reduce_scatter x1, waiting for transfers between devices, body(): lax.psum_scatter(grad_down, ('shard', 'ctx'), scatter_dimension=0, tiled=...  92.1 us
    reduce_scatter x1, waiting for transfers between devices, body(): lax.psum_scatter(grad_hidden, ('shard', 'ctx'), scatter_dimension=0, tile...  91.1 us
    reduce_scatter x1, waiting for transfers between devices, body(): lax.psum_scatter(joined.astype(jnp.bfloat16), 'ctx', scatter_dimension=0,...  71.2 us
    reduce_scatter x1, waiting for transfers between devices, body(): lax.psum_scatter(grad_value, ('shard', 'ctx'), scatter_dimension=0, tiled...  67.1 us
    reduce_scatter x1, waiting for transfers between devices, body(): lax.psum_scatter(grad_query, ('shard', 'ctx'), scatter_dimension=0, tiled...  67 us
    reduce_scatter x1, waiting for transfers between devices, body(): lax.psum_scatter(grad_key, ('shard', 'ctx'), scatter_dimension=0, tiled=T...  66.8 us
    reduce_scatter x1, waiting for transfers between devices, body(): lax.psum_scatter(grad_output, ('shard', 'ctx'), scatter_dimension=0, tile...  64.4 us
    psum x2, blocking collectives, body(): lax.psum((squares_local, jnp.sum(valid)), ('shard', 'ctx'))  61.4 us
  transfers between devices with their start and end apart: 16, of which 14 were waited for; matrix products, arithmetic and copies ran while one was open for 7% of the time, Pallas kernels for 0%

commit v1 on v0

v1 whole, which is shorter than its diff:
```python
from functools import partial
import math

import jax
import jax.numpy as jnp
from jax import lax
from jax.experimental import pallas as pl
from jax.experimental.pallas import tpu as pltpu
from jax.sharding import PartitionSpec as P

D = 1024
HEADS = 16
BF = jnp.bfloat16
F32 = jnp.float32
PAIR = 128
EPS = 1e-05


def contract(left, right, left_dim, right_dim):
    return lax.dot_general(
        left, right, (((left_dim,), (right_dim,)), ((), ())), preferred_element_type=F32
    )


PINNED = False
WEIGHT = 0.01


def cost(flops, nbytes):
    return pl.CostEstimate(flops=int(flops * WEIGHT), bytes_accessed=int(nbytes * WEIGHT), transcendentals=0)


def swap(value, axis, bit):
    size = lax.axis_size(axis)
    return lax.ppermute(value, axis, [(i, i ^ bit) for i in range(size)])


def swap_core(value):
    return swap(value, "tensor", 1)


def swap_outer(value):
    return swap(value, "tensor", 2)


def swap_shard(value):
    return swap(value, "shard", 1)


def swap_ctx(pieces):
    moved = {d: swap(pieces[d], "ctx", d) for d in reversed(range(1, len(pieces)))}
    return [pieces[0]] + [moved[d] for d in range(1, len(pieces))]


def sum_ctx(value):
    size = lax.axis_size("ctx")
    if size & (size - 1):
        return lax.psum(value, "ctx")
    bit = 1
    while bit < size:
        value = value + swap(value, "ctx", bit)
        bit *= 2
    return value


def sum_tokens(value):
    return sum_ctx(value + swap_shard(value))


def grid_call(kernel, name, grid, ins, outs, work, place, pinned=True):
    args = [a for a, _, _ in ins]
    nbytes = sum(a.size * a.dtype.itemsize for a in args)
    nbytes += sum(math.prod(s) * jnp.dtype(d).itemsize for s, d, _, _ in outs)
    without = lambda f: (lambda *i: f(*i[: len(grid)]))
    if pinned:
        args = [pltpu.with_memory_space_constraint(a, pltpu.HBM) for a in args]
    return pl.pallas_call(
        kernel,
        grid_spec=pltpu.PrefetchScalarGridSpec(
            num_scalar_prefetch=1,
            grid=grid,
            in_specs=[pl.BlockSpec(b, without(f)) for _, b, f in ins],
            out_specs=[pl.BlockSpec(b, without(f)) for _, _, b, f in outs],
        ),
        out_shape=[jax.ShapeDtypeStruct(s, d) for s, d, _, _ in outs],
        cost_estimate=cost(work, nbytes),
        compiler_params=pltpu.CompilerParams(vmem_limit_bytes=16 << 20),
        name=name,
    )(place, *args)


def call(kernel, name, args, outs, work, scratch=(), place=None, room=12, pinned=PINNED):
    nbytes = sum(a.size * a.dtype.itemsize for a in args)
    nbytes += sum(math.prod(s) * jnp.dtype(d).itemsize for s, d in outs)
    first = [] if place is None else [place]
    if pinned:
        args = [pltpu.with_memory_space_constraint(a, pltpu.VMEM) for a in args]
    return pl.pallas_call(
        kernel,
        in_specs=[pl.BlockSpec(memory_space=pltpu.SMEM)] * len(first)
        + [pl.BlockSpec(memory_space=pltpu.VMEM)] * len(args),
        out_specs=[pl.BlockSpec(memory_space=pltpu.VMEM)] * len(outs),
        out_shape=[jax.ShapeDtypeStruct(s, d) for s, d in outs],
        scratch_shapes=scratch,
        cost_estimate=cost(work, nbytes),
        compiler_params=pltpu.CompilerParams(vmem_limit_bytes=room << 20),
        name=name,
    )(*first, *args)


def whole(array):
    rank = array.ndim
    return (array, array.shape, lambda *i: (0,) * rank)


def turned(value, flip):
    half = value.shape[1] // 2
    return jnp.where(flip == 0, value, jnp.concatenate([value[:, half:], value[:, :half]], axis=1))


def entry_kernel(chunks, place, x_ref, embed_ref, *out_refs):
    core, flip = place[0], place[1]
    x = x_ref[...].astype(F32)
    rows = [x[:, s, :] + embed_ref[s : s + 1, :] for s in range(2 * chunks)]
    for c in range(chunks):
        own = turned(jnp.where(core == 0, rows[c], rows[chunks + c]), flip)
        out_refs[c][...] = own.astype(BF)
        out_refs[chunks + c][...] = own


def entry(place, x, embed):
    positions, seqs, width = x.shape
    chunks = seqs // 2
    block = math.gcd(64, positions)
    return grid_call(
        partial(entry_kernel, chunks),
        "entry",
        (positions // block,),
        [(x, (block, seqs, width), lambda i: (i, 0, 0)), whole(embed)],
        [
            ((positions, width), dtype, (block, width), lambda i: (i, 0))
            for dtype in (BF, F32)
            for _ in range(chunks)
        ],
        4 * x.size,
        place=place,
    )


def own_kernel(chunks, place, x_ref, *out_refs):
    core, flip = place[0], place[1]
    x = x_ref[...].astype(F32)
    for c in range(chunks):
        own = jnp.where(core == 0, x[:, c, :], x[:, chunks + c, :])
        out_refs[c][...] = turned(own, flip).astype(BF)


def own_rows(place, x):
    positions, seqs, width = x.shape
    chunks = seqs // 2
    block = math.gcd(64, positions)
    return grid_call(
        partial(own_kernel, chunks),
        "own_rows",
        (positions // block,),
        [(x, (block, seqs, width), lambda i: (i, 0, 0))],
        [((positions, width), BF, (block, width), lambda i: (i, 0))] * chunks,
        2 * x.size,
        place=place,
    )


def leave_kernel(chunks, dtype, place, *refs):
    core, flip = place[0], place[1]
    *ins, out_ref = refs
    own = [turned(ref[...].astype(F32), flip) for ref in ins[:chunks]]
    other = [turned(ref[...].astype(F32), flip) for ref in ins[chunks:]]
    rows = [jnp.where(core == 0, a, b) for a, b in zip(own, other)]
    rows += [jnp.where(core == 0, b, a) for a, b in zip(own, other)]
    out_ref[...] = jnp.stack(rows, axis=1).astype(dtype)


def leave(place, own):
    chunks = len(own)
    positions, width = own[0].shape
    dtype = own[0].dtype
    block = math.gcd(64, positions)
    arrays = [*own, *(swap_core(a) for a in own)]
    return grid_call(
        partial(leave_kernel, chunks, dtype),
        "leave",
        (positions // block,),
        [(a, (block, width), lambda i: (i, 0)) for a in arrays],
        [
            (
                (positions, 2 * chunks, width),
                dtype,
                (block, 2 * chunks, width),
                lambda i: (i, 0, 0),
            )
        ],
        2 * positions * width,
        place=place,
        pinned=False,
    )[0]


def pack_kernel(place, q_ref, k_ref, v_ref, out_ref):
    for g in range(q_ref.shape[1] // PAIR):
        for j, ref in enumerate((q_ref, k_ref, v_ref)):
            at = (3 * g + j) * PAIR
            out_ref[:, at : at + PAIR] = ref[:, g * PAIR : (g + 1) * PAIR]


def pack(place, q, k, v):
    rows, columns = q.shape
    return grid_call(
        pack_kernel,
        "pack",
        (1,),
        [whole(q), whole(k), whole(v)],
        [((rows, 3 * columns), BF, (rows, 3 * columns), lambda i: (0, 0))],
        0,
        place,
    )[0]


def pack_feed_kernel(place, out_ref, up_ref, down_ref, copy_ref, both_ref):
    each = up_ref.shape[1]
    copy_ref[...] = out_ref[...]
    both_ref[:, :each] = up_ref[...]
    both_ref[:, each:] = down_ref[...]


def pack_feed(place, out, up, down):
    rows, each = up.shape
    block = math.gcd(128, rows)
    tall = lambda a: (a, (block, a.shape[1]), lambda i: (i, 0))
    return grid_call(
        pack_feed_kernel,
        "pack_feed",
        (rows // block,),
        [tall(out), tall(up), tall(down)],
        [
            (out.shape, BF, (block, out.shape[1]), lambda i: (i, 0)),
            ((rows, 2 * each), BF, (block, 2 * each), lambda i: (i, 0)),
        ],
        0,
        place,
    )


def project_kernel(shift, place, x_ref, a_ref, b_ref, c_ref, d_ref, bias_ref, more_ref, *outs_and_all):
    *outs, pairs_ref = outs_and_all
    half = x_ref.shape[1] // 2
    per_core = len(outs) // 2
    wide = 3 * PAIR
    for core, (top, bottom) in enumerate(((a_ref, b_ref), (c_ref, d_ref))):

        def step(g, carry, core=core, top=top, bottom=bottom):
            at = pl.ds(pl.multiple_of(g * wide, wide), wide)
            value = contract(x_ref[:, :half], top[:, at], 1, 0)
            value += contract(x_ref[:, half:], bottom[:, at], 1, 0)
            pair = core * per_core + g
            bias = (bias_ref, more_ref)[core]
            for j, first in enumerate((shift, None, shift + per_core * PAIR)):
                part = value[:, j * PAIR : (j + 1) * PAIR]
                if first is not None:
                    part += bias[:, pl.ds(pl.multiple_of(first + g * PAIR, PAIR), PAIR)]
                pairs_ref[pair, :, j * PAIR : (j + 1) * PAIR] = part.astype(BF)
            return carry

        lax.fori_loop(0, per_core, step, 0)
    for d, out in enumerate(outs):
        out[...] = pairs_ref[place[2] ^ d]


def project(place, shift, x, weights, biases):
    rows, width = x.shape
    pairs = 2 * weights[0].shape[1] // (3 * PAIR)
    return call(
        partial(project_kernel, shift),
        "project",
        (x, *weights, *biases),
        [((rows, 3 * PAIR), BF)] * pairs,
        2 * rows * width * pairs * 3 * PAIR,
        scratch=[pltpu.VMEM((pairs, rows, 3 * PAIR), BF)],
        place=place,
    )


def project_back_kernel(pairs, place, *refs):
    pieces, (a_ref, b_ref, c_ref, d_ref, flat_ref, out_ref, sums_ref, pairs_ref) = (
        refs[:pairs],
        refs[pairs:],
    )
    for d, piece in enumerate(pieces):
        pairs_ref[place[2] ^ d] = piece[...]
    wide = 3 * PAIR
    for p in range(pairs):
        flat_ref[:, p * wide : (p + 1) * wide] = pairs_ref[p]
    half = a_ref.shape[0]
    middle = a_ref.shape[1]
    for at, first, second in ((0, a_ref, c_ref), (half, b_ref, d_ref)):
        value = contract(flat_ref[:, :middle], first[...], 1, 1)
        value += contract(flat_ref[:, middle:], second[...], 1, 1)
        out_ref[:, at : at + half] = value.astype(BF)
    sums_ref[...] = sum_rows(flat_ref[...].astype(F32))


def project_back(place, pieces, weights):
    rows, columns = pieces[0].shape
    pairs = len(pieces)
    width = 2 * weights[0].shape[0]
    return call(
        partial(project_back_kernel, pairs),
        "project_back",
        (*pieces, *weights),
        [((rows, pairs * columns), BF), ((rows, width), BF), ((1, pairs * columns), F32)],
        2 * rows * width * pairs * columns,
        scratch=[pltpu.VMEM((pairs, rows, columns), BF)],
        place=place,
    )


def merge_kernel(pairs, place, *refs):
    pieces, (a_ref, b_ref, c_ref, d_ref, flat_ref, out_ref, pairs_ref) = refs[:pairs], refs[pairs:]
    for d, piece in enumerate(pieces):
        pairs_ref[place[2] ^ d] = piece[...]
    for p in range(pairs):
        flat_ref[:, p * PAIR : (p + 1) * PAIR] = pairs_ref[p]
    half = a_ref.shape[0]
    middle = a_ref.shape[1]
    for at, first, second in ((0, a_ref, c_ref), (half, b_ref, d_ref)):
        value = contract(flat_ref[:, :middle], first[...], 1, 1)
        value += contract(flat_ref[:, middle:], second[...], 1, 1)
        out_ref[:, at : at + half] = value.astype(BF)


def merge(place, pieces, weights):
    rows, columns = pieces[0].shape
    pairs = len(pieces)
    width = 2 * weights[0].shape[0]
    return call(
        partial(merge_kernel, pairs),
        "merge",
        (*pieces, *weights),
        [((rows, pairs * columns), BF), ((rows, width), BF)],
        2 * rows * width * pairs * columns,
        scratch=[pltpu.VMEM((pairs, rows, columns), BF)],
        place=place,
    )


def lanes_of(part):
    lane = lax.broadcasted_iota(jnp.int32, (1, PAIR), 1)
    return lane < PAIR // 2 if part == 0 else lane >= PAIR // 2


def attend_kernel(scale, pieces, *refs):
    ins, outs, (log_ref, mixed_ref) = refs[:pieces], refs[pieces : 2 * pieces], refs[2 * pieces :]
    rows = ins[0].shape[0]
    join = lambda at: jnp.concatenate([ref[:, at : at + PAIR] for ref in ins], axis=0)
    q, k, v = join(0) * BF(scale), join(PAIR), join(2 * PAIR)
    lane = lax.broadcasted_iota(jnp.int32, (1, PAIR), 1)
    mixed_ref[...] = jnp.zeros_like(mixed_ref)

    def head(part, carry):
        lanes = (lane >= PAIR // 2) == (part == 1)
        k_head, v_head = jnp.where(lanes, k, BF(0)), jnp.where(lanes, v, BF(0))
        scores = contract(k_head, q, 1, 1)
        peak = jnp.max(scores, axis=0, keepdims=True)
        weights = jnp.exp(scores - peak)
        total = jnp.sum(weights, axis=0, keepdims=True)
        mixed_ref[...] += contract(v_head, weights.astype(BF), 0, 0) * (1.0 / total)
        log_ref[pl.ds(part, 1), :] = peak + jnp.log(total)
        return carry

    lax.fori_loop(0, 2, head, 0)
    mixed = mixed_ref[...].T.astype(BF)
    for d, out in enumerate(outs):
        out[...] = mixed[d * rows : (d + 1) * rows]


def attend(pieces, scale):
    rows = pieces[0].shape[0]
    length = rows * len(pieces)
    return call(
        partial(attend_kernel, scale, len(pieces)),
        "attend",
        pieces,
        [((rows, PAIR), BF)] * len(pieces) + [((2, length), F32)],
        16 * length * length * PAIR,
        scratch=[pltpu.VMEM((PAIR, length), F32)],
        room=24,
    )


def attend_back_kernel(scale, pieces, *refs):
    ins, grads = refs[:pieces], refs[pieces : 2 * pieces]
    log_ref, outs = refs[2 * pieces], refs[2 * pieces + 1 : 3 * pieces + 1]
    k_sum, v_sum, q_sum, q_ref, grad_ref = refs[3 * pieces + 1 :]
    rows = ins[0].shape[0]
    length = rows * pieces
    join = lambda refs, at: jnp.concatenate([ref[:, at : at + PAIR] for ref in refs], axis=0)
    k, v = join(ins, PAIR), join(ins, 2 * PAIR)
    q_ref[...] = join(ins, 0) * BF(scale)
    grad_ref[...] = join(grads, 0)
    k_sum[...] = jnp.zeros_like(k_sum)
    v_sum[...] = jnp.zeros_like(v_sum)
    q_sum[...] = jnp.zeros_like(q_sum)
    lane = lax.broadcasted_iota(jnp.int32, (1, PAIR), 1)
    block = math.gcd(512, length)

    def step(i, carry):
        part = i % 2
        at = pl.ds(pl.multiple_of(i // 2 * block, block), block)
        lanes = (lane >= PAIR // 2) == (part == 1)
        q, grad = q_ref[at, :], grad_ref[at, :]
        k_head, v_head = jnp.where(lanes, k, BF(0)), jnp.where(lanes, v, BF(0))
        q_head, grad_head = jnp.where(lanes, q, BF(0)), jnp.where(lanes, grad, BF(0))
        probs = jnp.exp(contract(k_head, q, 1, 1) - log_ref[pl.ds(part, 1), at])
        probs_grad = contract(v_head, grad, 1, 1)
        delta = jnp.sum(probs * probs_grad, axis=0, keepdims=True)
        scores_grad = (probs * (probs_grad - delta)).astype(BF)
        v_sum[...] += contract(probs.astype(BF), grad_head, 1, 0)
        k_sum[...] += contract(scores_grad, q_head, 1, 0)
        q_sum[:, at] += contract(k_head, scores_grad, 0, 0)
        return carry

    lax.fori_loop(0, 2 * length // block, step, 0)
    q_grad = (q_sum[...] * scale).T.astype(BF)
    for d, out in enumerate(outs):
        at = slice(d * rows, (d + 1) * rows)
        out[:, 0:PAIR] = q_grad[at, :]
        out[:, PAIR : 2 * PAIR] = k_sum[at, :].astype(BF)
        out[:, 2 * PAIR : 3 * PAIR] = v_sum[at, :].astype(BF)


def attend_back(pieces, grads, logs, scale):
    rows = pieces[0].shape[0]
    length = rows * len(pieces)
    return call(
        partial(attend_back_kernel, scale, len(pieces)),
        "attend_back",
        (*pieces, *grads, logs),
        [((rows, 3 * PAIR), BF)] * len(pieces),
        40 * length * length * PAIR,
        scratch=[pltpu.VMEM((length, PAIR), F32)] * 2
        + [pltpu.VMEM((PAIR, length), F32)]
        + [pltpu.VMEM((length, PAIR), BF)] * 2,
        room=24,
    )


def sum_rows(value):
    return jnp.sum(value, axis=0, keepdims=True)


def normal(value):
    center = jnp.mean(value, axis=-1, keepdims=True)
    offset = value - center
    spread = jnp.mean(offset * offset, axis=-1, keepdims=True)
    inverse = lax.rsqrt(spread + EPS)
    return offset * inverse, inverse


def normal_back(grad, unit, inverse):
    return inverse * (
        grad
        - jnp.mean(grad, axis=-1, keepdims=True)
        - unit * jnp.mean(grad * unit, axis=-1, keepdims=True)
    )


def by_rows(rows, run):
    size = math.gcd(64, rows)

    def step(i, carry):
        run(pl.ds(pl.multiple_of(i * size, size), size))
        return carry

    lax.fori_loop(0, rows // size, step, 0)


def feed_kernel(
    start_ref, mine_ref, theirs_ref, vec_ref, bias_ref, more_ref, a_ref, b_ref, c_ref, d_ref,
    first_ref, low_ref, hidden_ref, slope_ref, out_ref, acc,
):
    def norm(at):
        total = start_ref[at, :] + mine_ref[at, :].astype(F32) + theirs_ref[at, :].astype(F32)
        total += vec_ref[0:1, :]
        first_ref[at, :] = total
        unit, _ = normal(total)
        low_ref[at, :] = (unit * vec_ref[1:2, :] + vec_ref[2:3, :]).astype(BF)

    by_rows(start_ref.shape[0], norm)
    half, each = a_ref.shape[0], a_ref.shape[1] // 2
    size = math.gcd(512, each)
    acc[...] = jnp.zeros_like(acc)
    for core, (top, bottom) in enumerate(((a_ref, b_ref), (c_ref, d_ref))):

        def step(i, carry, core=core, top=top, bottom=bottom):
            here = pl.ds(pl.multiple_of(i * size, size), size)
            at = pl.ds(pl.multiple_of(core * each + i * size, size), size)
            down = pl.ds(pl.multiple_of(each + i * size, size), size)
            pre = contract(low_ref[:, :half], top[:, here], 1, 0)
            pre += contract(low_ref[:, half:], bottom[:, here], 1, 0)
            pre += (bias_ref, more_ref)[core][:, here]
            phi = 0.5 + 0.5 * lax.erf(pre * math.sqrt(0.5))
            hidden = (pre * phi).astype(BF)
            hidden_ref[:, at] = hidden
            bell = jnp.exp(-0.5 * (pre * pre)) * (1.0 / math.sqrt(2.0 * math.pi))
            slope_ref[:, at] = (phi + pre * bell).astype(BF)
            for k, weight in ((0, top), (half, bottom)):
                acc[:, k : k + half] += contract(hidden, weight[:, down], 1, 1)
            return carry

        lax.fori_loop(0, each // size, step, 0)
    out_ref[...] = acc[...].astype(BF)


def feed(start, mine, theirs, vec, biases, weights):
    rows, width = start.shape
    units = weights[0].shape[1]
    return call(
        feed_kernel,
        "feed",
        (start, mine, theirs, vec, *biases, *weights),
        [
            ((rows, width), F32),
            ((rows, width), BF),
            ((rows, units), BF),
            ((rows, units), BF),
            ((rows, width), BF),
        ],
        4 * rows * width * units,
        scratch=[pltpu.VMEM((rows, width), F32)],
    )


def feed_back_kernel(
    valid_row, tokens, place, first_ref, mine_ref, theirs_ref, vec_ref, teacher_ref, valid_ref, count_ref, slope_ref,
    a_ref, b_ref, c_ref, d_ref, result_ref, grad_ref, low_ref, pre_ref, out_ref, sums_ref, pre_sums_ref, acc, valid_sums,
):
    second = valid_ref.shape[0] // 2 + valid_row
    valid = jnp.where(
        place[0] == 0, valid_ref[valid_row : valid_row + 1, :], valid_ref[second : second + 1, :]
    )
    valid_sums[...] = jnp.broadcast_to(valid, (PAIR, valid.shape[1])).T
    sums_ref[...] = jnp.zeros_like(sums_ref)
    factor = 2.0 * tokens / count_ref[0:1, 0:1]

    def norm(at):
        valid = valid_sums[at, 0:1]
        unit, _ = normal(first_ref[at, :])
        normed = unit * vec_ref[1:2, :] + vec_ref[2:3, :]
        total = normed + mine_ref[at, :].astype(F32) + theirs_ref[at, :].astype(F32) + vec_ref[3:4, :]
        unit, inverse = normal(total)
        result = unit * vec_ref[4:5, :] + vec_ref[5:6, :]
        result_ref[at, :] = result.astype(BF)
        error = result - teacher_ref[at, :].astype(F32)
        result_grad = valid * factor * error
        grad = normal_back(result_grad * vec_ref[4:5, :], unit, inverse)
        grad_ref[at, :] = grad
        low = grad.astype(BF)
        low_ref[at, :] = low
        sums_ref[0:1, :] += sum_rows(result_grad * unit)
        sums_ref[1:2, :] += sum_rows(result_grad)
        sums_ref[2:3, :] += sum_rows(low.astype(F32))
        sums_ref[3:4, :] += sum_rows(valid * error * error)

    by_rows(first_ref.shape[0], norm)
    half, each = a_ref.shape[0], a_ref.shape[1] // 2
    size = math.gcd(512, each)
    acc[...] = jnp.zeros_like(acc)
    for core, (top, bottom) in enumerate(((a_ref, b_ref), (c_ref, d_ref))):

        def step(i, carry, core=core, top=top, bottom=bottom):
            here = pl.ds(pl.multiple_of(i * size, size), size)
            at = pl.ds(pl.multiple_of(core * each + i * size, size), size)
            down = pl.ds(pl.multiple_of(each + i * size, size), size)
            value = contract(low_ref[:, :half], top[:, down], 1, 0)
            value += contract(low_ref[:, half:], bottom[:, down], 1, 0)
            pre_grad = (value * slope_ref[:, at].astype(F32)).astype(BF)
            pre_ref[:, at] = pre_grad
            pre_sums_ref[:, at] = sum_rows(pre_grad.astype(F32))
            for k, weight in ((0, top), (half, bottom)):
                acc[:, k : k + half] += contract(pre_grad, weight[:, here], 1, 1)
            return carry

        lax.fori_loop(0, each // size, step, 0)
    out_ref[...] = acc[...].astype(BF)


def feed_back(place, row, tokens, first, mine, theirs, vec, teacher, valid, count, slope, weights):
    rows, width = first.shape
    units = slope.shape[1]
    return call(
        partial(feed_back_kernel, row, tokens),
        "feed_back",
        (first, mine, theirs, vec, teacher, valid, count, slope, *weights),
        [
            ((rows, width), BF),
            ((rows, width), F32),
            ((rows, width), BF),
            ((rows, units), BF),
            ((rows, width), BF),
            ((8, width), F32),
            ((1, units), F32),
        ],
        4 * rows * width * units,
        scratch=[pltpu.VMEM((rows, width), F32), pltpu.VMEM((rows, PAIR), F32)],
        place=place,
    )


def split_kernel(place, grad_ref, mine_ref, theirs_ref, first_ref, vec_ref, a_ref, b_ref, c_ref, d_ref, out_ref, low_ref, sums_ref, *outs_and_all):
    *outs, pairs_ref = outs_and_all
    sums_ref[...] = jnp.zeros_like(sums_ref)

    def norm(at):
        grad = grad_ref[at, :] + mine_ref[at, :].astype(F32) + theirs_ref[at, :].astype(F32)
        unit, inverse = normal(first_ref[at, :])
        out = normal_back(grad * vec_ref[1:2, :], unit, inverse)
        out_ref[at, :] = out
        low = out.astype(BF)
        low_ref[at, :] = low
        sums_ref[0:1, :] += sum_rows(grad * unit)
        sums_ref[1:2, :] += sum_rows(grad)
        sums_ref[2:3, :] += sum_rows(low.astype(F32))

    by_rows(grad_ref.shape[0], norm)
    half = a_ref.shape[0]
    per_core = len(outs) // 2
    for core, (top, bottom) in enumerate(((a_ref, b_ref), (c_ref, d_ref))):
        mixed = contract(low_ref[:, :half], top[...], 1, 0)
        mixed += contract(low_ref[:, half:], bottom[...], 1, 0)
        mixed = mixed.astype(BF)
        for p in range(per_core):
            pairs_ref[core * per_core + p] = mixed[:, p * PAIR : (p + 1) * PAIR]
    for d, piece in enumerate(outs):
        piece[...] = pairs_ref[place[2] ^ d]


def split(place, grad, mine, theirs, first, vec, weights):
    rows, width = grad.shape
    pairs = 2 * weights[0].shape[1] // PAIR
    return call(
        split_kernel,
        "split",
        (grad, mine, theirs, first, vec, *weights),
        [((rows, width), F32), ((rows, width), BF), ((8, width), F32)]
        + [((rows, PAIR), BF)] * pairs,
        2 * rows * width * pairs * PAIR,
        scratch=[pltpu.VMEM((pairs, rows, PAIR), BF)],
        place=place,
    )


def last_kernel(grad_ref, mine_ref, theirs_ref, out_ref, sums_ref):
    grad = grad_ref[...] + mine_ref[...].astype(F32) + theirs_ref[...].astype(F32)
    out_ref[...] = grad
    sums_ref[...] = jnp.broadcast_to(sum_rows(grad), sums_ref.shape)


def last(grad, mine, theirs):
    rows, width = grad.shape
    return call(
        last_kernel,
        "last",
        (grad, mine, theirs),
        [((rows, width), F32), ((8, width), F32)],
        4 * rows * width,
    )


def tally_kernel(chunks, each, place, *refs):
    two, one = refs[:chunks], refs[chunks : 2 * chunks]
    pre, qkv = refs[2 * chunks : 3 * chunks], refs[3 * chunks : 4 * chunks]
    zero, (features_ref, out_ref) = refs[4 * chunks : 5 * chunks], refs[5 * chunks :]
    core, flip, spot = place[0], place[1], place[3]
    add = lambda parts: sum(parts[1:], parts[0])
    out_ref[...] = jnp.zeros_like(out_ref)
    out_ref[0:4, :] = turned(add([ref[0:4, :] for ref in two]), flip)
    out_ref[4:7, :] = turned(add([ref[0:3, :] for ref in one]), flip)
    pre = add([ref[...] for ref in pre])
    qkv = add([ref[...] for ref in qkv])
    size = qkv.shape[1] // 2
    for slot in range(2):
        mine = core == slot
        out_ref[8 + slot : 9 + slot, :] = jnp.where(mine, pre[:, :each], pre[:, each:])
        out_ref[10 + slot : 11 + slot, :size] = jnp.where(mine, qkv[:, :size], qkv[:, size:])
    seqs = 2 * chunks
    for s in range(2 * seqs):
        here = jnp.logical_and(flip == s // seqs, core == s % seqs // chunks)
        row = turned(zero[s % chunks][0:1, :], flip)
        out_ref[12 + s : 13 + s, :] = jnp.where(here, row, 0.0)
    at = 12 + 2 * seqs
    features = features_ref[...].astype(F32)
    wide = features.shape[1]
    for s in range(2):
        here = jnp.logical_and(jnp.logical_and(core == 0, spot == 0), flip == s)
        for k in range(seqs):
            value = jnp.where(here, features[k : k + 1, :], 0.0)
            out_ref[at + s : at + s + 1, k * wide : (k + 1) * wide] = value


def tally(place, each, two, one, pre, qkv, zero, features):
    rows = -(-(14 + 2 * features.shape[0]) // 8) * 8
    return call(
        partial(tally_kernel, len(two), each),
        "tally",
        (*two, *one, *pre, *qkv, *zero, features),
        [((rows, two[0].shape[1]), F32)],
        0,
        place=place,
    )[0]


def grad_sum_kernel(pieces, cuts, *refs):
    total = refs[0][...].astype(F32)
    for ref in refs[1:pieces]:
        total = total + ref[...].astype(F32)
    for out, parts in zip(refs[pieces:], cuts):
        at = 0
        for start, size in parts:
            out[:, at : at + size] = total[:, start : start + size]
            at += size


def grad_sum(pieces, cuts):
    rows = pieces[0].shape[0]
    return call(
        partial(grad_sum_kernel, len(pieces), cuts),
        "grad_sum",
        pieces,
        [((rows, sum(size for _, size in parts)), F32) for parts in cuts],
        len(pieces) * pieces[0].size,
    )


def finish_kernel(each, size, shards, place, packed_ref, count_ref, time_ref, loss_ref, start_ref, hidden_ref, qkv_ref, *outs_and_all):
    *outs, all_ref = outs_and_all
    seqs = all_ref.shape[0]
    wide = all_ref.shape[1]
    per_row = seqs // shards
    at = 12 + seqs
    for s in range(seqs):
        k = s % per_row
        row = at + s // per_row
        all_ref[s : s + 1, :] = packed_ref[row : row + 1, k * wide : (k + 1) * wide]
    grads = packed_ref[12:at, :]
    time_ref[...] = lax.dot_general(
        all_ref[...],
        grads,
        (((0,), (0,)), ((), ())),
        precision=lax.Precision.HIGHEST,
        preferred_element_type=F32,
    )
    start_ref[...] = sum_rows(grads)
    total = jnp.sum(packed_ref[3:4, :], axis=1, keepdims=True)
    loss_ref[...] = total / (packed_ref.shape[1] * count_ref[0:1, 0:1])
    first = place[0] == 0
    hidden_ref[...] = jnp.where(first, packed_ref[8:9, :], packed_ref[9:10, :])[:, :each]
    qkv_ref[...] = jnp.where(first, packed_ref[10:11, :], packed_ref[11:12, :])[:, :size]
    for out, row in zip(outs, (0, 1, 2, 4, 5, 6)):
        out[...] = packed_ref[row : row + 1, :]


def finish(place, each, size, seqs, shards, wide, packed, count):
    width = packed.shape[1]
    return call(
        partial(finish_kernel, each, size, shards),
        "finish",
        (packed, count),
        [((wide, width), F32), ((1, 1), F32), ((1, width), F32), ((1, each), F32), ((1, size), F32)]
        + [((1, width), F32)] * 6,
        0,
        scratch=[pltpu.VMEM((seqs, wide), F32)],
        place=place,
    )


def token_sum(lefts, rights, rows, columns):
    total = None
    for left, right in zip(lefts, rights):
        term = contract(left[:, rows], right[:, columns], 0, 0)
        total = term if total is None else total + term
    return total


def grad_core_kernel(chunks, *refs):
    lefts, rights, out_ref = refs[:chunks], refs[chunks : 2 * chunks], refs[2 * chunks]
    rows, columns = out_ref.shape
    step = math.gcd(512, rows)

    def part(i, carry):
        at = pl.ds(pl.multiple_of(i * step, step), step)
        out_ref[at, :] = token_sum(lefts, rights, at, slice(columns, 2 * columns)).astype(BF)
        return carry

    lax.fori_loop(0, rows // step, part, 0)


def grad_core(lefts, rights):
    rows, columns = lefts[0].shape[1], rights[0].shape[1] // 2
    tokens = sum(a.shape[0] for a in lefts)
    return call(
        partial(grad_core_kernel, len(lefts)),
        "grad_core",
        (*lefts, *rights),
        [((rows, columns), BF)],
        2 * tokens * rows * columns,
    )[0]


def grad_shard_kernel(chunks, *refs):
    lefts, rights, (core_ref, out_ref) = refs[:chunks], refs[chunks : 2 * chunks], refs[2 * chunks :]
    half, columns = out_ref.shape
    size = math.gcd(256, half)

    def step(i, carry):
        at = pl.ds(pl.multiple_of(i * size, size), size)
        far = pl.ds(pl.multiple_of(half + i * size, size), size)
        value = token_sum(lefts, rights, far, slice(0, columns))
        out_ref[at, :] = (value + core_ref[far, :].astype(F32)).astype(BF)
        return carry

    lax.fori_loop(0, half // size, step, 0)


def grad_shard(lefts, rights, core):
    half, columns = lefts[0].shape[1] // 2, rights[0].shape[1] // 2
    tokens = sum(a.shape[0] for a in lefts)
    return call(
        partial(grad_shard_kernel, len(lefts)),
        "grad_shard",
        (*lefts, *rights, core),
        [((half, columns), BF)],
        2 * tokens * half * columns,
    )[0]


def grad_own_kernel(chunks, place, *refs):
    lefts, rights, (core_ref, shard_ref, *outs, acc) = (
        refs[:chunks],
        refs[chunks : 2 * chunks],
        refs[2 * chunks :],
    )
    half, columns = acc.shape
    size = math.gcd(256, half)

    def step(i, carry):
        at = pl.ds(pl.multiple_of(i * size, size), size)
        value = token_sum(lefts, rights, at, slice(0, columns))
        acc[at, :] = value + core_ref[at, :].astype(F32) + shard_ref[at, :].astype(F32)
        return carry

    lax.fori_loop(0, half // size, step, 0)
    rows = outs[0].shape[0]
    if len(outs) == 1:
        outs[0][...] = acc[...].astype(BF)
    else:
        for d, out in enumerate(outs):
            at = pl.multiple_of((place[2] ^ d) * rows, rows)
            out[...] = acc[pl.ds(at, rows), :].astype(out.dtype)


def grad_own(place, lefts, rights, core, shard, pieces):
    half, columns = lefts[0].shape[1] // 2, rights[0].shape[1] // 2
    tokens = sum(a.shape[0] for a in lefts)
    rows = half // pieces
    return call(
        partial(grad_own_kernel, len(lefts)),
        "grad_own",
        (*lefts, *rights, core, shard),
        [((rows, columns), F32 if pieces > 1 and d == 0 else BF) for d in range(pieces)],
        2 * tokens * half * columns,
        scratch=[pltpu.VMEM((half, columns), F32)],
        place=place,
    )


def heads_of(value):
    return value.reshape(value.shape[:-1] + (2, PAIR // 2))


def gathered_forward(qkv, scale):
    queries = heads_of(qkv[..., :PAIR])
    both = lax.all_gather(qkv[..., PAIR:], "ctx", axis=2, tiled=True)
    length = both.shape[2]
    block = math.gcd(length, 512)
    blocks = jnp.moveaxis(both.reshape(both.shape[:2] + (length // block, block, 2 * PAIR)), 2, 0)
    shape = queries.shape[:-1]

    def step(carry, piece):
        peak, total, summed = carry
        keys, values = heads_of(piece[..., :PAIR]), heads_of(piece[..., PAIR:])
        scores = jnp.einsum("gsqhd,gskhd->gsqhk", queries, keys, preferred_element_type=F32) * scale
        new_peak = jnp.maximum(peak, jnp.max(scores, axis=-1))
        fade = jnp.exp(peak - new_peak)
        weights = jnp.exp(scores - new_peak[..., None])
        total = total * fade + jnp.sum(weights, axis=-1)
        summed = summed * fade[..., None] + jnp.einsum(
            "gsqhk,gskhd->gsqhd", weights.astype(BF), values, preferred_element_type=F32
        )
        return (new_peak, total, summed), None

    first = (
        jnp.full(shape, -1e30, F32),
        jnp.zeros(shape, F32),
        jnp.zeros(queries.shape, F32),
    )
    (peak, total, summed), _ = lax.scan(step, first, blocks)
    attended = summed / total[..., None]
    mixed = attended.reshape(qkv.shape[:-1] + (PAIR,)).astype(BF)
    return mixed, (queries, blocks, peak + jnp.log(total), attended)


def gathered_backward(saved, grad, scale):
    queries, blocks, logs, attended = saved
    out_grad = heads_of(grad)
    delta = jnp.sum(out_grad.astype(F32) * attended, axis=-1)

    def step(q_grad, piece):
        keys, values = heads_of(piece[..., :PAIR]), heads_of(piece[..., PAIR:])
        scores = jnp.einsum("gsqhd,gskhd->gsqhk", queries, keys, preferred_element_type=F32) * scale
        weights = jnp.exp(scores - logs[..., None])
        weight_grad = jnp.einsum(
            "gsqhd,gskhd->gsqhk", out_grad, values, preferred_element_type=F32
        )
        score_grad = (weights * (weight_grad - delta[..., None])).astype(BF)
        v_grad = jnp.einsum(
            "gsqhk,gsqhd->gskhd", weights.astype(BF), out_grad, preferred_element_type=F32
        )
        k_grad = jnp.einsum("gsqhk,gsqhd->gskhd", score_grad, queries, preferred_element_type=F32)
        q_grad = q_grad + scale * jnp.einsum(
            "gsqhk,gskhd->gsqhd", score_grad, keys, preferred_element_type=F32
        )
        flat = lambda a: a.reshape(a.shape[:-2] + (PAIR,))
        return q_grad, jnp.concatenate([flat(k_grad) * scale, flat(v_grad)], axis=-1).astype(BF)

    q_grad, joined = lax.scan(step, jnp.zeros(queries.shape, F32), blocks)
    joined = jnp.moveaxis(joined, 0, 2)
    joined = joined.reshape(joined.shape[:2] + (-1, 2 * PAIR))
    owned = lax.psum_scatter(joined, "ctx", scatter_dimension=2, tiled=True)
    return jnp.concatenate([q_grad.reshape(grad.shape).astype(BF), owned], axis=-1)


class Order:
    def __init__(self):
        self.last = None

    def hold(self, *values):
        if self.last is None:
            return values
        return lax.optimization_barrier((*values, self.last))[: len(values)]

    def mark(self, value):
        self.last = value
        return value


def body(
    inputs,
    time_features,
    valid_mask,
    teacher,
    w_time,
    b_time,
    w_query,
    b_query,
    w_key,
    w_value,
    b_value,
    w_output,
    b_output,
    gain_one,
    shift_one,
    w_hidden,
    b_hidden,
    w_down,
    b_down,
    gain_two,
    shift_two,
):
    positions, seqs, width = inputs.shape
    half = width // 2
    chunks = seqs // 2
    columns = w_query.shape[1]
    per_core = columns // PAIR
    pairs = 2 * per_core
    each = w_hidden.shape[1]
    scale = 1.0 / math.sqrt(D // HEADS)
    ctx = lax.axis_size("ctx")
    shards = lax.axis_size("shard")
    by_units = pairs == ctx
    shard = lax.axis_index("shard")
    core = lax.axis_index("tensor") % 2
    spot = lax.axis_index("ctx")
    slot = spot if by_units else jnp.int32(0)
    place = jnp.stack([core, shard, slot, spot]).astype(jnp.int32)
    order = Order()

    def turn(value):
        return jnp.where(
            shard == 0, value, jnp.concatenate([value[..., half:], value[..., :half]], axis=-1)
        )

    def after(value, *others):
        return lax.optimization_barrier((value, *others))[0]

    qkv_mine = pack(place, w_query, w_key, w_value)
    qkv_across = swap_shard(qkv_mine)
    qkv_side = swap_core(qkv_mine)

    bias = jnp.concatenate([b_hidden, b_query, b_value]).reshape(1, -1)
    biases = (bias, swap_core(bias))
    vec = turn(
        jnp.stack([b_output, gain_one, shift_one, b_down, gain_two, shift_two, b_down, b_down])
    )
    valid = valid_mask.T.astype(F32)
    count = jnp.full((8, 128), jnp.sum(valid), F32)
    embed = jnp.dot(time_features, w_time, preferred_element_type=F32) + b_time
    place, vec, valid, embed, count = lax.optimization_barrier((place, vec, valid, embed, count))
    count = sum_ctx(count)
    count = count + swap_shard(after(count, qkv_across))
    tokens_all = positions * seqs * ctx * shards
    rows = entry(place, inputs, embed)
    low, start = rows[:chunks], rows[chunks:]
    out_mine, feed_mine = pack_feed(after(place, low[0]), w_output, w_hidden, w_down)
    out_side, feed_side = swap_core(out_mine), swap_core(feed_mine)
    teachers = own_rows(after(place, out_mine), teacher)
    order.mark(teachers[0])

    qkv_weights = (qkv_mine, qkv_across, qkv_side, swap_core(after(qkv_across, teachers[0])))
    out_across = swap_shard(after(out_mine, qkv_across))
    slots = []
    for c in range(chunks):
        (held,) = order.hold(low[c])
        slots.append(project(place, each, held, qkv_weights, biases))
        order.mark(slots[c][0])
    feed_across = swap_shard(after(feed_mine, out_across, slots[-1][0]))
    out_weights = (out_mine, out_across, out_side, swap_core(after(out_across, slots[-1][0])))
    kept, mixed = [], []
    for c in range(chunks):
        if by_units:
            sent = slots[c]
            if c > 0:
                sent = list(lax.optimization_barrier((*sent, *kept[c - 1][0]))[: len(sent)])
            pieces = swap_ctx(sent)
            *outs, logs = attend(order.hold(*pieces), scale)
            order.mark(logs)
            mixed.append(swap_ctx(outs))
            kept.append((pieces, logs))
        else:
            value, saved = gathered_forward(jnp.stack(slots[c])[:, None], scale)
            mixed.append([value[p, 0] for p in range(pairs)])
            kept.append(saved)
    firsts, norms, hiddens, slopes, feeds, flats, branches = [], [], [], [], [], [], []
    for c in range(chunks):
        held = order.hold(*mixed[c])
        flat, mine = merge(place, held, out_weights)
        order.mark(flat)
        flats.append(flat)
        branches.append((mine, swap_outer(mine)))
    feed_weights = (feed_mine, feed_across, feed_side, swap_core(after(feed_across, order.last)))
    for c in range(chunks):
        (held,) = order.hold(start[c])
        first, normed, hidden, slope, mine = feed(held, *branches[c], vec, biases, feed_weights)
        order.mark(normed)
        firsts.append(first)
        norms.append(normed)
        hiddens.append(hidden)
        slopes.append(slope)
        feeds.append((mine, swap_outer(mine)))

    results, sum_grads, feed_lows, pre_grads, backs, two_sums, pre_sums = [], [], [], [], [], [], []
    for c in range(chunks):
        (held,) = order.hold(firsts[c])
        result, sum_grad, feed_low, pre_grad, mine, two, pre_sum = feed_back(
            place, c, tokens_all, held, *feeds[c], vec, teachers[c], valid, count, slopes[c], feed_weights
        )
        order.mark(pre_sum)
        results.append(result)
        sum_grads.append(sum_grad)
        feed_lows.append(feed_low)
        pre_grads.append(pre_grad)
        backs.append((mine, swap_outer(mine)))
        two_sums.append(two)
        pre_sums.append(pre_sum)

    class Weight:
        def __init__(self, lefts, rights):
            self.lefts, self.rights = lefts, rights

        def held(self):
            first, = order.hold(self.lefts[0])
            return [first, *self.lefts[1:]]

        def core(self):
            value = order.mark(grad_core(self.held(), self.rights))
            self.from_core = swap_core(value)

        def shard(self):
            value = order.mark(grad_shard(self.held(), self.rights, self.from_core))
            self.from_shard = swap_shard(value)

        def own(self):
            count = ctx if by_units else 1
            own = grad_own(place, self.held(), self.rights, self.from_core, self.from_shard, count)
            order.mark(own[0])
            if by_units:
                self.pieces = swap_ctx(own)
            else:
                pieces = lax.all_to_all(own[0].reshape(ctx, half // ctx, -1), "ctx", 0, 0)
                self.pieces = [jnp.sum(pieces.astype(F32), axis=0)]

        def total(self, cuts):
            outs = grad_sum(order.hold(*self.pieces), cuts)
            order.mark(outs[0])
            return outs

    first_grads, branch_lows, one_sums, mixed_grads = [], [], [], []

    def run_split(c):
        (held,) = order.hold(sum_grads[c])
        first_grad, branch_low, one, *outs = split(
            place, held, *backs[c], firsts[c], vec, out_weights
        )
        order.mark(one)
        first_grads.append(first_grad)
        branch_lows.append(branch_low)
        one_sums.append(one)
        mixed_grads.append(swap_ctx(outs) if by_units else outs)

    qkv_grads = []

    def run_attend_back(c):
        if by_units:
            pieces, logs = kept[c]
            (logs,) = order.hold(logs)
            outs = attend_back(pieces, mixed_grads[c], logs, scale)
            order.mark(outs[0])
            qkv_grads.append(swap_ctx(outs))
        else:
            value = gathered_backward(kept[c], jnp.stack(mixed_grads[c])[:, None], scale)
            qkv_grads.append([value[p, 0] for p in range(pairs)])

    qkv_sums, qkv_flats, last_parts = [], [], []

    def run_project_back(c):
        held = order.hold(*qkv_grads[c])
        flat, mine, qkv_sum = project_back(place, held, qkv_weights)
        order.mark(qkv_sum)
        qkv_sums.append(qkv_sum)
        qkv_flats.append(flat)
        last_parts.append((mine, swap_outer(mine)))

    starts, zero_sums = [], []

    def run_last(c):
        (held,) = order.hold(first_grads[c])
        start_grad, zero = last(held, *last_parts[c])
        order.mark(zero)
        starts.append(start_grad)
        zero_sums.append(zero)

    down = Weight(feed_lows, hiddens)
    hidden = Weight(norms, pre_grads)
    output = Weight(branch_lows, flats)
    qkv = Weight(low, qkv_flats)
    down.core()
    run_split(0)
    hidden.core()
    down.shard()
    (held,) = order.hold(place)
    layer_out = order.mark(leave(held, results))
    run_split(1)
    hidden.shard()
    run_attend_back(0)
    output.core()
    run_attend_back(1)
    output.shard()
    run_project_back(0)
    run_project_back(1)
    qkv.core()
    down.own()
    qkv.shard()
    run_last(0)
    run_last(1)
    packed = order.mark(
        tally(place, each, two_sums, one_sums, pre_sums, qkv_sums, zero_sums, time_features)
    )
    packed = sum_tokens(packed + swap_core(packed))
    hidden.own()
    qkv.own()
    output.own()
    (held,) = order.hold(place)
    grad_inputs = order.mark(leave(held, starts))
    everything = lambda weight: [[(0, weight.rights[0].shape[1] // 2)]]
    (grad_w_down,) = down.total(everything(down))
    (grad_w_hidden,) = hidden.total(everything(hidden))
    (grad_w_output,) = output.total(everything(output))
    grad_w_query, grad_w_key, grad_w_value = qkv.total(
        [[((3 * g + j) * PAIR, PAIR) for g in range(per_core)] for j in range(3)]
    )

    (held,) = order.hold(place)
    grad_w_time, loss, start_sum, hidden_sum, qkv_sum, *rest = finish(
        held, each, 3 * columns, shards * seqs, shards, time_features.shape[1], packed, count
    )
    qkv_sum = qkv_sum.reshape(per_core, 3, PAIR)
    return (
        layer_out,
        loss.reshape(()),
        grad_inputs,
        grad_w_time,
        start_sum.reshape(-1),
        grad_w_query,
        qkv_sum[:, 0].reshape(-1),
        grad_w_key,
        grad_w_value,
        qkv_sum[:, 2].reshape(-1),
        grad_w_output,
        rest[5].reshape(-1),
        rest[3].reshape(-1),
        rest[4].reshape(-1),
        grad_w_hidden,
        hidden_sum.reshape(-1),
        grad_w_down,
        rest[2].reshape(-1),
        rest[0].reshape(-1),
        rest[1].reshape(-1),
    )


def solution(mesh):
    placed = (
        P("ctx", "shard", None),
        P("shard", None),
        P("ctx", "shard"),
        P("ctx", "shard", None),
        P(),
        P(),
        P("shard", "tensor"),
        P("tensor"),
        P("shard", "tensor"),
        P("shard", "tensor"),
        P("tensor"),
        P("shard", "tensor"),
        P(),
        P(),
        P(),
        P("shard", "tensor"),
        P("tensor"),
        P("shard", "tensor"),
        P(),
        P(),
        P(),
    )
    return jax.shard_map(
        body,
        mesh=mesh,
        in_specs=placed,
        out_specs=(
            P("ctx", "shard", None),
            P(),
            P("ctx", "shard", None),
            P(),
            P(),
            P(("shard", "ctx"), "tensor"),
            P("tensor"),
            P(("shard", "ctx"), "tensor"),
            P(("shard", "ctx"), "tensor"),
            P("tensor"),
            P(("shard", "ctx"), "tensor"),
            P(),
            P(),
            P(),
            P(("shard", "ctx"), "tensor"),
            P("tensor"),
            P(("shard", "ctx"), "tensor"),
            P(),
            P(),
            P(),
        ),
        check_vma=False,
    )
```

time: 1150 us -> 370 us (0.32)
  waiting for transfers between devices: 754 us -> 170 us
  matrix products: 123 us -> 1.49 us
  Pallas kernels: 0 us -> 104 us
  blocking collectives: 94.3 us -> 0 us
  starting transfers between devices: 1.53 us -> 89.1 us
  local copies, waits for them, and re-layouts: 85 us -> 2.38 us
  other arithmetic: 63.5 us -> 2.15 us
  between operations: 19.9 us -> 1.25 us
    reduce_scatter x7 -> x0, waiting for transfers between devices: 520 us -> none  [the longest x1 92.1 us: body(): lax.psum_scatter(grad_down, ('shard', 'ctx'), scatter_dimension=0, tiled=...]
    psum x5 -> x0, waiting for transfers between devices: 178 us -> none  [the longest x1 52 us: body(): lax.psum(start_part.astype(jnp.bfloat16), 'tensor').astype(jnp.float32)]
    ppermute x0 -> x73, waiting for transfers between devices: none -> 170 us  [swap(): return lax.ppermute(value, axis, [(i, i ^ bit) for i in range(size)])]
    dot_general x34 -> x1, matrix products: 123 us -> 1.49 us  [body(): embed = jnp.dot(time_features, w_time, preferred_element_type=F32) + b_time]
    pallas_call x0 -> x42, Pallas kernels: none -> 104 us  [the longest x36 81.5 us: call(): pl.pallas_call(kernel, in_specs=[pl.BlockSpec(memory_space=pltpu.SMEM)] *...]
    ppermute x0 -> x73, starting transfers between devices: none -> 89.1 us  [swap(): return lax.ppermute(value, axis, [(i, i ^ bit) for i in range(size)])]
    psum x2 -> x0, blocking collectives: 61.4 us -> none  [body(): lax.psum((squares_local, jnp.sum(valid)), ('shard', 'ctx'))]
    all_gather x4 -> x0, waiting for transfers between devices: 55.5 us -> none  [the longest x1 40.1 us: body(): lax.all_gather(value_local, 'ctx', axis=0, tiled=True)]
  transfers between devices with their start and end apart: 16 -> 73, of which waited for: 14 -> 27; matrix products, arithmetic and copies ran while one was open for 7% -> 1% of each run, Pallas kernels for 0% -> 24%
where the time goes in v1:
time: 370 us
  waiting for transfers between devices  170 us (46%)
  Pallas kernels  104 us (28%)
  starting transfers between devices  89.1 us (24%)
    ppermute x73, waiting for transfers between devices, swap(): return lax.ppermute(value, axis, [(i, i ^ bit) for i in range(size)])  170 us
    ppermute x73, starting transfers between devices, swap(): return lax.ppermute(value, axis, [(i, i ^ bit) for i in range(size)])  89.1 us
    pallas_call x36, Pallas kernels, call(): pl.pallas_call(kernel, in_specs=[pl.BlockSpec(memory_space=pltpu.SMEM)] *...  81.5 us
    pallas_call x6, Pallas kernels, grid_call(): pl.pallas_call(kernel, grid_spec=pltpu.PrefetchScalarGridSpec(num_scalar_...  22.1 us
  transfers between devices with their start and end apart: 73, of which 27 were waited for; matrix products, arithmetic and copies ran while one was open for 1% of the time, Pallas kernels for 24%

profile of v1, /device:TPU:0, one launch (start us, length us, event | category | flops | bytes accessed | tf_op | source)
XLA Modules:
  0.0 369.7 jit_solution(8420312250131053678)
XLA Ops:
  0.8 1.8 pack.1.a_ref.refs_4_
  3.1 2.6 collective-permute-start
  10.7 4.1 %entry.1 = (bf16[256,1024]{1,0:T(8,128)(2,1)S(1)}, bf16[256,1024]{1,0:T(8,128)(2,1)S(1)}, f32[256,1024]{1,0:T(8,128)S(1)}, f32[256,1024]{1,0:T(8,128)S(1)}) custom-call(s32[4]{0:T(128)S(1)} %pad_add_fusion.place, bf16[256,4,1024]{2,1,0:T(4,128)(2,1)} %x_ref.2, f32[4,1024]{1,0:T(4,128)} %convolution_add_fusion.embed_ref), custom_call_target="tpu_custom_call" | custom-call | flops 41943 | bytes 52592 | tf_op jit(solution)/shard_map/entry/pallas_call | solution.py:77
  14.8 3.0 pack_feed.1
  17.8 3.7 own_rows.1
  21.5 2.3 collective-permute-done.b_ref.refs_5_
  23.8 1.8 collective-permute-start.16
  26.8 2.4 project.2
  29.2 2.4 project.3
  32.5 1.7 collective-permute-start.20
  35.8 2.6 collective-permute-start.5
  38.6 4.9 %collective-permute-done.4.refs_1_ = bf16[256,384]{1,0:T(8,128)(2,1)S(1)} collective-permute-done((bf16[256,384]{1,0:T(8,128)(2,1)S(1)}, bf16[256,384]{1,0:T(8,128)(2,1)S(1)}, u32[]{:S(2)}, u32[]{:S(2)}) %collective-permute-start.4) | collective-permute-done | bytes 196640 | tf_op jit(solution)/shard_map/ppermute | solution.py:35
  43.6 9.4 %collective-permute-done.5.refs_2_ = bf16[256,384]{1,0:T(8,128)(2,1)S(1)} collective-permute-done((bf16[256,384]{1,0:T(8,128)(2,1)S(1)}, bf16[256,384]{1,0:T(8,128)(2,1)S(1)}, u32[]{:S(2)}, u32[]{:S(2)}) %collective-permute-start.5) | collective-permute-done | bytes 196640 | tf_op jit(solution)/shard_map/ppermute | solution.py:35
  53.0 3.0 collective-permute-start.7
  58.4 3.7 %attend.2 = (bf16[256,128]{1,0:T(8,128)(2,1)S(1)}, bf16[256,128]{1,0:T(8,128)(2,1)S(1)}, bf16[256,128]{1,0:T(8,128)(2,1)S(1)}, bf16[256,128]{1,0:T(8,128)(2,1)S(1)}, f32[2,1024]{1,0:T(2,128)S(1)}) custom-call(bf16[256,384]{1,0:T(8,128)(2,1)S(1)} %get-tuple-element.244.refs_0_, bf16[256,384]{1,0:T(8,128)(2,1)S(1)} %collective-permute-done.4.refs_1_, ...), custom_call_target="tpu_custom_call" | custom-call | flops 21474836 | bytes 10567 | tf_op jit(solution)/shard_map/attend/pallas_call | solution.py:98
  63.8 10.1 %collective-permute-done.8.refs_2_ = bf16[256,384]{1,0:T(8,128)(2,1)S(1)} collective-permute-done((bf16[256,384]{1,0:T(8,128)(2,1)S(1)}, bf16[256,384]{1,0:T(8,128)(2,1)S(1)}, u32[]{:S(2)}, u32[]{:S(2)}) %collective-permute-start.8) | collective-permute-done | bytes 196640 | tf_op jit(solution)/shard_map/ppermute | solution.py:35
  73.9 1.7 collective-permute-start.15
  75.6 3.7 %attend.3 = (bf16[256,128]{1,0:T(8,128)(2,1)S(1)}, bf16[256,128]{1,0:T(8,128)(2,1)S(1)}, bf16[256,128]{1,0:T(8,128)(2,1)S(1)}, bf16[256,128]{1,0:T(8,128)(2,1)S(1)}, f32[2,1024]{1,0:T(2,128)S(1)}) custom-call(bf16[256,384]{1,0:T(8,128)(2,1)S(1)} %get-tuple-element.249.refs_0_, bf16[256,384]{1,0:T(8,128)(2,1)S(1)} %collective-permute-done.7.refs_1_, ...), custom_call_target="tpu_custom_call" | custom-call | flops 21474836 | bytes 10567 | tf_op jit(solution)/shard_map/attend/pallas_call | solution.py:98
  79.3 3.3 collective-permute-start.10
  82.6 2.4 collective-permute-start.12
  86.2 1.8 collective-permute-done.11.refs_2_
  92.0 12.7 %collective-permute-done.19.theirs_ref = bf16[256,1024]{1,0:T(8,128)(2,1)S(1)} collective-permute-done((bf16[256,1024]{1,0:T(8,128)(2,1)S(1)}, bf16[256,1024]{1,0:T(8,128)(2,1)S(1)}, u32[]{:S(2)}, u32[]{:S(2)}) %collective-permute-start.19) | collective-permute-done | bytes 524320 | tf_op jit(solution)/shard_map/ppermute | solution.py:35
  104.7 5.0 %feed.2 = (f32[256,1024]{1,0:T(8,128)S(1)}, bf16[256,1024]{1,0:T(8,128)(2,1)S(1)}, bf16[256,2048]{1,0:T(8,128)(2,1)S(1)}, bf16[256,2048]{1,0:T(8,128)(2,1)S(1)}, bf16[256,1024]{1,0:T(8,128)(2,1)S(1)}) custom-call(f32[256,1024]{1,0:T(8,128)S(1)} %get-tuple-element.274.start_ref, bf16[256,1024]{1,0:T(8,128)(2,1)S(1)} %get-tuple-element.275.mine_ref, ...), custom_call_target="tpu_custom_call" | custom-call | flops 21474836 | bytes 147251 | tf_op jit(solution)/shard_map/feed/pallas_call | solution.py:98
  111.4 4.6 %collective-permute-done.23.theirs_ref = bf16[256,1024]{1,0:T(8,128)(2,1)S(1)} collective-permute-done((bf16[256,1024]{1,0:T(8,128)(2,1)S(1)}, bf16[256,1024]{1,0:T(8,128)(2,1)S(1)}, u32[]{:S(2)}, u32[]{:S(2)}) %collective-permute-start.23) | collective-permute-done | bytes 524320 | tf_op jit(solution)/shard_map/ppermute | solution.py:35
  116.0 5.2 %feed.3 = (f32[256,1024]{1,0:T(8,128)S(1)}, bf16[256,1024]{1,0:T(8,128)(2,1)S(1)}, bf16[256,2048]{1,0:T(8,128)(2,1)S(1)}, bf16[256,2048]{1,0:T(8,128)(2,1)S(1)}, bf16[256,1024]{1,0:T(8,128)(2,1)S(1)}) custom-call(f32[256,1024]{1,0:T(8,128)S(1)} %get-tuple-element.283.start_ref, bf16[256,1024]{1,0:T(8,128)(2,1)S(1)} %get-tuple-element.284.mine_ref, ...), custom_call_target="tpu_custom_call" | custom-call | flops 21474836 | bytes 147251 | tf_op jit(solution)/shard_map/feed/pallas_call | solution.py:98
  123.9 2.5 collective-permute-done.25
  126.4 1.7 collective-permute-start.26
  128.1 2.8 collective-permute-done.26
  131.5 3.1 collective-permute-done.27
  134.5 6.9 %feed_back.2 = (bf16[256,1024]{1,0:T(8,128)(2,1)S(1)}, f32[256,1024]{1,0:T(8,128)S(1)}, bf16[256,1024]{1,0:T(8,128)(2,1)S(1)}, bf16[256,2048]{1,0:T(8,128)(2,1)S...) custom-call(s32[4]{0:T(128)S(1)} %pad_add_fusion.place, ...), custom_call_target="tpu_custom_call" | custom-call | flops 21474836 | bytes 158105 | tf_op jit(solution)/shard_map/feed_back/pallas_call | solution.py:98
  142.0 6.9 %feed_back.3 = (bf16[256,1024]{1,0:T(8,128)(2,1)S(1)}, f32[256,1024]{1,0:T(8,128)S(1)}, bf16[256,1024]{1,0:T(8,128)(2,1)S(1)}, bf16[256,2048]{1,0:T(8,128)(2,1)S...) custom-call(s32[4]{0:T(128)S(1)} %pad_add_fusion.place, ...), custom_call_target="tpu_custom_call" | custom-call | flops 21474836 | bytes 158105 | tf_op jit(solution)/shard_map/feed_back/pallas_call | solution.py:98
  151.4 2.4 split.2
  157.0 3.3 collective-permute-done.32.refs_3_
  161.4 1.8 collective-permute-start.35
  165.6 4.8 %leave.2 = bf16[256,4,1024]{2,1,0:T(4,128)(2,1)} custom-call(s32[4]{0:T(128)S(1)} %pad_add_fusion.place, bf16[256,1024]{1,0:T(8,128)(2,1)S(1)} %get-tuple-element.313.refs_0_, bf16[256,1024]{1,0:T(8,128)(2,1)S(1)} %get-tuple-element.314.refs_1_, bf16[256,1024]{1,0:T(8,128)(2,1)S(1)} %collective-permute-done.31.refs_2_, ...), custom_call_target="tpu_custom_call" | custom-call | flops 5242 | bytes 41943 | tf_op jit(solution)/shard_map/leave/pallas_call | solution.py:77
  170.4 2.4 split.3
  173.8 7.0 %attend_back.2 = (bf16[256,384]{1,0:T(8,128)(2,1)S(1)}, bf16[256,384]{1,0:T(8,128)(2,1)S(1)}, bf16[256,384]{1,0:T(8,128)(2,1)S(1)}, bf16[256,384]{1,0:T(8,128)(2,1)S(1)}) custom-call(bf16[256,384]{1,0:T(8,128)(2,1)S(1)} %get-tuple-element.244.refs_0_, bf16[256,384]{1,0:T(8,128)(2,1)S(1)} %collective-permute-done.4.refs_1_, ...), custom_call_target="tpu_custom_call" | custom-call | flops 53687092 | bytes 18432 | tf_op jit(solution)/shard_map/attend_back/pallas_call | solution.py:98
  185.5 1.9 collective-permute-start.43
  187.3 4.7 %collective-permute-done.41.refs_5_ = bf16[256,128]{1,0:T(8,128)(2,1)S(1)} collective-permute-done((bf16[256,128]{1,0:T(8,128)(2,1)S(1)}, bf16[256,128]{1,0:T(8,128)(2,1)S(1)}, u32[]{:S(2)}, u32[]{:S(2)}) %collective-permute-start.41) | collective-permute-done | bytes 65568 | tf_op jit(solution)/shard_map/ppermute | solution.py:35
  192.6 1.9 collective-permute-start.40
  194.5 7.0 %attend_back.3 = (bf16[256,384]{1,0:T(8,128)(2,1)S(1)}, bf16[256,384]{1,0:T(8,128)(2,1)S(1)}, bf16[256,384]{1,0:T(8,128)(2,1)S(1)}, bf16[256,384]{1,0:T(8,128)(2,1)S(1)}) custom-call(bf16[256,384]{1,0:T(8,128)(2,1)S(1)} %get-tuple-element.249.refs_0_, bf16[256,384]{1,0:T(8,128)(2,1)S(1)} %collective-permute-done.7.refs_1_, ...), custom_call_target="tpu_custom_call" | custom-call | flops 53687092 | bytes 18432 | tf_op jit(solution)/shard_map/attend_back/pallas_call | solution.py:98
  204.1 1.9 collective-permute-start.47
  206.6 1.9 collective-permute-done.39.refs_2_
  208.5 1.6 project_back.2
  210.2 2.2 collective-permute-done.45.refs_1_
  212.4 12.2 %collective-permute-done.46.refs_2_ = bf16[256,384]{1,0:T(8,128)(2,1)S(1)} collective-permute-done((bf16[256,384]{1,0:T(8,128)(2,1)S(1)}, bf16[256,384]{1,0:T(8,128)(2,1)S(1)}, u32[]{:S(2)}, u32[]{:S(2)}) %collective-permute-start.46) | collective-permute-done | bytes 196640 | tf_op jit(solution)/shard_map/ppermute | solution.py:35
  224.6 1.7 project_back.3
  231.7 21.9 %collective-permute-done.48.refs_5_ = bf16[512,1024]{1,0:T(8,128)(2,1)S(1)} collective-permute-done((bf16[512,1024]{1,0:T(8,128)(2,1)S(1)}, bf16[512,1024]{1,0:T(8,128)(2,1)S(1)}, u32[]{:S(2)}, u32[]{:S(2)}) %collective-permute-start.48) | collective-permute-done | bytes 1048608 | tf_op jit(solution)/shard_map/ppermute | solution.py:35
  255.8 4.7 %collective-permute-start.64 = (bf16[128,1024]{1,0:T(8,128)(2,1)S(1)}, bf16[128,1024]{1,0:T(8,128)(2,1)S(1)}, u32[]{:S(2)}, u32[]{:S(2)}) collective-permute-start(bf16[128,1024]{1,0:T(8,128)(2,1)S(1)} %get-tuple-element.383), channel_id=1, source_target_pairs={{0,4},{4,0},{8,12},{12,8},{1,5},{5,1},{9,13},{13,9},{2,6},{6,2},{1... | collective-permute-start | bytes 786440 | tf_op jit(solution)/shard_map/ppermute | solution.py:35
  262.9 18.3 %collective-permute-done.57.refs_5_ = bf16[512,256]{1,0:T(8,128)(2,1)S(1)} collective-permute-done((bf16[512,256]{1,0:T(8,128)(2,1)S(1)}, bf16[512,256]{1,0:T(8,128)(2,1)S(1)}, u32[]{:S(2)}, u32[]{:S(2)}) %collective-permute-start.57) | collective-permute-done | bytes 262176 | tf_op jit(solution)/shard_map/ppermute | solution.py:35
  283.9 1.6 collective-permute-start.66
  287.1 16.3 %collective-permute-done.70 = f32[24,1024]{1,0:T(8,128)S(1)} collective-permute-done((f32[24,1024]{1,0:T(8,128)S(1)}, f32[24,1024]{1,0:T(8,128)S(1)}, u32[]{:S(2)}, u32[]{:S(2)}) %collective-permute-start.70) | collective-permute-done | bytes 98336 | tf_op jit(solution)/shard_map/ppermute | solution.py:35
  303.4 4.7 %collective-permute-start.61 = (bf16[128,1024]{1,0:T(8,128)(2,1)S(1)}, bf16[128,1024]{1,0:T(8,128)(2,1)S(1)}, u32[]{:S(2)}, u32[]{:S(2)}) collective-permute-start(bf16[128,1024]{1,0:T(8,128)(2,1)S(1)} %get-tuple-element.380), channel_id=1, source_target_pairs={{0,4},{4,0},{8,12},{12,8},{1,5},{5,1},{9,13},{13,9},{2,6},{6,2},{1... | collective-permute-start | bytes 786440 | tf_op jit(solution)/shard_map/ppermute | solution.py:35
  308.2 6.6 %collective-permute-done.61.refs_1_ = bf16[128,1024]{1,0:T(8,128)(2,1)S(1)} collective-permute-done((bf16[128,1024]{1,0:T(8,128)(2,1)S(1)}, bf16[128,1024]{1,0:T(8,128)(2,1)S(1)}, u32[]{:S(2)}, u32[]{:S(2)}) %collective-permute-start.61) | collective-permute-done | bytes 262176 | tf_op jit(solution)/shard_map/ppermute | solution.py:35
  314.8 1.9 collective-permute-start.62
  316.7 2.2 collective-permute-start.63
  322.8 13.6 %collective-permute-done.62.refs_2_ = bf16[128,1024]{1,0:T(8,128)(2,1)S(1)} collective-permute-done((bf16[128,1024]{1,0:T(8,128)(2,1)S(1)}, bf16[128,1024]{1,0:T(8,128)(2,1)S(1)}, u32[]{:S(2)}, u32[]{:S(2)}) %collective-permute-start.62) | collective-permute-done | bytes 262176 | tf_op jit(solution)/shard_map/ppermute | solution.py:35
  336.3 5.7 %collective-permute-start.54 = (bf16[128,768]{1,0:T(8,128)(2,1)S(1)}, bf16[128,768]{1,0:T(8,128)(2,1)S(1)}, u32[]{:S(2)}, u32[]{:S(2)}) collective-permute-start(bf16[128,768]{1,0:T(8,128)(2,1)S(1)} %get-tuple-element.372), channel_id=1, source_target_pairs={{0,4},{4,0},{8,12},{12,8},{1,5},{5,1},{9,13},{13,9},{2,6},{6,2},{1... | collective-permute-start | bytes 589832 | tf_op jit(solution)/shard_map/ppermute | solution.py:35
  342.6 1.9 collective-permute-start.56
  344.5 1.8 collective-permute-start.59
  346.3 2.2 collective-permute-start.60
  348.5 4.8 %leave.3 = f32[256,4,1024]{2,1,0:T(4,128)} custom-call(s32[4]{0:T(128)S(1)} %pad_add_fusion.place, f32[256,1024]{1,0:T(8,128)S(1)} %get-tuple-element.387.refs_0_, f32[256,1024]{1,0:T(8,128)S(1)} %get-tuple-element.388.refs_1_, f32[256,1024]{1,0:T(8,128)S(1)} %collective-permute-done.67.refs_2_, f32[256,1024]{1,0:T(8,128)S(1)} %collective-permute-done.68.refs_3_), custom_call_target="tpu_custom_call" | custom-call | flops 5242 | bytes 83886 | tf_op jit(solution)/shard_map/leave/pallas_call | solution.py:77
  355.1 10.0 %collective-permute-done.59.refs_2_ = bf16[128,256]{1,0:T(8,128)(2,1)S(1)} collective-permute-done((bf16[128,256]{1,0:T(8,128)(2,1)S(1)}, bf16[128,256]{1,0:T(8,128)(2,1)S(1)}, u32[]{:S(2)}, u32[]{:S(2)}) %collective-permute-start.59) | collective-permute-done | bytes 65568 | tf_op jit(solution)/shard_map/ppermute | solution.py:35
  366.6 2.6 finish.1
  (156 shorter events, 65.5 us)
Async XLA Ops:
  2.5 24.2 %collective-permute-start.1 = (bf16[512,768]{1,0:T(8,128)(2,1)S(1)}, bf16[512,768]{1,0:T(8,128)(2,1)S(1)}, u32[]{:S(2)}, u32[]{:S(2)}) collective-permute-start(bf16[512,768]{1,0:T(8,128)(2,1)S(1)} %pack.1.a_ref.refs_4_), channel_id=1, source_target_pairs={{0,1},{1,0},{2,3},{3,2},{4,5},{5,4},{6,7},{7,6},{8,9},{9,8},{10,11... | collective-permute-start | bytes 2359304 | tf_op jit(solution)/shard_map/ppermute | solution.py:35
  3.1 20.7 %collective-permute-start = (bf16[512,768]{1,0:T(8,128)(2,1)S(1)}, bf16[512,768]{1,0:T(8,128)(2,1)S(1)}, u32[]{:S(2)}, u32[]{:S(2)}) collective-permute-start(bf16[512,768]{1,0:T(8,128)(2,1)S(1)} %pack.1.a_ref.refs_4_), channel_id=1, source_target_pairs={{0,16},{16,0},{1,17},{17,1},{2,18},{18,2},{3,19},{19,3},{4,20},{20... | collective-permute-start | bytes 2359304 | tf_op jit(solution)/shard_map/ppermute | solution.py:35
  23.8 8.7 %collective-permute-start.16 = (bf16[512,256]{1,0:T(8,128)(2,1)S(1)}, bf16[512,256]{1,0:T(8,128)(2,1)S(1)}, u32[]{:S(2)}, u32[]{:S(2)}) collective-permute-start(bf16[512,256]{1,0:T(8,128)(2,1)S(1)} %get-tuple-element.266.refs_4_.a_ref), channel_id=1, source_target_pairs={{0,16},{16,0},{1,17},{17,1},{2,18},{18,2},{3,19},{19,3},{4,20},{20... | collective-permute-start | bytes 786440 | tf_op jit(solution)/shard_map/ppermute | solution.py:35
  32.5 57.4 %collective-permute-start.20 = (bf16[512,2048]{1,0:T(8,128)(2,1)S(1)}, bf16[512,2048]{1,0:T(8,128)(2,1)S(1)}, u32[]{:S(2)}, u32[]{:S(2)}) collective-permute-start(bf16[512,2048]{1,0:T(8,128)(2,1)S(1)} %get-tuple-element.278.a_ref), channel_id=1, source_target_pairs={{0,16},{16,0},{1,17},{17,1},{2,18},{18,2},{3,19},{19,3},{4,20},{20... | collective-permute-start | bytes 6291464 | tf_op jit(solution)/shard_map/ppermute | solution.py:35
  34.2 9.3 %collective-permute-start.4 = (bf16[256,384]{1,0:T(8,128)(2,1)S(1)}, bf16[256,384]{1,0:T(8,128)(2,1)S(1)}, u32[]{:S(2)}, u32[]{:S(2)}) collective-permute-start(bf16[256,384]{1,0:T(8,128)(2,1)S(1)} %get-tuple-element.237), channel_id=1, source_target_pairs={{0,4},{4,0},{8,12},{12,8},{1,5},{5,1},{9,13},{13,9},{2,6},{6,2},{1... | collective-permute-start | bytes 589832 | tf_op jit(solution)/shard_map/ppermute | solution.py:35
  35.8 17.2 %collective-permute-start.5 = (bf16[256,384]{1,0:T(8,128)(2,1)S(1)}, bf16[256,384]{1,0:T(8,128)(2,1)S(1)}, u32[]{:S(2)}, u32[]{:S(2)}) collective-permute-start(bf16[256,384]{1,0:T(8,128)(2,1)S(1)} %get-tuple-element.238), channel_id=1, source_target_pairs={{0,8},{4,12},{8,0},{12,4},{1,9},{5,13},{9,1},{13,5},{2,10},{6,14},... | collective-permute-start | bytes 589832 | tf_op jit(solution)/shard_map/ppermute | solution.py:35
  38.4 14.6 %collective-permute-start.6 = (bf16[256,384]{1,0:T(8,128)(2,1)S(1)}, bf16[256,384]{1,0:T(8,128)(2,1)S(1)}, u32[]{:S(2)}, u32[]{:S(2)}) collective-permute-start(bf16[256,384]{1,0:T(8,128)(2,1)S(1)} %get-tuple-element.239), channel_id=1, source_target_pairs={{0,12},{4,8},{8,4},{12,0},{1,13},{5,9},{9,5},{13,1},{2,14},{6,10},... | collective-permute-start | bytes 589832 | tf_op jit(solution)/shard_map/ppermute | solution.py:35
  38.6 19.8 %collective-permute-start.17 = (bf16[512,256]{1,0:T(8,128)(2,1)S(1)}, bf16[512,256]{1,0:T(8,128)(2,1)S(1)}, u32[]{:S(2)}, u32[]{:S(2)}) collective-permute-start(bf16[512,256]{1,0:T(8,128)(2,1)S(1)} %get-tuple-element.266.refs_4_.a_ref), channel_id=1, source_target_pairs={{0,1},{1,0},{2,3},{3,2},{4,5},{5,4},{6,7},{7,6},{8,9},{9,8},{10,11... | collective-permute-start | bytes 786440 | tf_op jit(solution)/shard_map/ppermute | solution.py:35
  53.0 9.2 %collective-permute-start.7 = (bf16[256,384]{1,0:T(8,128)(2,1)S(1)}, bf16[256,384]{1,0:T(8,128)(2,1)S(1)}, u32[]{:S(2)}, u32[]{:S(2)}) collective-permute-start(bf16[256,384]{1,0:T(8,128)(2,1)S(1)} %get-tuple-element.241), channel_id=1, source_target_pairs={{0,4},{4,0},{8,12},{12,8},{1,5},{5,1},{9,13},{13,9},{2,6},{6,2},{1... | collective-permute-start | bytes 589832 | tf_op jit(solution)/shard_map/ppermute | solution.py:35
  55.9 18.0 %collective-permute-start.8 = (bf16[256,384]{1,0:T(8,128)(2,1)S(1)}, bf16[256,384]{1,0:T(8,128)(2,1)S(1)}, u32[]{:S(2)}, u32[]{:S(2)}) collective-permute-start(bf16[256,384]{1,0:T(8,128)(2,1)S(1)} %get-tuple-element.242), channel_id=1, source_target_pairs={{0,8},{4,12},{8,0},{12,4},{1,9},{5,13},{9,1},{13,5},{2,10},{6,14},... | collective-permute-start | bytes 589832 | tf_op jit(solution)/shard_map/ppermute | solution.py:35
  57.0 17.0 %collective-permute-start.9 = (bf16[256,384]{1,0:T(8,128)(2,1)S(1)}, bf16[256,384]{1,0:T(8,128)(2,1)S(1)}, u32[]{:S(2)}, u32[]{:S(2)}) collective-permute-start(bf16[256,384]{1,0:T(8,128)(2,1)S(1)} %get-tuple-element.243), channel_id=1, source_target_pairs={{0,12},{4,8},{8,4},{12,0},{1,13},{5,9},{9,5},{13,1},{2,14},{6,10},... | collective-permute-start | bytes 589832 | tf_op jit(solution)/shard_map/ppermute | solution.py:35
  58.4 26.6 %collective-permute-start.18 = (bf16[512,256]{1,0:T(8,128)(2,1)S(1)}, bf16[512,256]{1,0:T(8,128)(2,1)S(1)}, u32[]{:S(2)}, u32[]{:S(2)}) collective-permute-start(bf16[512,256]{1,0:T(8,128)(2,1)S(1)} %collective-permute-done.16.refs_5_.b_ref), channel_id=1, source_target_pairs={{0,1},{1,0},{2,3},{3,2},{4,5},{5,4},{6,7},{7,6},{8,9},{9,8},{10,11... | collective-permute-start | bytes 786440 | tf_op jit(solution)/shard_map/ppermute | solution.py:35
  62.2 17.1 %collective-permute-start.13 = (bf16[256,128]{1,0:T(8,128)(2,1)S(1)}, bf16[256,128]{1,0:T(8,128)(2,1)S(1)}, u32[]{:S(2)}, u32[]{:S(2)}) collective-permute-start(bf16[256,128]{1,0:T(8,128)(2,1)S(1)} %get-tuple-element.258), channel_id=1, source_target_pairs={{0,4},{4,0},{8,12},{12,8},{1,5},{5,1},{9,13},{13,9},{2,6},{6,2},{1... | collective-permute-start | bytes 196616 | tf_op jit(solution)/shard_map/ppermute | solution.py:35
  73.9 8.7 %collective-permute-start.14 = (bf16[256,128]{1,0:T(8,128)(2,1)S(1)}, bf16[256,128]{1,0:T(8,128)(2,1)S(1)}, u32[]{:S(2)}, u32[]{:S(2)}) collective-permute-start(bf16[256,128]{1,0:T(8,128)(2,1)S(1)} %get-tuple-element.259), channel_id=1, source_target_pairs={{0,8},{4,12},{8,0},{12,4},{1,9},{5,13},{9,1},{13,5},{2,10},{6,14},... | collective-permute-start | bytes 196616 | tf_op jit(solution)/shard_map/ppermute | solution.py:35
  73.9 8.7 %collective-permute-start.15 = (bf16[256,128]{1,0:T(8,128)(2,1)S(1)}, bf16[256,128]{1,0:T(8,128)(2,1)S(1)}, u32[]{:S(2)}, u32[]{:S(2)}) collective-permute-start(bf16[256,128]{1,0:T(8,128)(2,1)S(1)} %get-tuple-element.260), channel_id=1, source_target_pairs={{0,12},{4,8},{8,4},{12,0},{1,13},{5,9},{9,5},{13,1},{2,14},{6,10},... | collective-permute-start | bytes 196616 | tf_op jit(solution)/shard_map/ppermute | solution.py:35
  79.3 6.8 %collective-permute-start.10 = (bf16[256,128]{1,0:T(8,128)(2,1)S(1)}, bf16[256,128]{1,0:T(8,128)(2,1)S(1)}, u32[]{:S(2)}, u32[]{:S(2)}) collective-permute-start(bf16[256,128]{1,0:T(8,128)(2,1)S(1)} %get-tuple-element.254), channel_id=1, source_target_pairs={{0,4},{4,0},{8,12},{12,8},{1,5},{5,1},{9,13},{13,9},{2,6},{6,2},{1... | collective-permute-start | bytes 196616 | tf_op jit(solution)/shard_map/ppermute | solution.py:35
  85.0 7.0 %collective-permute-start.21 = (bf16[512,2048]{1,0:T(8,128)(2,1)S(1)}, bf16[512,2048]{1,0:T(8,128)(2,1)S(1)}, u32[]{:S(2)}, u32[]{:S(2)}) collective-permute-start(bf16[512,2048]{1,0:T(8,128)(2,1)S(1)} %get-tuple-element.278.a_ref), channel_id=1, source_target_pairs={{0,1},{1,0},{2,3},{3,2},{4,5},{5,4},{6,7},{7,6},{8,9},{9,8},{10,11... | collective-permute-start | bytes 6291464 | tf_op jit(solution)/shard_map/ppermute | solution.py:35
  89.9 14.9 %collective-permute-start.22 = (bf16[512,2048]{1,0:T(8,128)(2,1)S(1)}, bf16[512,2048]{1,0:T(8,128)(2,1)S(1)}, u32[]{:S(2)}, u32[]{:S(2)}) collective-permute-start(bf16[512,2048]{1,0:T(8,128)(2,1)S(1)} %collective-permute-done.20.b_ref), channel_id=1, source_target_pairs={{0,1},{1,0},{2,3},{3,2},{4,5},{5,4},{6,7},{7,6},{8,9},{9,8},{10,11... | collective-permute-start | bytes 6291464 | tf_op jit(solution)/shard_map/ppermute | solution.py:35
  90.0 14.8 %collective-permute-start.19 = (bf16[256,1024]{1,0:T(8,128)(2,1)S(1)}, bf16[256,1024]{1,0:T(8,128)(2,1)S(1)}, u32[]{:S(2)}, u32[]{:S(2)}) collective-permute-start(bf16[256,1024]{1,0:T(8,128)(2,1)S(1)} %get-tuple-element.275.mine_ref), channel_id=1, source_target_pairs={{0,2},{1,3},{2,0},{3,1},{4,6},{5,7},{6,4},{7,5},{8,10},{9,11},{10,... | collective-permute-start | bytes 1572872 | tf_op jit(solution)/shard_map/ppermute | solution.py:35
  91.6 24.4 %collective-permute-start.23 = (bf16[256,1024]{1,0:T(8,128)(2,1)S(1)}, bf16[256,1024]{1,0:T(8,128)(2,1)S(1)}, u32[]{:S(2)}, u32[]{:S(2)}) collective-permute-start(bf16[256,1024]{1,0:T(8,128)(2,1)S(1)} %get-tuple-element.284.mine_ref), channel_id=1, source_target_pairs={{0,2},{1,3},{2,0},{3,1},{4,6},{5,7},{6,4},{7,5},{8,10},{9,11},{10,... | collective-permute-start | bytes 1572872 | tf_op jit(solution)/shard_map/ppermute | solution.py:35
  109.8 24.8 %collective-permute-start.24 = (bf16[256,1024]{1,0:T(8,128)(2,1)S(1)}, bf16[256,1024]{1,0:T(8,128)(2,1)S(1)}, u32[]{:S(2)}, u32[]{:S(2)}) collective-permute-start(bf16[256,1024]{1,0:T(8,128)(2,1)S(1)} %get-tuple-element.287.mine_ref), channel_id=1, source_target_pairs={{0,2},{1,3},{2,0},{3,1},{4,6},{5,7},{6,4},{7,5},{8,10},{9,11},{10,... | collective-permute-start | bytes 1572872 | tf_op jit(solution)/shard_map/ppermute | solution.py:35
  121.2 20.8 %collective-permute-start.28 = (bf16[256,1024]{1,0:T(8,128)(2,1)S(1)}, bf16[256,1024]{1,0:T(8,128)(2,1)S(1)}, u32[]{:S(2)}, u32[]{:S(2)}) collective-permute-start(bf16[256,1024]{1,0:T(8,128)(2,1)S(1)} %get-tuple-element.297.mine_ref), channel_id=1, source_target_pairs={{0,2},{1,3},{2,0},{3,1},{4,6},{5,7},{6,4},{7,5},{8,10},{9,11},{10,... | collective-permute-start | bytes 1572872 | tf_op jit(solution)/shard_map/ppermute | solution.py:35
  141.4 10.0 %collective-permute-start.29 = (bf16[256,1024]{1,0:T(8,128)(2,1)S(1)}, bf16[256,1024]{1,0:T(8,128)(2,1)S(1)}, u32[]{:S(2)}, u32[]{:S(2)}) collective-permute-start(bf16[256,1024]{1,0:T(8,128)(2,1)S(1)} %get-tuple-element.306.mine_ref), channel_id=1, source_target_pairs={{0,2},{1,3},{2,0},{3,1},{4,6},{5,7},{6,4},{7,5},{8,10},{9,11},{10,... | collective-permute-start | bytes 1572872 | tf_op jit(solution)/shard_map/ppermute | solution.py:35
  150.4 12.8 %collective-permute-start.30 = (bf16[1024,1024]{1,0:T(8,128)(2,1)S(1)}, bf16[1024,1024]{1,0:T(8,128)(2,1)S(1)}, u32[]{:S(2)}, u32[]{:S(2)}) collective-permute-start(bf16[1024,1024]{1,0:T(8,128)(2,1)S(1)} %grad_core.4), channel_id=1, source_target_pairs={{0,1},{1,0},{2,3},{3,2},{4,5},{5,4},{6,7},{7,6},{8,9},{9,8},{10,11... | collective-permute-start | bytes 6291464 | tf_op jit(solution)/shard_map/ppermute | solution.py:35
  155.3 17.5 %collective-permute-start.37 = (bf16[1024,1024]{1,0:T(8,128)(2,1)S(1)}, bf16[1024,1024]{1,0:T(8,128)(2,1)S(1)}, u32[]{:S(2)}, u32[]{:S(2)}) collective-permute-start(bf16[1024,1024]{1,0:T(8,128)(2,1)S(1)} %grad_core.5), channel_id=1, source_target_pairs={{0,1},{1,0},{2,3},{3,2},{4,5},{5,4},{6,7},{7,6},{8,9},{9,8},{10,11... | collective-permute-start | bytes 6291464 | tf_op jit(solution)/shard_map/ppermute | solution.py:35
  156.0 14.5 %collective-permute-start.33 = (bf16[256,1024]{1,0:T(8,128)(2,1)S(1)}, bf16[256,1024]{1,0:T(8,128)(2,1)S(1)}, u32[]{:S(2)}, u32[]{:S(2)}) collective-permute-start(bf16[256,1024]{1,0:T(8,128)(2,1)S(1)} %get-tuple-element.319.mine_ref), channel_id=1, source_target_pairs={{0,2},{1,3},{2,0},{3,1},{4,6},{5,7},{6,4},{7,5},{8,10},{9,11},{10,... | collective-permute-start | bytes 1572872 | tf_op jit(solution)/shard_map/ppermute | solution.py:35
  160.3 13.5 %collective-permute-start.34 = (bf16[256,128]{1,0:T(8,128)(2,1)S(1)}, bf16[256,128]{1,0:T(8,128)(2,1)S(1)}, u32[]{:S(2)}, u32[]{:S(2)}) collective-permute-start(bf16[256,128]{1,0:T(8,128)(2,1)S(1)} %get-tuple-element.322), channel_id=1, source_target_pairs={{0,4},{4,0},{8,12},{12,8},{1,5},{5,1},{9,13},{13,9},{2,6},{6,2},{1... | collective-permute-start | bytes 196616 | tf_op jit(solution)/shard_map/ppermute | solution.py:35
  161.4 12.4 %collective-permute-start.35 = (bf16[256,128]{1,0:T(8,128)(2,1)S(1)}, bf16[256,128]{1,0:T(8,128)(2,1)S(1)}, u32[]{:S(2)}, u32[]{:S(2)}) collective-permute-start(bf16[256,128]{1,0:T(8,128)(2,1)S(1)} %get-tuple-element.323), channel_id=1, source_target_pairs={{0,8},{4,12},{8,0},{12,4},{1,9},{5,13},{9,1},{13,5},{2,10},{6,14},... | collective-permute-start | bytes 196616 | tf_op jit(solution)/shard_map/ppermute | solution.py:35
  163.2 10.6 %collective-permute-start.36 = (bf16[256,128]{1,0:T(8,128)(2,1)S(1)}, bf16[256,128]{1,0:T(8,128)(2,1)S(1)}, u32[]{:S(2)}, u32[]{:S(2)}) collective-permute-start(bf16[256,128]{1,0:T(8,128)(2,1)S(1)} %get-tuple-element.324), channel_id=1, source_target_pairs={{0,12},{4,8},{8,4},{12,0},{1,13},{5,9},{9,5},{13,1},{2,14},{6,10},... | collective-permute-start | bytes 196616 | tf_op jit(solution)/shard_map/ppermute | solution.py:35
  181.8 22.3 %collective-permute-start.44 = (bf16[1024,256]{1,0:T(8,128)(2,1)S(1)}, bf16[1024,256]{1,0:T(8,128)(2,1)S(1)}, u32[]{:S(2)}, u32[]{:S(2)}) collective-permute-start(bf16[1024,256]{1,0:T(8,128)(2,1)S(1)} %grad_core.6), channel_id=1, source_target_pairs={{0,1},{1,0},{2,3},{3,2},{4,5},{5,4},{6,7},{7,6},{8,9},{9,8},{10,11... | collective-permute-start | bytes 1572872 | tf_op jit(solution)/shard_map/ppermute | solution.py:35
  181.9 20.7 %collective-permute-start.38 = (bf16[256,384]{1,0:T(8,128)(2,1)S(1)}, bf16[256,384]{1,0:T(8,128)(2,1)S(1)}, u32[]{:S(2)}, u32[]{:S(2)}) collective-permute-start(bf16[256,384]{1,0:T(8,128)(2,1)S(1)} %get-tuple-element.328), channel_id=1, source_target_pairs={{0,4},{4,0},{8,12},{12,8},{1,5},{5,1},{9,13},{13,9},{2,6},{6,2},{1... | collective-permute-start | bytes 589832 | tf_op jit(solution)/shard_map/ppermute | solution.py:35
  182.9 9.1 %collective-permute-start.41 = (bf16[256,128]{1,0:T(8,128)(2,1)S(1)}, bf16[256,128]{1,0:T(8,128)(2,1)S(1)}, u32[]{:S(2)}, u32[]{:S(2)}) collective-permute-start(bf16[256,128]{1,0:T(8,128)(2,1)S(1)} %get-tuple-element.333), channel_id=1, source_target_pairs={{0,4},{4,0},{8,12},{12,8},{1,5},{5,1},{9,13},{13,9},{2,6},{6,2},{1... | collective-permute-start | bytes 196616 | tf_op jit(solution)/shard_map/ppermute | solution.py:35
  184.0 8.6 %collective-permute-start.42 = (bf16[256,128]{1,0:T(8,128)(2,1)S(1)}, bf16[256,128]{1,0:T(8,128)(2,1)S(1)}, u32[]{:S(2)}, u32[]{:S(2)}) collective-permute-start(bf16[256,128]{1,0:T(8,128)(2,1)S(1)} %get-tuple-element.334), channel_id=1, source_target_pairs={{0,8},{4,12},{8,0},{12,4},{1,9},{5,13},{9,1},{13,5},{2,10},{6,14},... | collective-permute-start | bytes 196616 | tf_op jit(solution)/shard_map/ppermute | solution.py:35
  185.5 9.1 %collective-permute-start.43 = (bf16[256,128]{1,0:T(8,128)(2,1)S(1)}, bf16[256,128]{1,0:T(8,128)(2,1)S(1)}, u32[]{:S(2)}, u32[]{:S(2)}) collective-permute-start(bf16[256,128]{1,0:T(8,128)(2,1)S(1)} %get-tuple-element.335), channel_id=1, source_target_pairs={{0,12},{4,8},{8,4},{12,0},{1,13},{5,9},{9,5},{13,1},{2,14},{6,10},... | collective-permute-start | bytes 196616 | tf_op jit(solution)/shard_map/ppermute | solution.py:35
  192.0 16.5 %collective-permute-start.39 = (bf16[256,384]{1,0:T(8,128)(2,1)S(1)}, bf16[256,384]{1,0:T(8,128)(2,1)S(1)}, u32[]{:S(2)}, u32[]{:S(2)}) collective-permute-start(bf16[256,384]{1,0:T(8,128)(2,1)S(1)} %get-tuple-element.329), channel_id=1, source_target_pairs={{0,8},{4,12},{8,0},{12,4},{1,9},{5,13},{9,1},{13,5},{2,10},{6,14},... | collective-permute-start | bytes 589832 | tf_op jit(solution)/shard_map/ppermute | solution.py:35
  192.6 15.9 %collective-permute-start.40 = (bf16[256,384]{1,0:T(8,128)(2,1)S(1)}, bf16[256,384]{1,0:T(8,128)(2,1)S(1)}, u32[]{:S(2)}, u32[]{:S(2)}) collective-permute-start(bf16[256,384]{1,0:T(8,128)(2,1)S(1)} %get-tuple-element.330), channel_id=1, source_target_pairs={{0,12},{4,8},{8,4},{12,0},{1,13},{5,9},{9,5},{13,1},{2,14},{6,10},... | collective-permute-start | bytes 589832 | tf_op jit(solution)/shard_map/ppermute | solution.py:35
  201.6 10.8 %collective-permute-start.45 = (bf16[256,384]{1,0:T(8,128)(2,1)S(1)}, bf16[256,384]{1,0:T(8,128)(2,1)S(1)}, u32[]{:S(2)}, u32[]{:S(2)}) collective-permute-start(bf16[256,384]{1,0:T(8,128)(2,1)S(1)} %get-tuple-element.346), channel_id=1, source_target_pairs={{0,4},{4,0},{8,12},{12,8},{1,5},{5,1},{9,13},{13,9},{2,6},{6,2},{1... | collective-permute-start | bytes 589832 | tf_op jit(solution)/shard_map/ppermute | solution.py:35
  202.6 21.9 %collective-permute-start.46 = (bf16[256,384]{1,0:T(8,128)(2,1)S(1)}, bf16[256,384]{1,0:T(8,128)(2,1)S(1)}, u32[]{:S(2)}, u32[]{:S(2)}) collective-permute-start(bf16[256,384]{1,0:T(8,128)(2,1)S(1)} %get-tuple-element.347), channel_id=1, source_target_pairs={{0,8},{4,12},{8,0},{12,4},{1,9},{5,13},{9,1},{13,5},{2,10},{6,14},... | collective-permute-start | bytes 589832 | tf_op jit(solution)/shard_map/ppermute | solution.py:35
  204.1 20.4 %collective-permute-start.47 = (bf16[256,384]{1,0:T(8,128)(2,1)S(1)}, bf16[256,384]{1,0:T(8,128)(2,1)S(1)}, u32[]{:S(2)}, u32[]{:S(2)}) collective-permute-start(bf16[256,384]{1,0:T(8,128)(2,1)S(1)} %get-tuple-element.348), channel_id=1, source_target_pairs={{0,12},{4,8},{8,4},{12,0},{1,13},{5,9},{9,5},{13,1},{2,14},{6,10},... | collective-permute-start | bytes 589832 | tf_op jit(solution)/shard_map/ppermute | solution.py:35
  227.5 28.3 %collective-permute-start.49 = (bf16[1024,768]{1,0:T(8,128)(2,1)S(1)}, bf16[1024,768]{1,0:T(8,128)(2,1)S(1)}, u32[]{:S(2)}, u32[]{:S(2)}) collective-permute-start(bf16[1024,768]{1,0:T(8,128)(2,1)S(1)} %grad_core.7), channel_id=1, source_target_pairs={{0,1},{1,0},{2,3},{3,2},{4,5},{5,4},{6,7},{7,6},{8,9},{9,8},{10,11... | collective-permute-start | bytes 4718600 | tf_op jit(solution)/shard_map/ppermute | solution.py:35
  227.6 26.0 %collective-permute-start.48 = (bf16[512,1024]{1,0:T(8,128)(2,1)S(1)}, bf16[512,1024]{1,0:T(8,128)(2,1)S(1)}, u32[]{:S(2)}, u32[]{:S(2)}) collective-permute-start(bf16[512,1024]{1,0:T(8,128)(2,1)S(1)} %grad_shard.4), channel_id=1, source_target_pairs={{0,16},{16,0},{1,17},{17,1},{2,18},{18,2},{3,19},{19,3},{4,20},{20... | collective-permute-start | bytes 3145736 | tf_op jit(solution)/shard_map/ppermute | solution.py:35
  228.2 55.7 %collective-permute-start.52 = (bf16[512,1024]{1,0:T(8,128)(2,1)S(1)}, bf16[512,1024]{1,0:T(8,128)(2,1)S(1)}, u32[]{:S(2)}, u32[]{:S(2)}) collective-permute-start(bf16[512,1024]{1,0:T(8,128)(2,1)S(1)} %grad_shard.5), channel_id=1, source_target_pairs={{0,16},{16,0},{1,17},{17,1},{2,18},{18,2},{3,19},{19,3},{4,20},{20... | collective-permute-start | bytes 3145736 | tf_op jit(solution)/shard_map/ppermute | solution.py:35
  229.7 31.7 %collective-permute-start.50 = (bf16[256,1024]{1,0:T(8,128)(2,1)S(1)}, bf16[256,1024]{1,0:T(8,128)(2,1)S(1)}, u32[]{:S(2)}, u32[]{:S(2)}) collective-permute-start(bf16[256,1024]{1,0:T(8,128)(2,1)S(1)} %get-tuple-element.362.mine_ref), channel_id=1, source_target_pairs={{0,2},{1,3},{2,0},{3,1},{4,6},{5,7},{6,4},{7,5},{8,10},{9,11},{10,... | collective-permute-start | bytes 1572872 | tf_op jit(solution)/shard_map/ppermute | solution.py:35
  230.4 31.2 %collective-permute-start.51 = (bf16[256,1024]{1,0:T(8,128)(2,1)S(1)}, bf16[256,1024]{1,0:T(8,128)(2,1)S(1)}, u32[]{:S(2)}, u32[]{:S(2)}) collective-permute-start(bf16[256,1024]{1,0:T(8,128)(2,1)S(1)} %get-tuple-element.366.mine_ref), channel_id=1, source_target_pairs={{0,2},{1,3},{2,0},{3,1},{4,6},{5,7},{6,4},{7,5},{8,10},{9,11},{10,... | collective-permute-start | bytes 1572872 | tf_op jit(solution)/shard_map/ppermute | solution.py:35
  253.6 27.6 %collective-permute-start.57 = (bf16[512,256]{1,0:T(8,128)(2,1)S(1)}, bf16[512,256]{1,0:T(8,128)(2,1)S(1)}, u32[]{:S(2)}, u32[]{:S(2)}) collective-permute-start(bf16[512,256]{1,0:T(8,128)(2,1)S(1)} %grad_shard.6), channel_id=1, source_target_pairs={{0,16},{16,0},{1,17},{17,1},{2,18},{18,2},{3,19},{19,3},{4,20},{20... | collective-permute-start | bytes 786440 | tf_op jit(solution)/shard_map/ppermute | solution.py:35
  255.8 25.5 %collective-permute-start.64 = (bf16[128,1024]{1,0:T(8,128)(2,1)S(1)}, bf16[128,1024]{1,0:T(8,128)(2,1)S(1)}, u32[]{:S(2)}, u32[]{:S(2)}) collective-permute-start(bf16[128,1024]{1,0:T(8,128)(2,1)S(1)} %get-tuple-element.383), channel_id=1, source_target_pairs={{0,4},{4,0},{8,12},{12,8},{1,5},{5,1},{9,13},{13,9},{2,6},{6,2},{1... | collective-permute-start | bytes 786440 | tf_op jit(solution)/shard_map/ppermute | solution.py:35
  262.6 19.2 %collective-permute-start.69 = (f32[24,1024]{1,0:T(8,128)S(1)}, f32[24,1024]{1,0:T(8,128)S(1)}, u32[]{:S(2)}, u32[]{:S(2)}) collective-permute-start(f32[24,1024]{1,0:T(8,128)S(1)} %tally.1), channel_id=1, source_target_pairs={{0,1},{1,0},{2,3},{3,2},{4,5},{5,4},{6,7},{7,6},{8,9},{9,8},{10,11... | collective-permute-start | bytes 294920 | tf_op jit(solution)/shard_map/ppermute | solution.py:35
  262.7 19.6 %collective-permute-start.65 = (bf16[128,1024]{1,0:T(8,128)(2,1)S(1)}, bf16[128,1024]{1,0:T(8,128)(2,1)S(1)}, u32[]{:S(2)}, u32[]{:S(2)}) collective-permute-start(bf16[128,1024]{1,0:T(8,128)(2,1)S(1)} %get-tuple-element.384), channel_id=1, source_target_pairs={{0,8},{4,12},{8,0},{12,4},{1,9},{5,13},{9,1},{13,5},{2,10},{6,14},... | collective-permute-start | bytes 786440 | tf_op jit(solution)/shard_map/ppermute | solution.py:35
  281.2 63.3 %collective-permute-start.68 = (f32[256,1024]{1,0:T(8,128)S(1)}, f32[256,1024]{1,0:T(8,128)S(1)}, u32[]{:S(2)}, u32[]{:S(2)}) collective-permute-start(f32[256,1024]{1,0:T(8,128)S(1)} %get-tuple-element.388.refs_1_), channel_id=1, source_target_pairs={{0,1},{1,0},{2,3},{3,2},{4,5},{5,4},{6,7},{7,6},{8,9},{9,8},{10,11... | collective-permute-start | bytes 3145736 | tf_op jit(solution)/shard_map/ppermute | solution.py:35
  281.3 65.0 %collective-permute-start.67 = (f32[256,1024]{1,0:T(8,128)S(1)}, f32[256,1024]{1,0:T(8,128)S(1)}, u32[]{:S(2)}, u32[]{:S(2)}) collective-permute-start(f32[256,1024]{1,0:T(8,128)S(1)} %get-tuple-element.387.refs_0_), channel_id=1, source_target_pairs={{0,1},{1,0},{2,3},{3,2},{4,5},{5,4},{6,7},{7,6},{8,9},{9,8},{10,11... | collective-permute-start | bytes 3145736 | tf_op jit(solution)/shard_map/ppermute | solution.py:35
  281.8 37.2 %collective-permute-start.53 = (bf16[512,768]{1,0:T(8,128)(2,1)S(1)}, bf16[512,768]{1,0:T(8,128)(2,1)S(1)}, u32[]{:S(2)}, u32[]{:S(2)}) collective-permute-start(bf16[512,768]{1,0:T(8,128)(2,1)S(1)} %grad_shard.7), channel_id=1, source_target_pairs={{0,16},{16,0},{1,17},{17,1},{2,18},{18,2},{3,19},{19,3},{4,20},{20... | collective-permute-start | bytes 2359304 | tf_op jit(solution)/shard_map/ppermute | solution.py:35
  282.3 21.1 %collective-permute-start.70 = (f32[24,1024]{1,0:T(8,128)S(1)}, f32[24,1024]{1,0:T(8,128)S(1)}, u32[]{:S(2)}, u32[]{:S(2)}) collective-permute-start(f32[24,1024]{1,0:T(8,128)S(1)} %add.39), channel_id=1, source_target_pairs={{0,16},{16,0},{1,17},{17,1},{2,18},{18,2},{3,19},{19,3},{4,20},{20... | collective-permute-start | bytes 294920 | tf_op jit(solution)/shard_map/ppermute | solution.py:35
  283.9 24.2 %collective-permute-start.66 = (bf16[128,1024]{1,0:T(8,128)(2,1)S(1)}, bf16[128,1024]{1,0:T(8,128)(2,1)S(1)}, u32[]{:S(2)}, u32[]{:S(2)}) collective-permute-start(bf16[128,1024]{1,0:T(8,128)(2,1)S(1)} %get-tuple-element.385), channel_id=1, source_target_pairs={{0,12},{4,8},{8,4},{12,0},{1,13},{5,9},{9,5},{13,1},{2,14},{6,10},... | collective-permute-start | bytes 786440 | tf_op jit(solution)/shard_map/ppermute | solution.py:35
  303.4 11.4 %collective-permute-start.61 = (bf16[128,1024]{1,0:T(8,128)(2,1)S(1)}, bf16[128,1024]{1,0:T(8,128)(2,1)S(1)}, u32[]{:S(2)}, u32[]{:S(2)}) collective-permute-start(bf16[128,1024]{1,0:T(8,128)(2,1)S(1)} %get-tuple-element.380), channel_id=1, source_target_pairs={{0,4},{4,0},{8,12},{12,8},{1,5},{5,1},{9,13},{13,9},{2,6},{6,2},{1... | collective-permute-start | bytes 786440 | tf_op jit(solution)/shard_map/ppermute | solution.py:35
  308.1 8.6 %collective-permute-start.71 = (f32[24,1024]{1,0:T(8,128)S(1)}, f32[24,1024]{1,0:T(8,128)S(1)}, u32[]{:S(2)}, u32[]{:S(2)}) collective-permute-start(f32[24,1024]{1,0:T(8,128)S(1)} %add.40), channel_id=1, source_target_pairs={{0,4},{4,0},{8,12},{12,8},{1,5},{5,1},{9,13},{13,9},{2,6},{6,2},{1... | collective-permute-start | bytes 294920 | tf_op jit(solution)/shard_map/ppermute | solution.py:35
  314.8 21.5 %collective-permute-start.62 = (bf16[128,1024]{1,0:T(8,128)(2,1)S(1)}, bf16[128,1024]{1,0:T(8,128)(2,1)S(1)}, u32[]{:S(2)}, u32[]{:S(2)}) collective-permute-start(bf16[128,1024]{1,0:T(8,128)(2,1)S(1)} %get-tuple-element.381), channel_id=1, source_target_pairs={{0,8},{4,12},{8,0},{12,4},{1,9},{5,13},{9,1},{13,5},{2,10},{6,14},... | collective-permute-start | bytes 786440 | tf_op jit(solution)/shard_map/ppermute | solution.py:35
  316.7 19.6 %collective-permute-start.63 = (bf16[128,1024]{1,0:T(8,128)(2,1)S(1)}, bf16[128,1024]{1,0:T(8,128)(2,1)S(1)}, u32[]{:S(2)}, u32[]{:S(2)}) collective-permute-start(bf16[128,1024]{1,0:T(8,128)(2,1)S(1)} %get-tuple-element.382), channel_id=1, source_target_pairs={{0,12},{4,8},{8,4},{12,0},{1,13},{5,9},{9,5},{13,1},{2,14},{6,10},... | collective-permute-start | bytes 786440 | tf_op jit(solution)/shard_map/ppermute | solution.py:35
  319.0 23.7 %collective-permute-start.72 = (f32[24,1024]{1,0:T(8,128)S(1)}, f32[24,1024]{1,0:T(8,128)S(1)}, u32[]{:S(2)}, u32[]{:S(2)}) collective-permute-start(f32[24,1024]{1,0:T(8,128)S(1)} %add.41), channel_id=1, source_target_pairs={{0,8},{4,12},{8,0},{12,4},{1,9},{5,13},{9,1},{13,5},{2,10},{6,14},... | collective-permute-start | bytes 294920 | tf_op jit(solution)/shard_map/ppermute | solution.py:35
  336.3 6.3 %collective-permute-start.58 = (bf16[128,256]{1,0:T(8,128)(2,1)S(1)}, bf16[128,256]{1,0:T(8,128)(2,1)S(1)}, u32[]{:S(2)}, u32[]{:S(2)}) collective-permute-start(bf16[128,256]{1,0:T(8,128)(2,1)S(1)} %get-tuple-element.377), channel_id=1, source_target_pairs={{0,4},{4,0},{8,12},{12,8},{1,5},{5,1},{9,13},{13,9},{2,6},{6,2},{1... | collective-permute-start | bytes 196616 | tf_op jit(solution)/shard_map/ppermute | solution.py:35
  336.3 29.4 %collective-permute-start.54 = (bf16[128,768]{1,0:T(8,128)(2,1)S(1)}, bf16[128,768]{1,0:T(8,128)(2,1)S(1)}, u32[]{:S(2)}, u32[]{:S(2)}) collective-permute-start(bf16[128,768]{1,0:T(8,128)(2,1)S(1)} %get-tuple-element.372), channel_id=1, source_target_pairs={{0,4},{4,0},{8,12},{12,8},{1,5},{5,1},{9,13},{13,9},{2,6},{6,2},{1... | collective-permute-start | bytes 589832 | tf_op jit(solution)/shard_map/ppermute | solution.py:35
  342.6 23.1 %collective-permute-start.55 = (bf16[128,768]{1,0:T(8,128)(2,1)S(1)}, bf16[128,768]{1,0:T(8,128)(2,1)S(1)}, u32[]{:S(2)}, u32[]{:S(2)}) collective-permute-start(bf16[128,768]{1,0:T(8,128)(2,1)S(1)} %get-tuple-element.373), channel_id=1, source_target_pairs={{0,8},{4,12},{8,0},{12,4},{1,9},{5,13},{9,1},{13,5},{2,10},{6,14},... | collective-permute-start | bytes 589832 | tf_op jit(solution)/shard_map/ppermute | solution.py:35
  342.6 23.1 %collective-permute-start.56 = (bf16[128,768]{1,0:T(8,128)(2,1)S(1)}, bf16[128,768]{1,0:T(8,128)(2,1)S(1)}, u32[]{:S(2)}, u32[]{:S(2)}) collective-permute-start(bf16[128,768]{1,0:T(8,128)(2,1)S(1)} %get-tuple-element.374), channel_id=1, source_target_pairs={{0,12},{4,8},{8,4},{12,0},{1,13},{5,9},{9,5},{13,1},{2,14},{6,10},... | collective-permute-start | bytes 589832 | tf_op jit(solution)/shard_map/ppermute | solution.py:35
  344.5 20.6 %collective-permute-start.59 = (bf16[128,256]{1,0:T(8,128)(2,1)S(1)}, bf16[128,256]{1,0:T(8,128)(2,1)S(1)}, u32[]{:S(2)}, u32[]{:S(2)}) collective-permute-start(bf16[128,256]{1,0:T(8,128)(2,1)S(1)} %get-tuple-element.378), channel_id=1, source_target_pairs={{0,8},{4,12},{8,0},{12,4},{1,9},{5,13},{9,1},{13,5},{2,10},{6,14},... | collective-permute-start | bytes 196616 | tf_op jit(solution)/shard_map/ppermute | solution.py:35
  346.3 18.8 %collective-permute-start.60 = (bf16[128,256]{1,0:T(8,128)(2,1)S(1)}, bf16[128,256]{1,0:T(8,128)(2,1)S(1)}, u32[]{:S(2)}, u32[]{:S(2)}) collective-permute-start(bf16[128,256]{1,0:T(8,128)(2,1)S(1)} %get-tuple-element.379), channel_id=1, source_target_pairs={{0,12},{4,8},{8,4},{12,0},{1,13},{5,9},{9,5},{13,1},{2,14},{6,10},... | collective-permute-start | bytes 196616 | tf_op jit(solution)/shard_map/ppermute | solution.py:35
  (15 other events, 95.3 us)

commit v2 on v1

--- a/solution.py
+++ b/solution.py
@@ -23,11 +23,14 @@
 
 
 PINNED = False
-WEIGHT = 0.01
-
-
-def cost(flops, nbytes):
-    return pl.CostEstimate(flops=int(flops * WEIGHT), bytes_accessed=int(nbytes * WEIGHT), transcendentals=0)
+SCALES = {"project": 0.1, "attend": 1, "merge": 0.1, "feed": 0.1, "feed_back": 0.003, "split": 30, "attend_back": 1, "project_back": 100, "last": 10, "grad_core": 30, "grad_shard": 30, "grad_own": 30, "grad_sum": 30, "tally": 30, "leave": 30, "entry": 10, "own_rows": 1, "pack": 0.01, "pack_feed": 0.01}
+
+
+def cost(name, flops, nbytes):
+    scale = SCALES.get(name, 1)
+    return pl.CostEstimate(
+        flops=int(flops * scale), bytes_accessed=int(nbytes * scale), transcendentals=0
+    )
 
 
 def swap(value, axis, bit):
@@ -83,7 +86,7 @@
             out_specs=[pl.BlockSpec(b, without(f)) for _, _, b, f in outs],
         ),
         out_shape=[jax.ShapeDtypeStruct(s, d) for s, d, _, _ in outs],
-        cost_estimate=cost(work, nbytes),
+        cost_estimate=cost(name, work, nbytes),
         compiler_params=pltpu.CompilerParams(vmem_limit_bytes=16 << 20),
         name=name,
     )(place, *args)
@@ -102,7 +105,7 @@
         out_specs=[pl.BlockSpec(memory_space=pltpu.VMEM)] * len(outs),
         out_shape=[jax.ShapeDtypeStruct(s, d) for s, d in outs],
         scratch_shapes=scratch,
-        cost_estimate=cost(work, nbytes),
+        cost_estimate=cost(name, work, nbytes),
         compiler_params=pltpu.CompilerParams(vmem_limit_bytes=room << 20),
         name=name,
     )(*first, *args)
@@ -170,36 +173,33 @@
     )
 
 
-def leave_kernel(chunks, dtype, place, *refs):
+def leave_kernel(chunks, dtype, place, own_ref, other_ref, out_ref):
     core, flip = place[0], place[1]
-    *ins, out_ref = refs
-    own = [turned(ref[...].astype(F32), flip) for ref in ins[:chunks]]
-    other = [turned(ref[...].astype(F32), flip) for ref in ins[chunks:]]
+    own = [turned(own_ref[c].astype(F32), flip) for c in range(chunks)]
+    other = [turned(other_ref[c].astype(F32), flip) for c in range(chunks)]
     rows = [jnp.where(core == 0, a, b) for a, b in zip(own, other)]
     rows += [jnp.where(core == 0, b, a) for a, b in zip(own, other)]
     out_ref[...] = jnp.stack(rows, axis=1).astype(dtype)
 
 
-def leave(place, own):
-    chunks = len(own)
-    positions, width = own[0].shape
-    dtype = own[0].dtype
+def leave(place, own, other):
+    chunks, positions, width = own.shape
     block = math.gcd(64, positions)
-    arrays = [*own, *(swap_core(a) for a in own)]
+    piece = ((chunks, block, width), lambda i: (0, i, 0))
     return grid_call(
-        partial(leave_kernel, chunks, dtype),
+        partial(leave_kernel, chunks, own.dtype),
         "leave",
         (positions // block,),
-        [(a, (block, width), lambda i: (i, 0)) for a in arrays],
+        [(own, *piece), (other, *piece)],
         [
             (
                 (positions, 2 * chunks, width),
-                dtype,
+                own.dtype,
                 (block, 2 * chunks, width),
                 lambda i: (i, 0, 0),
             )
         ],
-        2 * positions * width,
+        2 * own.size,
         place=place,
         pinned=False,
     )[0]
@@ -290,7 +290,7 @@
 
 
 def project_back_kernel(pairs, place, *refs):
-    pieces, (a_ref, b_ref, c_ref, d_ref, flat_ref, out_ref, sums_ref, pairs_ref) = (
+    pieces, (a_ref, b_ref, c_ref, d_ref, flat_ref, out_ref, sums_ref, start_ref, pairs_ref) = (
         refs[:pairs],
         refs[pairs:],
     )
@@ -305,6 +305,7 @@
         value = contract(flat_ref[:, :middle], first[...], 1, 1)
         value += contract(flat_ref[:, middle:], second[...], 1, 1)
         out_ref[:, at : at + half] = value.astype(BF)
+        start_ref[:, at : at + half] = sum_rows(value)
     sums_ref[...] = sum_rows(flat_ref[...].astype(F32))
 
 
@@ -316,7 +317,12 @@
         partial(project_back_kernel, pairs),
         "project_back",
         (*pieces, *weights),
-        [((rows, pairs * columns), BF), ((rows, width), BF), ((1, pairs * columns), F32)],
+        [
+            ((rows, pairs * columns), BF),
+            ((rows, width), BF),
+            ((1, pairs * columns), F32),
+            ((1, width), F32),
+        ],
         2 * rows * width * pairs * columns,
         scratch=[pltpu.VMEM((pairs, rows, columns), BF)],
         place=place,
@@ -540,13 +546,15 @@
 
 
 def feed_back_kernel(
-    valid_row, tokens, place, first_ref, mine_ref, theirs_ref, vec_ref, teacher_ref, valid_ref, count_ref, slope_ref,
+    valid_row, tokens, place, earlier_ref, first_ref, mine_ref, theirs_ref, vec_ref, teacher_ref, valid_ref, count_ref, slope_ref,
     a_ref, b_ref, c_ref, d_ref, result_ref, grad_ref, low_ref, pre_ref, out_ref, sums_ref, pre_sums_ref, acc, valid_sums,
 ):
     second = valid_ref.shape[0] // 2 + valid_row
     valid = jnp.where(
         place[0] == 0, valid_ref[valid_row : valid_row + 1, :], valid_ref[second : second + 1, :]
     )
+    for c in range(valid_row):
+        result_ref[c] = earlier_ref[c]
     valid_sums[...] = jnp.broadcast_to(valid, (PAIR, valid.shape[1])).T
     sums_ref[...] = jnp.zeros_like(sums_ref)
     factor = 2.0 * tokens / count_ref[0:1, 0:1]
@@ -558,7 +566,7 @@
         total = normed + mine_ref[at, :].astype(F32) + theirs_ref[at, :].astype(F32) + vec_ref[3:4, :]
         unit, inverse = normal(total)
         result = unit * vec_ref[4:5, :] + vec_ref[5:6, :]
-        result_ref[at, :] = result.astype(BF)
+        result_ref[valid_row, at, :] = result.astype(BF)
         error = result - teacher_ref[at, :].astype(F32)
         result_grad = valid * factor * error
         grad = normal_back(result_grad * vec_ref[4:5, :], unit, inverse)
@@ -593,15 +601,15 @@
     out_ref[...] = acc[...].astype(BF)
 
 
-def feed_back(place, row, tokens, first, mine, theirs, vec, teacher, valid, count, slope, weights):
+def feed_back(place, row, tokens, earlier, first, mine, theirs, vec, teacher, valid, count, slope, weights):
     rows, width = first.shape
     units = slope.shape[1]
     return call(
         partial(feed_back_kernel, row, tokens),
         "feed_back",
-        (first, mine, theirs, vec, teacher, valid, count, slope, *weights),
+        (earlier, first, mine, theirs, vec, teacher, valid, count, slope, *weights),
         [
-            ((rows, width), BF),
+            ((row + 1, rows, width), BF),
             ((rows, width), F32),
             ((rows, width), BF),
             ((rows, units), BF),
@@ -629,6 +637,7 @@
         sums_ref[0:1, :] += sum_rows(grad * unit)
         sums_ref[1:2, :] += sum_rows(grad)
         sums_ref[2:3, :] += sum_rows(low.astype(F32))
+        sums_ref[3:4, :] += sum_rows(out)
 
     by_rows(grad_ref.shape[0], norm)
     half = a_ref.shape[0]
@@ -658,27 +667,27 @@
     )
 
 
-def last_kernel(grad_ref, mine_ref, theirs_ref, out_ref, sums_ref):
-    grad = grad_ref[...] + mine_ref[...].astype(F32) + theirs_ref[...].astype(F32)
-    out_ref[...] = grad
-    sums_ref[...] = jnp.broadcast_to(sum_rows(grad), sums_ref.shape)
-
-
-def last(grad, mine, theirs):
+def last_kernel(row, earlier_ref, grad_ref, mine_ref, theirs_ref, out_ref):
+    for c in range(row):
+        out_ref[c] = earlier_ref[c]
+    out_ref[row] = grad_ref[...] + mine_ref[...].astype(F32) + theirs_ref[...].astype(F32)
+
+
+def last(row, earlier, grad, mine, theirs):
     rows, width = grad.shape
     return call(
-        last_kernel,
+        partial(last_kernel, row),
         "last",
-        (grad, mine, theirs),
-        [((rows, width), F32), ((8, width), F32)],
+        (earlier, grad, mine, theirs),
+        [((row + 1, rows, width), F32)],
         4 * rows * width,
-    )
+    )[0]
 
 
 def tally_kernel(chunks, each, place, *refs):
     two, one = refs[:chunks], refs[chunks : 2 * chunks]
     pre, qkv = refs[2 * chunks : 3 * chunks], refs[3 * chunks : 4 * chunks]
-    zero, (features_ref, out_ref) = refs[4 * chunks : 5 * chunks], refs[5 * chunks :]
+    start, (features_ref, out_ref) = refs[4 * chunks : 5 * chunks], refs[5 * chunks :]
     core, flip, spot = place[0], place[1], place[3]
     add = lambda parts: sum(parts[1:], parts[0])
     out_ref[...] = jnp.zeros_like(out_ref)
@@ -692,26 +701,25 @@
         out_ref[8 + slot : 9 + slot, :] = jnp.where(mine, pre[:, :each], pre[:, each:])
         out_ref[10 + slot : 11 + slot, :size] = jnp.where(mine, qkv[:, :size], qkv[:, size:])
     seqs = 2 * chunks
-    for s in range(2 * seqs):
-        here = jnp.logical_and(flip == s // seqs, core == s % seqs // chunks)
-        row = turned(zero[s % chunks][0:1, :], flip)
-        out_ref[12 + s : 13 + s, :] = jnp.where(here, row, 0.0)
-    at = 12 + 2 * seqs
     features = features_ref[...].astype(F32)
     wide = features.shape[1]
     for s in range(2):
         here = jnp.logical_and(jnp.logical_and(core == 0, spot == 0), flip == s)
         for k in range(seqs):
             value = jnp.where(here, features[k : k + 1, :], 0.0)
-            out_ref[at + s : at + s + 1, k * wide : (k + 1) * wide] = value
-
-
-def tally(place, each, two, one, pre, qkv, zero, features):
-    rows = -(-(14 + 2 * features.shape[0]) // 8) * 8
+            out_ref[12 + s : 13 + s, k * wide : (k + 1) * wide] = value
+    for s in range(2 * seqs):
+        here = jnp.logical_and(flip == s // seqs, core == s % seqs // chunks)
+        row = turned(0.5 * one[s % chunks][3:4, :] + start[s % chunks][...], flip)
+        out_ref[16 + s : 17 + s, :] = jnp.where(here, row, 0.0)
+
+
+def tally(place, each, two, one, pre, qkv, start, features):
+    rows = -(-(16 + 2 * features.shape[0]) // 8) * 8
     return call(
         partial(tally_kernel, len(two), each),
         "tally",
-        (*two, *one, *pre, *qkv, *zero, features),
+        (*two, *one, *pre, *qkv, *start, features),
         [((rows, two[0].shape[1]), F32)],
         0,
         place=place,
@@ -740,17 +748,16 @@
     )
 
 
-def finish_kernel(each, size, shards, place, packed_ref, count_ref, time_ref, loss_ref, start_ref, hidden_ref, qkv_ref, *outs_and_all):
+def finish_kernel(each, size, shards, place, packed_ref, other_ref, count_ref, time_ref, loss_ref, start_ref, hidden_ref, qkv_ref, *outs_and_all):
     *outs, all_ref = outs_and_all
     seqs = all_ref.shape[0]
     wide = all_ref.shape[1]
     per_row = seqs // shards
-    at = 12 + seqs
     for s in range(seqs):
         k = s % per_row
-        row = at + s // per_row
+        row = 12 + s // per_row
         all_ref[s : s + 1, :] = packed_ref[row : row + 1, k * wide : (k + 1) * wide]
-    grads = packed_ref[12:at, :]
+    grads = packed_ref[16 : 16 + seqs, :] + other_ref[...]
     time_ref[...] = lax.dot_general(
         all_ref[...],
         grads,
@@ -768,12 +775,12 @@
         out[...] = packed_ref[row : row + 1, :]
 
 
-def finish(place, each, size, seqs, shards, wide, packed, count):
+def finish(place, each, size, seqs, shards, wide, packed, other, count):
     width = packed.shape[1]
     return call(
         partial(finish_kernel, each, size, shards),
         "finish",
-        (packed, count),
+        (packed, other, count),
         [((wide, width), F32), ((1, 1), F32), ((1, width), F32), ((1, each), F32), ((1, size), F32)]
         + [((1, width), F32)] * 6,
         0,
@@ -790,71 +797,87 @@
     return total
 
 
-def grad_core_kernel(chunks, *refs):
-    lefts, rights, out_ref = refs[:chunks], refs[chunks : 2 * chunks], refs[2 * chunks]
-    rows, columns = out_ref.shape
+def each_weight(weights, refs):
+    at, column, out = 0, 0, []
+    for chunks, columns in weights:
+        out.append((refs[at : at + chunks], refs[at + chunks : at + 2 * chunks], column, columns))
+        at += 2 * chunks
+        column += columns
+    return out, refs[at:]
+
+
+def weight_args(weights):
+    args = [a for lefts, rights in weights for a in (*lefts, *rights)]
+    shapes = [(len(lefts), rights[0].shape[1] // 2) for lefts, rights in weights]
+    tokens = sum(a.shape[0] for a in weights[0][0])
+    return args, shapes, weights[0][0][0].shape[1], sum(c for _, c in shapes), tokens
+
+
+def grad_core_kernel(weights, *refs):
+    weights, (out_ref,) = each_weight(weights, refs)
+    rows = out_ref.shape[0]
     step = math.gcd(512, rows)
 
     def part(i, carry):
         at = pl.ds(pl.multiple_of(i * step, step), step)
-        out_ref[at, :] = token_sum(lefts, rights, at, slice(columns, 2 * columns)).astype(BF)
+        for lefts, rights, first, columns in weights:
+            value = token_sum(lefts, rights, at, slice(columns, 2 * columns))
+            out_ref[at, first : first + columns] = value.astype(BF)
         return carry
 
     lax.fori_loop(0, rows // step, part, 0)
 
 
-def grad_core(lefts, rights):
-    rows, columns = lefts[0].shape[1], rights[0].shape[1] // 2
-    tokens = sum(a.shape[0] for a in lefts)
-    return call(
-        partial(grad_core_kernel, len(lefts)),
+def grad_core(weights):
+    args, shapes, rows, columns, tokens = weight_args(weights)
+    return call(
+        partial(grad_core_kernel, shapes),
         "grad_core",
-        (*lefts, *rights),
+        args,
         [((rows, columns), BF)],
         2 * tokens * rows * columns,
     )[0]
 
 
-def grad_shard_kernel(chunks, *refs):
-    lefts, rights, (core_ref, out_ref) = refs[:chunks], refs[chunks : 2 * chunks], refs[2 * chunks :]
-    half, columns = out_ref.shape
+def grad_shard_kernel(weights, *refs):
+    weights, (core_ref, out_ref) = each_weight(weights, refs)
+    half = out_ref.shape[0]
     size = math.gcd(256, half)
 
     def step(i, carry):
         at = pl.ds(pl.multiple_of(i * size, size), size)
         far = pl.ds(pl.multiple_of(half + i * size, size), size)
-        value = token_sum(lefts, rights, far, slice(0, columns))
-        out_ref[at, :] = (value + core_ref[far, :].astype(F32)).astype(BF)
+        for lefts, rights, first, columns in weights:
+            here = slice(first, first + columns)
+            value = token_sum(lefts, rights, far, slice(0, columns))
+            out_ref[at, here] = (value + core_ref[far, here].astype(F32)).astype(BF)
         return carry
 
     lax.fori_loop(0, half // size, step, 0)
 
 
-def grad_shard(lefts, rights, core):
-    half, columns = lefts[0].shape[1] // 2, rights[0].shape[1] // 2
-    tokens = sum(a.shape[0] for a in lefts)
-    return call(
-        partial(grad_shard_kernel, len(lefts)),
+def grad_shard(weights, core):
+    args, shapes, rows, columns, tokens = weight_args(weights)
+    return call(
+        partial(grad_shard_kernel, shapes),
         "grad_shard",
-        (*lefts, *rights, core),
-        [((half, columns), BF)],
-        2 * tokens * half * columns,
+        (*args, core),
+        [((rows // 2, columns), BF)],
+        tokens * rows * columns,
     )[0]
 
 
-def grad_own_kernel(chunks, place, *refs):
-    lefts, rights, (core_ref, shard_ref, *outs, acc) = (
-        refs[:chunks],
-        refs[chunks : 2 * chunks],
-        refs[2 * chunks :],
-    )
-    half, columns = acc.shape
+def grad_own_kernel(weights, place, *refs):
+    weights, (core_ref, shard_ref, *outs, acc) = each_weight(weights, refs)
+    half = acc.shape[0]
     size = math.gcd(256, half)
 
     def step(i, carry):
         at = pl.ds(pl.multiple_of(i * size, size), size)
-        value = token_sum(lefts, rights, at, slice(0, columns))
-        acc[at, :] = value + core_ref[at, :].astype(F32) + shard_ref[at, :].astype(F32)
+        for lefts, rights, first, columns in weights:
+            here = slice(first, first + columns)
+            value = token_sum(lefts, rights, at, slice(0, columns))
+            acc[at, here] = value + core_ref[at, here].astype(F32) + shard_ref[at, here].astype(F32)
         return carry
 
     lax.fori_loop(0, half // size, step, 0)
@@ -867,18 +890,21 @@
             out[...] = acc[pl.ds(at, rows), :].astype(out.dtype)
 
 
-def grad_own(place, lefts, rights, core, shard, pieces):
-    half, columns = lefts[0].shape[1] // 2, rights[0].shape[1] // 2
-    tokens = sum(a.shape[0] for a in lefts)
-    rows = half // pieces
-    return call(
-        partial(grad_own_kernel, len(lefts)),
+def grad_own(place, weights, core, shard, pieces):
+    args, shapes, rows, columns, tokens = weight_args(weights)
+    half = rows // 2
+    return call(
+        partial(grad_own_kernel, shapes),
         "grad_own",
-        (*lefts, *rights, core, shard),
-        [((rows, columns), F32 if pieces > 1 and d == 0 else BF) for d in range(pieces)],
-        2 * tokens * half * columns,
+        (*args, core, shard),
+        [
+            ((half // pieces, columns), F32 if pieces > 1 and d == 0 else BF)
+            for d in range(pieces)
+        ],
+        tokens * rows * columns,
         scratch=[pltpu.VMEM((half, columns), F32)],
         place=place,
+        room=16,
     )
 
 
@@ -946,6 +972,15 @@
     joined = joined.reshape(joined.shape[:2] + (-1, 2 * PAIR))
     owned = lax.psum_scatter(joined, "ctx", scatter_dimension=2, tiled=True)
     return jnp.concatenate([q_grad.reshape(grad.shape).astype(BF), owned], axis=-1)
+
+
+GATE = 0
+
+
+class Values:
+    def __getattr__(self, name):
+        self.__dict__[name] = made = {}
+        return made
 
 
 class Order:
@@ -1024,193 +1059,215 @@
     count = jnp.full((8, 128), jnp.sum(valid), F32)
     embed = jnp.dot(time_features, w_time, preferred_element_type=F32) + b_time
     place, vec, valid, embed, count = lax.optimization_barrier((place, vec, valid, embed, count))
-    count = sum_ctx(count)
-    count = count + swap_shard(after(count, qkv_across))
     tokens_all = positions * seqs * ctx * shards
     rows = entry(place, inputs, embed)
     low, start = rows[:chunks], rows[chunks:]
-    out_mine, feed_mine = pack_feed(after(place, low[0]), w_output, w_hidden, w_down)
+    near = sum_ctx(count)
+    count = near + swap_shard(after(near, qkv_across))
+    out_mine, feed_mine = pack_feed(after(place, low[0], near), w_output, w_hidden, w_down)
     out_side, feed_side = swap_core(out_mine), swap_core(feed_mine)
-    teachers = own_rows(after(place, out_mine), teacher)
-    order.mark(teachers[0])
-
-    qkv_weights = (qkv_mine, qkv_across, qkv_side, swap_core(after(qkv_across, teachers[0])))
+    order.mark(out_mine)
+
+    qkv_weights = (qkv_mine, qkv_across, qkv_side, swap_core(after(qkv_across, feed_mine)))
     out_across = swap_shard(after(out_mine, qkv_across))
-    slots = []
-    for c in range(chunks):
+    val = Values()
+
+    def run_project(c):
         (held,) = order.hold(low[c])
-        slots.append(project(place, each, held, qkv_weights, biases))
-        order.mark(slots[c][0])
-    feed_across = swap_shard(after(feed_mine, out_across, slots[-1][0]))
-    out_weights = (out_mine, out_across, out_side, swap_core(after(out_across, slots[-1][0])))
-    kept, mixed = [], []
-    for c in range(chunks):
+        val.slots[c] = project(place, each, held, qkv_weights, biases)
+        order.mark(val.slots[c][0])
+        if not val.out:
+            behind = val.slots[c][0]
+            val.feed_across[0] = swap_shard(after(feed_mine, out_across, behind))
+            val.out[0] = (out_mine, out_across, out_side, swap_core(after(out_across, behind)))
+
+    def run_teacher():
+        (held,) = order.hold(place)
+        val.teacher[0] = own_rows(held, teacher)
+        order.mark(val.teacher[0][0])
+
+    def run_attend(c):
+        slots = val.slots[c]
         if by_units:
-            sent = slots[c]
-            if c > 0:
-                sent = list(lax.optimization_barrier((*sent, *kept[c - 1][0]))[: len(sent)])
-            pieces = swap_ctx(sent)
+            if c > 0 and GATE:
+                behind = val.kept[c - 1][0][-GATE:]
+                slots = list(lax.optimization_barrier((*slots, *behind))[: len(slots)])
+            pieces = swap_ctx(slots)
             *outs, logs = attend(order.hold(*pieces), scale)
             order.mark(logs)
-            mixed.append(swap_ctx(outs))
-            kept.append((pieces, logs))
+            val.mixed[c] = swap_ctx(outs)
+            val.kept[c] = (pieces, logs)
         else:
-            value, saved = gathered_forward(jnp.stack(slots[c])[:, None], scale)
-            mixed.append([value[p, 0] for p in range(pairs)])
-            kept.append(saved)
-    firsts, norms, hiddens, slopes, feeds, flats, branches = [], [], [], [], [], [], []
-    for c in range(chunks):
-        held = order.hold(*mixed[c])
-        flat, mine = merge(place, held, out_weights)
+            value, saved = gathered_forward(jnp.stack(slots)[:, None], scale)
+            val.mixed[c] = [value[p, 0] for p in range(pairs)]
+            val.kept[c] = saved
+
+    def run_merge(c):
+        held = order.hold(*val.mixed[c])
+        flat, mine = merge(place, held, val.out[0])
         order.mark(flat)
-        flats.append(flat)
-        branches.append((mine, swap_outer(mine)))
-    feed_weights = (feed_mine, feed_across, feed_side, swap_core(after(feed_across, order.last)))
-    for c in range(chunks):
-        (held,) = order.hold(start[c])
-        first, normed, hidden, slope, mine = feed(held, *branches[c], vec, biases, feed_weights)
+        val.flat[c] = flat
+        val.branch[c] = (mine, swap_outer(mine))
+        if not val.feed_weights:
+            across = val.feed_across[0]
+            side = swap_core(after(across, flat))
+            val.feed_weights[0] = (feed_mine, across, feed_side, side)
+
+    def run_feed(c):
+        held, _ = order.hold(start[c], count)
+        first, normed, hidden, slope, mine = feed(
+            held, *val.branch[c], vec, biases, val.feed_weights[0]
+        )
         order.mark(normed)
-        firsts.append(first)
-        norms.append(normed)
-        hiddens.append(hidden)
-        slopes.append(slope)
-        feeds.append((mine, swap_outer(mine)))
-
-    results, sum_grads, feed_lows, pre_grads, backs, two_sums, pre_sums = [], [], [], [], [], [], []
-    for c in range(chunks):
-        (held,) = order.hold(firsts[c])
-        result, sum_grad, feed_low, pre_grad, mine, two, pre_sum = feed_back(
-            place, c, tokens_all, held, *feeds[c], vec, teachers[c], valid, count, slopes[c], feed_weights
+        val.first[c], val.norm[c], val.hidden[c], val.slope[c] = first, normed, hidden, slope
+        val.feed[c] = (mine, swap_outer(mine))
+
+    def run_feed_back(c):
+        (held,) = order.hold(val.first[c])
+        earlier = val.result[c - 1] if c else vec[None]
+        args = (held, *val.feed[c], vec, val.teacher[0][c], valid, count, val.slope[c])
+        result, grad, low_grad, pre_grad, mine, two, pre_sum = feed_back(
+            place, c, tokens_all, earlier, *args, val.feed_weights[0]
         )
         order.mark(pre_sum)
-        results.append(result)
-        sum_grads.append(sum_grad)
-        feed_lows.append(feed_low)
-        pre_grads.append(pre_grad)
-        backs.append((mine, swap_outer(mine)))
-        two_sums.append(two)
-        pre_sums.append(pre_sum)
-
-    class Weight:
-        def __init__(self, lefts, rights):
-            self.lefts, self.rights = lefts, rights
-
-        def held(self):
-            first, = order.hold(self.lefts[0])
-            return [first, *self.lefts[1:]]
-
-        def core(self):
-            value = order.mark(grad_core(self.held(), self.rights))
-            self.from_core = swap_core(value)
-
-        def shard(self):
-            value = order.mark(grad_shard(self.held(), self.rights, self.from_core))
-            self.from_shard = swap_shard(value)
-
-        def own(self):
-            count = ctx if by_units else 1
-            own = grad_own(place, self.held(), self.rights, self.from_core, self.from_shard, count)
-            order.mark(own[0])
-            if by_units:
-                self.pieces = swap_ctx(own)
-            else:
-                pieces = lax.all_to_all(own[0].reshape(ctx, half // ctx, -1), "ctx", 0, 0)
-                self.pieces = [jnp.sum(pieces.astype(F32), axis=0)]
-
-        def total(self, cuts):
-            outs = grad_sum(order.hold(*self.pieces), cuts)
-            order.mark(outs[0])
-            return outs
-
-    first_grads, branch_lows, one_sums, mixed_grads = [], [], [], []
+        val.result[c], val.sum_grad[c], val.feed_low[c] = result, grad, low_grad
+        val.pre_grad[c], val.two[c], val.pre_sum[c] = pre_grad, two, pre_sum
+        val.back[c] = (mine, swap_outer(mine))
+        if c == chunks - 1:
+            val.result_other[0] = swap_core(result)
 
     def run_split(c):
-        (held,) = order.hold(sum_grads[c])
+        (held,) = order.hold(val.sum_grad[c])
         first_grad, branch_low, one, *outs = split(
-            place, held, *backs[c], firsts[c], vec, out_weights
+            place, held, *val.back[c], val.first[c], vec, val.out[0]
         )
         order.mark(one)
-        first_grads.append(first_grad)
-        branch_lows.append(branch_low)
-        one_sums.append(one)
-        mixed_grads.append(swap_ctx(outs) if by_units else outs)
-
-    qkv_grads = []
+        val.first_grad[c], val.branch_low[c], val.one[c] = first_grad, branch_low, one
+        val.mixed_grad[c] = swap_ctx(outs) if by_units else outs
 
     def run_attend_back(c):
         if by_units:
-            pieces, logs = kept[c]
+            pieces, logs = val.kept[c]
             (logs,) = order.hold(logs)
-            outs = attend_back(pieces, mixed_grads[c], logs, scale)
+            outs = attend_back(pieces, val.mixed_grad[c], logs, scale)
             order.mark(outs[0])
-            qkv_grads.append(swap_ctx(outs))
+            val.qkv_grad[c] = swap_ctx(outs)
         else:
-            value = gathered_backward(kept[c], jnp.stack(mixed_grads[c])[:, None], scale)
-            qkv_grads.append([value[p, 0] for p in range(pairs)])
-
-    qkv_sums, qkv_flats, last_parts = [], [], []
+            value = gathered_backward(
+                val.kept[c], jnp.stack(val.mixed_grad[c])[:, None], scale
+            )
+            val.qkv_grad[c] = [value[p, 0] for p in range(pairs)]
 
     def run_project_back(c):
-        held = order.hold(*qkv_grads[c])
-        flat, mine, qkv_sum = project_back(place, held, qkv_weights)
+        held = order.hold(*val.qkv_grad[c])
+        flat, mine, qkv_sum, start_sum = project_back(place, held, qkv_weights)
         order.mark(qkv_sum)
-        qkv_sums.append(qkv_sum)
-        qkv_flats.append(flat)
-        last_parts.append((mine, swap_outer(mine)))
-
-    starts, zero_sums = [], []
+        val.qkv_sum[c], val.qkv_flat[c], val.start_sum[c] = qkv_sum, flat, start_sum
+        val.last[c] = (mine, swap_outer(mine))
 
     def run_last(c):
-        (held,) = order.hold(first_grads[c])
-        start_grad, zero = last(held, *last_parts[c])
-        order.mark(zero)
-        starts.append(start_grad)
-        zero_sums.append(zero)
-
-    down = Weight(feed_lows, hiddens)
-    hidden = Weight(norms, pre_grads)
-    output = Weight(branch_lows, flats)
-    qkv = Weight(low, qkv_flats)
-    down.core()
+        (held,) = order.hold(val.first_grad[c])
+        earlier = val.start[c - 1] if c else held[None]
+        val.start[c] = order.mark(last(c, earlier, held, *val.last[c]))
+        if c == chunks - 1:
+            val.start_other[0] = swap_core(val.start[c])
+
+    def every(values):
+        return [values[c] for c in range(chunks)]
+
+    def held_pairs(name):
+        if name == "f":
+            pairs_of = [(every(val.norm), every(val.pre_grad)), (every(val.feed_low), every(val.hidden))]
+        else:
+            pairs_of = [(low, every(val.qkv_flat)), (every(val.branch_low), every(val.flat))]
+        (lefts, rights), *others = pairs_of
+        (first,) = order.hold(lefts[0])
+        return [([first, *lefts[1:]], rights), *others]
+
+    def run_core(name):
+        val.core[name] = swap_core(order.mark(grad_core(held_pairs(name))))
+
+    def run_shard(name):
+        value = order.mark(grad_shard(held_pairs(name), val.core[name]))
+        val.shard[name] = swap_shard(value)
+
+    def run_own(name):
+        number = ctx if by_units else 1
+        own = grad_own(place, held_pairs(name), val.core[name], val.shard[name], number)
+        order.mark(own[0])
+        if by_units:
+            val.pieces[name] = swap_ctx(own)
+        else:
+            pieces = lax.all_to_all(own[0].reshape(ctx, half // ctx, -1), "ctx", 0, 0)
+            val.pieces[name] = [jnp.sum(pieces.astype(F32), axis=0)]
+
+    wide = 3 * columns
+    cuts = {
+        "f": [[(0, each)], [(each, each)]],
+        "a": [[((3 * g + j) * PAIR, PAIR) for g in range(per_core)] for j in range(3)]
+        + [[(wide, columns)]],
+    }
+
+    def run_total(name):
+        val.grad[name] = grad_sum(order.hold(*val.pieces[name]), cuts[name])
+        order.mark(val.grad[name][0])
+
+    def run_leave(last):
+        (held,) = order.hold(place)
+        kind = val.start if last else val.result
+        other = val.start_other if last else val.result_other
+        val.leave[last] = order.mark(leave(held, kind[chunks - 1], other[0]))
+
+    def run_tally():
+        sums = [every(v) for v in (val.two, val.one, val.pre_sum, val.qkv_sum, val.start_sum)]
+        sums[0][0] = order.hold(sums[0][0])[0]
+        packed = order.mark(tally(place, each, *sums, time_features))
+        packed = sum_ctx(packed)
+        packed = packed + swap_core(packed)
+        packed = packed + swap_shard(packed)
+        val.packed[0] = (packed, swap_outer(packed[16 : 16 + shards * seqs]))
+
+    def run_finish():
+        (held,) = order.hold(place)
+        sizes = (each, 3 * columns, shards * seqs, shards, time_features.shape[1])
+        val.finish[0] = finish(held, *sizes, *val.packed[0], count)
+        order.mark(val.finish[0][1])
+
+    run_project(0)
+    run_teacher()
+    run_project(1)
+    run_attend(0)
+    run_attend(1)
+    run_merge(0)
+    run_merge(1)
+    run_feed(0)
+    run_feed(1)
+    run_feed_back(0)
+    run_feed_back(1)
     run_split(0)
-    hidden.core()
-    down.shard()
-    (held,) = order.hold(place)
-    layer_out = order.mark(leave(held, results))
+    run_core("f")
+    run_shard("f")
     run_split(1)
-    hidden.shard()
     run_attend_back(0)
-    output.core()
     run_attend_back(1)
-    output.shard()
+    run_leave(False)
     run_project_back(0)
     run_project_back(1)
-    qkv.core()
-    down.own()
-    qkv.shard()
+    run_tally()
+    run_core("a")
+    run_own("f")
     run_last(0)
+    run_shard("a")
     run_last(1)
-    packed = order.mark(
-        tally(place, each, two_sums, one_sums, pre_sums, qkv_sums, zero_sums, time_features)
-    )
-    packed = sum_tokens(packed + swap_core(packed))
-    hidden.own()
-    qkv.own()
-    output.own()
-    (held,) = order.hold(place)
-    grad_inputs = order.mark(leave(held, starts))
-    everything = lambda weight: [[(0, weight.rights[0].shape[1] // 2)]]
-    (grad_w_down,) = down.total(everything(down))
-    (grad_w_hidden,) = hidden.total(everything(hidden))
-    (grad_w_output,) = output.total(everything(output))
-    grad_w_query, grad_w_key, grad_w_value = qkv.total(
-        [[((3 * g + j) * PAIR, PAIR) for g in range(per_core)] for j in range(3)]
-    )
-
-    (held,) = order.hold(place)
-    grad_w_time, loss, start_sum, hidden_sum, qkv_sum, *rest = finish(
-        held, each, 3 * columns, shards * seqs, shards, time_features.shape[1], packed, count
-    )
+    run_total("f")
+    run_own("a")
+    run_leave(True)
+    run_finish()
+    run_total("a")
+    layer_out, grad_inputs = val.leave[False], val.leave[True]
+    grad_w_hidden, grad_w_down = val.grad["f"]
+    grad_w_query, grad_w_key, grad_w_value, grad_w_output = val.grad["a"]
+    grad_w_time, loss, start_sum, hidden_sum, qkv_sum, *rest = val.finish[0]
     qkv_sum = qkv_sum.reshape(per_core, 3, PAIR)
     return (
         layer_out,

time: 370 us -> 300 us (0.81)
  waiting for transfers between devices: 170 us -> 90.2 us
  starting transfers between devices: 89.1 us -> 97 us
    ppermute x73 -> x62, waiting for transfers between devices: 170 us -> 90.2 us  [swap(): return lax.ppermute(value, axis, [(i, i ^ bit) for i in range(size)])]
    ppermute x73 -> x62, starting transfers between devices: 89.1 us -> 97 us  [swap(): return lax.ppermute(value, axis, [(i, i ^ bit) for i in range(size)])]
    pallas_call x36 -> x28, Pallas kernels: 81.5 us -> 81.4 us  [call(): pl.pallas_call(kernel, in_specs=[pl.BlockSpec(memory_space=pltpu.SMEM)] *...]
  transfers between devices with their start and end apart: 73 -> 62, of which waited for: 27 -> 21; matrix products, arithmetic and copies ran while one was open for 1% -> 2% of each run, Pallas kernels for 24% -> 32%
where the time goes in v2:
time: 300 us; the launch traced here: 299 us
  Pallas kernels  104 us (35%)
  starting transfers between devices  97 us (32%)
  waiting for transfers between devices  90.2 us (30%)
  local copies, waits for them, and re-layouts  3.35 us (1%)
    ppermute x62, starting transfers between devices, swap(): return lax.ppermute(value, axis, [(i, i ^ bit) for i in range(size)])  97 us
    ppermute x62, waiting for transfers between devices, swap(): return lax.ppermute(value, axis, [(i, i ^ bit) for i in range(size)])  90.2 us
    pallas_call x28, Pallas kernels, call(): pl.pallas_call(kernel, in_specs=[pl.BlockSpec(memory_space=pltpu.SMEM)] *...  81.4 us
    pallas_call x6, Pallas kernels, grid_call(): pl.pallas_call(kernel, grid_spec=pltpu.PrefetchScalarGridSpec(num_scalar_...  22.5 us
  transfers between devices with their start and end apart: 62, of which 21 were waited for; matrix products, arithmetic and copies ran while one was open for 2% of the time, Pallas kernels for 32%

profile of v2, /device:TPU:0, one launch (start us, length us, event | category | flops | bytes accessed | tf_op | source)
XLA Modules:
  0.0 299.4 jit_solution(5678654786339233283)
XLA Ops:
  0.8 1.8 pack.1.a_ref.refs_4_
  2.5 3.0 %collective-permute-start.2 = (bf16[512,768]{1,0:T(8,128)(2,1)S(1)}, bf16[512,768]{1,0:T(8,128)(2,1)S(1)}, u32[]{:S(2)}, u32[]{:S(2)}) collective-permute-start(bf16[512,768]{1,0:T(8,128)(2,1)S(1)} %pack.1.a_ref.refs_4_), channel_id=1, source_target_pairs={{0,16},{16,0},{1,17},{17,1},{2,18},{18,2},{3,19},{19,3},{4,20},{20... | collective-permute-start | bytes 2359304 | tf_op jit(solution)/shard_map/ppermute | solution.py:38
  10.6 1.6 collective-permute-start
  12.2 2.0 collective-permute-done
  14.3 2.7 collective-permute-start.1
  16.9 4.1 %entry.1 = (bf16[256,1024]{1,0:T(8,128)(2,1)S(1)}, bf16[256,1024]{1,0:T(8,128)(2,1)S(1)}, f32[256,1024]{1,0:T(8,128)S(1)}, f32[256,1024]{1,0:T(8,128)S(1)}) custom-call(s32[4]{0:T(128)S(1)} %pad_add_fusion.place, bf16[256,4,1024]{2,1,0:T(4,128)(2,1)} %x_ref.2, f32[4,1024]{1,0:T(4,128)} %convolution_add_fusion.embed_ref), custom_call_target="tpu_custom_call" | custom-call | flops 41943040 | bytes 52592640 | tf_op jit(solution)/shard_map/entry/pallas_call | solution.py:80
  21.1 3.0 %pack_feed.1 = (bf16[512,256]{1,0:T(8,128)(2,1)S(1)}, bf16[512,2048]{1,0:T(8,128)(2,1)S(1)}) custom-call(s32[4]{0:T(128)S(1)} %pad_add_fusion.place, bf16[512,256]{1,0:T(8,128)(2,1)} %out_ref.1, bf16[512,1024]{1,0:T(8,128)(2,1)} %up_ref.1, bf16[512,1024]{1,0:T(8,128)(2,1)} %down_ref.1), custom_call_target="tpu_custom_call" | custom-call | bytes 47185 | tf_op jit(solution)/shard_map/pack_feed/pallas_call | solution.py:80
  26.5 2.4 project.2
  28.8 4.1 %collective-permute-done.19.refs_5_.b_ref = bf16[512,256]{1,0:T(8,128)(2,1)S(1)} collective-permute-done((bf16[512,256]{1,0:T(8,128)(2,1)S(1)}, bf16[512,256]{1,0:T(8,128)(2,1)S(1)}, u32[]{:S(2)}, u32[]{:S(2)}) %collective-permute-start.19) | collective-permute-done | bytes 262176 | tf_op jit(solution)/shard_map/ppermute | solution.py:38
  33.6 1.6 collective-permute-start.10
  35.1 2.6 collective-permute-start.11
  37.9 3.7 %own_rows.1 = (bf16[256,1024]{1,0:T(8,128)(2,1)S(1)}, bf16[256,1024]{1,0:T(8,128)(2,1)S(1)}) custom-call(s32[4]{0:T(128)S(1)} %pad_add_fusion.place, bf16[256,4,1024]{2,1,0:T(4,128)(2,1)} %x_ref.3), custom_call_target="tpu_custom_call" | custom-call | flops 2097152 | bytes 3145728 | tf_op jit(solution)/shard_map/own_rows/pallas_call | solution.py:80
  41.6 2.4 project.3
  44.7 3.5 %collective-permute-start.7 = (bf16[256,384]{1,0:T(8,128)(2,1)S(1)}, bf16[256,384]{1,0:T(8,128)(2,1)S(1)}, u32[]{:S(2)}, u32[]{:S(2)}) collective-permute-start(bf16[256,384]{1,0:T(8,128)(2,1)S(1)} %get-tuple-element.212), channel_id=1, source_target_pairs={{0,8},{4,12},{8,0},{12,4},{1,9},{5,13},{9,1},{13,5},{2,10},{6,14},... | collective-permute-start | bytes 589832 | tf_op jit(solution)/shard_map/ppermute | solution.py:38
  48.2 4.1 %collective-permute-done.11.refs_2_ = bf16[256,384]{1,0:T(8,128)(2,1)S(1)} collective-permute-done((bf16[256,384]{1,0:T(8,128)(2,1)S(1)}, bf16[256,384]{1,0:T(8,128)(2,1)S(1)}, u32[]{:S(2)}, u32[]{:S(2)}) %collective-permute-start.11) | collective-permute-done | bytes 196640 | tf_op jit(solution)/shard_map/ppermute | solution.py:38
  52.4 2.5 collective-permute-start.8
  54.9 3.7 %attend.2 = (bf16[256,128]{1,0:T(8,128)(2,1)S(1)}, bf16[256,128]{1,0:T(8,128)(2,1)S(1)}, bf16[256,128]{1,0:T(8,128)(2,1)S(1)}, bf16[256,128]{1,0:T(8,128)(2,1)S(1)}, f32[2,1024]{1,0:T(2,128)S(1)}) custom-call(bf16[256,384]{1,0:T(8,128)(2,1)S(1)} %get-tuple-element.220.refs_0_, bf16[256,384]{1,0:T(8,128)(2,1)S(1)} %collective-permute-done.10.refs_1_, ...), custom_call_target="tpu_custom_call" | custom-call | flops 2147483648 | bytes 1056768 | tf_op jit(solution)/shard_map/attend/pallas_call | solution.py:101
  58.6 10.7 %collective-permute-start.16 = (bf16[256,128]{1,0:T(8,128)(2,1)S(1)}, bf16[256,128]{1,0:T(8,128)(2,1)S(1)}, u32[]{:S(2)}, u32[]{:S(2)}) collective-permute-start(bf16[256,128]{1,0:T(8,128)(2,1)S(1)} %get-tuple-element.234), channel_id=1, source_target_pairs={{0,4},{4,0},{8,12},{12,8},{1,5},{5,1},{9,13},{13,9},{2,6},{6,2},{1... | collective-permute-start | bytes 196616 | tf_op jit(solution)/shard_map/ppermute | solution.py:38
  69.9 3.3 %collective-permute-start.17 = (bf16[256,128]{1,0:T(8,128)(2,1)S(1)}, bf16[256,128]{1,0:T(8,128)(2,1)S(1)}, u32[]{:S(2)}, u32[]{:S(2)}) collective-permute-start(bf16[256,128]{1,0:T(8,128)(2,1)S(1)} %get-tuple-element.235), channel_id=1, source_target_pairs={{0,8},{4,12},{8,0},{12,4},{1,9},{5,13},{9,1},{13,5},{2,10},{6,14},... | collective-permute-start | bytes 196616 | tf_op jit(solution)/shard_map/ppermute | solution.py:38
  74.5 3.7 %attend.3 = (bf16[256,128]{1,0:T(8,128)(2,1)S(1)}, bf16[256,128]{1,0:T(8,128)(2,1)S(1)}, bf16[256,128]{1,0:T(8,128)(2,1)S(1)}, bf16[256,128]{1,0:T(8,128)(2,1)S(1)}, f32[2,1024]{1,0:T(2,128)S(1)}) custom-call(bf16[256,384]{1,0:T(8,128)(2,1)S(1)} %get-tuple-element.225.refs_0_, bf16[256,384]{1,0:T(8,128)(2,1)S(1)} %collective-permute-done.6.refs_1_, ...), custom_call_target="tpu_custom_call" | custom-call | flops 2147483648 | bytes 1056768 | tf_op jit(solution)/shard_map/attend/pallas_call | solution.py:101
  80.4 1.6 collective-permute-start.22
  83.9 2.9 collective-permute-done.9
  86.8 1.8 collective-permute-start.14
  90.0 3.6 %collective-permute-done.14.refs_2_ = bf16[256,128]{1,0:T(8,128)(2,1)S(1)} collective-permute-done((bf16[256,128]{1,0:T(8,128)(2,1)S(1)}, bf16[256,128]{1,0:T(8,128)(2,1)S(1)}, u32[]{:S(2)}, u32[]{:S(2)}) %collective-permute-start.14) | collective-permute-done | bytes 65568 | tf_op jit(solution)/shard_map/ppermute | solution.py:38
  96.4 5.0 %feed.2 = (f32[256,1024]{1,0:T(8,128)S(1)}, bf16[256,1024]{1,0:T(8,128)(2,1)S(1)}, bf16[256,2048]{1,0:T(8,128)(2,1)S(1)}, bf16[256,2048]{1,0:T(8,128)(2,1)S(1)}, bf16[256,1024]{1,0:T(8,128)(2,1)S(1)}) custom-call(f32[256,1024]{1,0:T(8,128)S(1)} %get-tuple-element.250.start_ref, bf16[256,1024]{1,0:T(8,128)(2,1)S(1)} %get-tuple-element.251.mine_ref, ...), custom_call_target="tpu_custom_call" | custom-call | flops 214748368 | bytes 1472512 | tf_op jit(solution)/shard_map/feed/pallas_call | solution.py:101
  101.5 1.6 collective-permute-start.27
  103.0 7.7 %collective-permute-done.26.theirs_ref = bf16[256,1024]{1,0:T(8,128)(2,1)S(1)} collective-permute-done((bf16[256,1024]{1,0:T(8,128)(2,1)S(1)}, bf16[256,1024]{1,0:T(8,128)(2,1)S(1)}, u32[]{:S(2)}, u32[]{:S(2)}) %collective-permute-start.26) | collective-permute-done | bytes 524320 | tf_op jit(solution)/shard_map/ppermute | solution.py:38
  110.8 5.2 %feed.3 = (f32[256,1024]{1,0:T(8,128)S(1)}, bf16[256,1024]{1,0:T(8,128)(2,1)S(1)}, bf16[256,2048]{1,0:T(8,128)(2,1)S(1)}, bf16[256,2048]{1,0:T(8,128)(2,1)S(1)}, bf16[256,1024]{1,0:T(8,128)(2,1)S(1)}) custom-call(f32[256,1024]{1,0:T(8,128)S(1)} %get-tuple-element.257.start_ref, bf16[256,1024]{1,0:T(8,128)(2,1)S(1)} %get-tuple-element.258.mine_ref, ...), custom_call_target="tpu_custom_call" | custom-call | flops 214748368 | bytes 1472512 | tf_op jit(solution)/shard_map/feed/pallas_call | solution.py:101
  116.6 5.4 %collective-permute-done.27.theirs_ref = bf16[256,1024]{1,0:T(8,128)(2,1)S(1)} collective-permute-done((bf16[256,1024]{1,0:T(8,128)(2,1)S(1)}, bf16[256,1024]{1,0:T(8,128)(2,1)S(1)}, u32[]{:S(2)}, u32[]{:S(2)}) %collective-permute-start.27) | collective-permute-done | bytes 524320 | tf_op jit(solution)/shard_map/ppermute | solution.py:38
  122.0 6.9 %feed_back.2 = (bf16[1,256,1024]{2,1,0:T(8,128)(2,1)S(1)}, f32[256,1024]{1,0:T(8,128)S(1)}, bf16[256,1024]{1,0:T(8,128)(2,1)S(1)}, bf16[256,2048]{1,0:T(8,128)(2...) custom-call(s32[4]{0:T(128)S(1)} %pad_add_fusion.place, ...), custom_call_target="tpu_custom_call" | custom-call | flops 6442450 | bytes 47529 | tf_op jit(solution)/shard_map/feed_back/pallas_call | solution.py:101
  129.4 3.8 %collective-permute-done.28.theirs_ref = bf16[256,1024]{1,0:T(8,128)(2,1)S(1)} collective-permute-done((bf16[256,1024]{1,0:T(8,128)(2,1)S(1)}, bf16[256,1024]{1,0:T(8,128)(2,1)S(1)}, u32[]{:S(2)}, u32[]{:S(2)}) %collective-permute-start.28) | collective-permute-done | bytes 524320 | tf_op jit(solution)/shard_map/ppermute | solution.py:38
  133.2 6.9 %feed_back.3 = (bf16[2,256,1024]{2,1,0:T(8,128)(2,1)S(1)}, f32[256,1024]{1,0:T(8,128)S(1)}, bf16[256,1024]{1,0:T(8,128)(2,1)S(1)}, bf16[256,2048]{1,0:T(8,128)(2...) custom-call(s32[4]{0:T(128)S(1)} %pad_add_fusion.place, ...), custom_call_target="tpu_custom_call" | custom-call | flops 6442450 | bytes 50577 | tf_op jit(solution)/shard_map/feed_back/pallas_call | solution.py:101
  141.4 2.4 split.2
  143.9 2.6 grad_core.2
  149.7 4.1 %collective-permute-done.30.refs_8_ = bf16[1024,2048]{1,0:T(8,128)(2,1)S(1)} collective-permute-done((bf16[1024,2048]{1,0:T(8,128)(2,1)S(1)}, bf16[1024,2048]{1,0:T(8,128)(2,1)S(1)}, u32[]{:S(2)}, u32[]{:S(2)}) %collective-permute-start.30) | collective-permute-done | bytes 4194336 | tf_op jit(solution)/shard_map/ppermute | solution.py:38
  154.6 2.8 grad_shard.2
  157.4 3.5 %collective-permute-done.31.theirs_ref = bf16[256,1024]{1,0:T(8,128)(2,1)S(1)} collective-permute-done((bf16[256,1024]{1,0:T(8,128)(2,1)S(1)}, bf16[256,1024]{1,0:T(8,128)(2,1)S(1)}, u32[]{:S(2)}, u32[]{:S(2)}) %collective-permute-start.31) | collective-permute-done | bytes 524320 | tf_op jit(solution)/shard_map/ppermute | solution.py:38
  162.0 2.5 split.3
  164.5 2.5 collective-permute-start.33
  167.0 1.9 collective-permute-start.34
  168.9 7.0 %attend_back.2 = (bf16[256,384]{1,0:T(8,128)(2,1)S(1)}, bf16[256,384]{1,0:T(8,128)(2,1)S(1)}, bf16[256,384]{1,0:T(8,128)(2,1)S(1)}, bf16[256,384]{1,0:T(8,128)(2,1)S(1)}) custom-call(bf16[256,384]{1,0:T(8,128)(2,1)S(1)} %get-tuple-element.220.refs_0_, bf16[256,384]{1,0:T(8,128)(2,1)S(1)} %collective-permute-done.10.refs_1_, ...), custom_call_target="tpu_custom_call" | custom-call | flops 5368709120 | bytes 1843200 | tf_op jit(solution)/shard_map/attend_back/pallas_call | solution.py:101
  176.0 2.4 collective-permute-start.43
  178.5 1.9 collective-permute-start.44
  180.4 7.2 %attend_back.3 = (bf16[256,384]{1,0:T(8,128)(2,1)S(1)}, bf16[256,384]{1,0:T(8,128)(2,1)S(1)}, bf16[256,384]{1,0:T(8,128)(2,1)S(1)}, bf16[256,384]{1,0:T(8,128)(2,1)S(1)}) custom-call(bf16[256,384]{1,0:T(8,128)(2,1)S(1)} %get-tuple-element.225.refs_0_, bf16[256,384]{1,0:T(8,128)(2,1)S(1)} %collective-permute-done.6.refs_1_, ...), custom_call_target="tpu_custom_call" | custom-call | flops 5368709120 | bytes 1843200 | tf_op jit(solution)/shard_map/attend_back/pallas_call | solution.py:101
  187.7 4.9 %leave.2 = bf16[256,4,1024]{2,1,0:T(4,128)(2,1)} custom-call(s32[4]{0:T(128)S(1)} %pad_add_fusion.place, bf16[2,256,1024]{2,1,0:T(8,128)(2,1)S(1)} %get-tuple-element.301.own_ref, bf16[2,256,1024]{2,1,0:T(8,128)(2,1)S(1)} %collective-permute-done.38.other_ref), custom_call_target="tpu_custom_call" | custom-call | flops 31457280 | bytes 125829120 | tf_op jit(solution)/shard_map/leave/pallas_call | solution.py:80
  192.7 2.5 collective-permute-start.40
  195.1 1.9 collective-permute-start.41
  197.0 2.5 project_back.2
  200.0 8.7 %collective-permute-done.40.refs_2_ = bf16[256,384]{1,0:T(8,128)(2,1)S(1)} collective-permute-done((bf16[256,384]{1,0:T(8,128)(2,1)S(1)}, bf16[256,384]{1,0:T(8,128)(2,1)S(1)}, u32[]{:S(2)}, u32[]{:S(2)}) %collective-permute-start.40) | collective-permute-done | bytes 196640 | tf_op jit(solution)/shard_map/ppermute | solution.py:38
  208.8 1.7 project_back.3
  213.8 3.5 %grad_own.2 = (f32[128,2048]{1,0:T(8,128)S(1)}, bf16[128,2048]{1,0:T(8,128)(2,1)S(1)}, bf16[128,2048]{1,0:T(8,128)(2,1)S(1)}, bf16[128,2048]{1,0:T(8,128)(2,1)S(1)}) custom-call(s32[4]{0:T(128)S(1)} %pad_add_fusion.place, bf16[256,1024]{1,0:T(8,128)(2,1)S(1)} %copy-done.12, bf16[256,1024]{1,0:T(8,128)(2,1)S(1)} %copy-done.14, ...), custom_call_target="tpu_custom_call" | custom-call | flops 32212254720 | bytes 456130560 | tf_op jit(solution)/shard_map/grad_own/pallas_call | solution.py:101
  221.3 3.7 %collective-permute-start.46 = (bf16[128,2048]{1,0:T(8,128)(2,1)S(1)}, bf16[128,2048]{1,0:T(8,128)(2,1)S(1)}, u32[]{:S(2)}, u32[]{:S(2)}) collective-permute-start(bf16[128,2048]{1,0:T(8,128)(2,1)S(1)} %get-tuple-element.330), channel_id=1, source_target_pairs={{0,4},{4,0},{8,12},{12,8},{1,5},{5,1},{9,13},{13,9},{2,6},{6,2},{1... | collective-permute-start | bytes 1572872 | tf_op jit(solution)/shard_map/ppermute | solution.py:38
  225.4 2.0 collective-permute-start.48
  227.4 6.4 %collective-permute-done.51.theirs_ref = bf16[256,1024]{1,0:T(8,128)(2,1)S(1)} collective-permute-done((bf16[256,1024]{1,0:T(8,128)(2,1)S(1)}, bf16[256,1024]{1,0:T(8,128)(2,1)S(1)}, u32[]{:S(2)}, u32[]{:S(2)}) %collective-permute-start.51) | collective-permute-done | bytes 524320 | tf_op jit(solution)/shard_map/ppermute | solution.py:38
  233.8 3.7 %collective-permute-start.54 = (f32[24,1024]{1,0:T(8,128)S(1)}, f32[24,1024]{1,0:T(8,128)S(1)}, u32[]{:S(2)}, u32[]{:S(2)}) collective-permute-start(f32[24,1024]{1,0:T(8,128)S(1)} %tally.1), channel_id=1, source_target_pairs={{0,4},{4,0},{8,12},{12,8},{1,5},{5,1},{9,13},{13,9},{2,6},{6,2},{1... | collective-permute-start | bytes 294920 | tf_op jit(solution)/shard_map/ppermute | solution.py:38
  237.7 22.2 %collective-permute-done.54 = f32[24,1024]{1,0:T(8,128)S(1)} collective-permute-done((f32[24,1024]{1,0:T(8,128)S(1)}, f32[24,1024]{1,0:T(8,128)S(1)}, u32[]{:S(2)}, u32[]{:S(2)}) %collective-permute-start.54) | collective-permute-done | bytes 98336 | tf_op jit(solution)/shard_map/ppermute | solution.py:38
  259.9 3.0 collective-permute-start.55
  264.4 1.6 grad_own.3
  266.0 12.6 %collective-permute-start.59 = (bf16[128,1024]{1,0:T(8,128)(2,1)S(1)}, bf16[128,1024]{1,0:T(8,128)(2,1)S(1)}, u32[]{:S(2)}, u32[]{:S(2)}) collective-permute-start(bf16[128,1024]{1,0:T(8,128)(2,1)S(1)} %get-tuple-element.352), channel_id=1, source_target_pairs={{0,4},{4,0},{8,12},{12,8},{1,5},{5,1},{9,13},{13,9},{2,6},{6,2},{1... | collective-permute-start | bytes 786440 | tf_op jit(solution)/shard_map/ppermute | solution.py:38
  279.1 2.0 collective-permute-start.61
  283.6 3.8 %collective-permute-done.57 = f32[24,1024]{1,0:T(8,128)S(1)} collective-permute-done((f32[24,1024]{1,0:T(8,128)S(1)}, f32[24,1024]{1,0:T(8,128)S(1)}, u32[]{:S(2)}, u32[]{:S(2)}) %collective-permute-start.57) | collective-permute-done | bytes 98336 | tf_op jit(solution)/shard_map/ppermute | solution.py:38
  287.4 1.6 collective-permute-start.58
  289.0 5.0 %leave.3 = f32[256,4,1024]{2,1,0:T(4,128)} custom-call(s32[4]{0:T(128)S(1)} %pad_add_fusion.place, f32[2,256,1024]{2,1,0:T(8,128)S(1)} %last.3.own_ref, f32[2,256,1024]{2,1,0:T(8,128)S(1)} %collective-permute-done.53.other_ref), custom_call_target="tpu_custom_call" | custom-call | flops 31457280 | bytes 251658240 | tf_op jit(solution)/shard_map/leave/pallas_call | solution.py:80
  294.0 2.6 finish.1
  (159 shorter events, 42.5 us)
Async XLA Ops:
  2.5 21.5 %collective-permute-start.2 = (bf16[512,768]{1,0:T(8,128)(2,1)S(1)}, bf16[512,768]{1,0:T(8,128)(2,1)S(1)}, u32[]{:S(2)}, u32[]{:S(2)}) collective-permute-start(bf16[512,768]{1,0:T(8,128)(2,1)S(1)} %pack.1.a_ref.refs_4_), channel_id=1, source_target_pairs={{0,16},{16,0},{1,17},{17,1},{2,18},{18,2},{3,19},{19,3},{4,20},{20... | collective-permute-start | bytes 2359304 | tf_op jit(solution)/shard_map/ppermute | solution.py:38
  10.6 3.7 %collective-permute-start = (f32[8,128]{1,0:T(8,128)S(1)}, f32[8,128]{1,0:T(8,128)S(1)}, u32[]{:S(2)}, u32[]{:S(2)}) collective-permute-start(f32[8,128]{1,0:T(8,128)S(1)} %broadcast_in_dim.10), channel_id=1, source_target_pairs={{0,4},{4,0},{8,12},{12,8},{1,5},{5,1},{9,13},{13,9},{2,6},{6,2},{1... | collective-permute-start | bytes 12296 | tf_op jit(solution)/shard_map/ppermute | solution.py:38
  12.2 14.2 %collective-permute-start.3 = (bf16[512,768]{1,0:T(8,128)(2,1)S(1)}, bf16[512,768]{1,0:T(8,128)(2,1)S(1)}, u32[]{:S(2)}, u32[]{:S(2)}) collective-permute-start(bf16[512,768]{1,0:T(8,128)(2,1)S(1)} %pack.1.a_ref.refs_4_), channel_id=1, source_target_pairs={{0,1},{1,0},{2,3},{3,2},{4,5},{5,4},{6,7},{7,6},{8,9},{9,8},{10,11... | collective-permute-start | bytes 2359304 | tf_op jit(solution)/shard_map/ppermute | solution.py:38
  14.3 6.8 %collective-permute-start.1 = (f32[8,128]{1,0:T(8,128)S(1)}, f32[8,128]{1,0:T(8,128)S(1)}, u32[]{:S(2)}, u32[]{:S(2)}) collective-permute-start(f32[8,128]{1,0:T(8,128)S(1)} %add.36), channel_id=1, source_target_pairs={{0,8},{4,12},{8,0},{12,4},{1,9},{5,13},{9,1},{13,5},{2,10},{6,14},... | collective-permute-start | bytes 12296 | tf_op jit(solution)/shard_map/ppermute | solution.py:38
  24.1 2.4 collective-permute-start.4
  24.2 8.7 %collective-permute-start.19 = (bf16[512,256]{1,0:T(8,128)(2,1)S(1)}, bf16[512,256]{1,0:T(8,128)(2,1)S(1)}, u32[]{:S(2)}, u32[]{:S(2)}) collective-permute-start(bf16[512,256]{1,0:T(8,128)(2,1)S(1)} %get-tuple-element.242.refs_4_.a_ref), channel_id=1, source_target_pairs={{0,16},{16,0},{1,17},{17,1},{2,18},{18,2},{3,19},{19,3},{4,20},{20... | collective-permute-start | bytes 786440 | tf_op jit(solution)/shard_map/ppermute | solution.py:38
  24.9 1.6 collective-permute-start.5
  32.9 47.4 %collective-permute-start.23 = (bf16[512,2048]{1,0:T(8,128)(2,1)S(1)}, bf16[512,2048]{1,0:T(8,128)(2,1)S(1)}, u32[]{:S(2)}, u32[]{:S(2)}) collective-permute-start(bf16[512,2048]{1,0:T(8,128)(2,1)S(1)} %get-tuple-element.252.a_ref), channel_id=1, source_target_pairs={{0,16},{16,0},{1,17},{17,1},{2,18},{18,2},{3,19},{19,3},{4,20},{20... | collective-permute-start | bytes 6291464 | tf_op jit(solution)/shard_map/ppermute | solution.py:38
  33.6 11.2 %collective-permute-start.10 = (bf16[256,384]{1,0:T(8,128)(2,1)S(1)}, bf16[256,384]{1,0:T(8,128)(2,1)S(1)}, u32[]{:S(2)}, u32[]{:S(2)}) collective-permute-start(bf16[256,384]{1,0:T(8,128)(2,1)S(1)} %get-tuple-element.217), channel_id=1, source_target_pairs={{0,4},{4,0},{8,12},{12,8},{1,5},{5,1},{9,13},{13,9},{2,6},{6,2},{1... | collective-permute-start | bytes 589832 | tf_op jit(solution)/shard_map/ppermute | solution.py:38
  35.1 17.2 %collective-permute-start.11 = (bf16[256,384]{1,0:T(8,128)(2,1)S(1)}, bf16[256,384]{1,0:T(8,128)(2,1)S(1)}, u32[]{:S(2)}, u32[]{:S(2)}) collective-permute-start(bf16[256,384]{1,0:T(8,128)(2,1)S(1)} %get-tuple-element.218), channel_id=1, source_target_pairs={{0,8},{4,12},{8,0},{12,4},{1,9},{5,13},{9,1},{13,5},{2,10},{6,14},... | collective-permute-start | bytes 589832 | tf_op jit(solution)/shard_map/ppermute | solution.py:38
  37.7 17.2 %collective-permute-start.12 = (bf16[256,384]{1,0:T(8,128)(2,1)S(1)}, bf16[256,384]{1,0:T(8,128)(2,1)S(1)}, u32[]{:S(2)}, u32[]{:S(2)}) collective-permute-start(bf16[256,384]{1,0:T(8,128)(2,1)S(1)} %get-tuple-element.219), channel_id=1, source_target_pairs={{0,12},{4,8},{8,4},{12,0},{1,13},{5,9},{9,5},{13,1},{2,14},{6,10},... | collective-permute-start | bytes 589832 | tf_op jit(solution)/shard_map/ppermute | solution.py:38
  44.0 25.4 %collective-permute-start.6 = (bf16[256,384]{1,0:T(8,128)(2,1)S(1)}, bf16[256,384]{1,0:T(8,128)(2,1)S(1)}, u32[]{:S(2)}, u32[]{:S(2)}) collective-permute-start(bf16[256,384]{1,0:T(8,128)(2,1)S(1)} %get-tuple-element.211), channel_id=1, source_target_pairs={{0,4},{4,0},{8,12},{12,8},{1,5},{5,1},{9,13},{13,9},{2,6},{6,2},{1... | collective-permute-start | bytes 589832 | tf_op jit(solution)/shard_map/ppermute | solution.py:38
  44.7 24.6 %collective-permute-start.7 = (bf16[256,384]{1,0:T(8,128)(2,1)S(1)}, bf16[256,384]{1,0:T(8,128)(2,1)S(1)}, u32[]{:S(2)}, u32[]{:S(2)}) collective-permute-start(bf16[256,384]{1,0:T(8,128)(2,1)S(1)} %get-tuple-element.212), channel_id=1, source_target_pairs={{0,8},{4,12},{8,0},{12,4},{1,9},{5,13},{9,1},{13,5},{2,10},{6,14},... | collective-permute-start | bytes 589832 | tf_op jit(solution)/shard_map/ppermute | solution.py:38
  52.4 17.5 %collective-permute-start.8 = (bf16[256,384]{1,0:T(8,128)(2,1)S(1)}, bf16[256,384]{1,0:T(8,128)(2,1)S(1)}, u32[]{:S(2)}, u32[]{:S(2)}) collective-permute-start(bf16[256,384]{1,0:T(8,128)(2,1)S(1)} %get-tuple-element.213), channel_id=1, source_target_pairs={{0,12},{4,8},{8,4},{12,0},{1,13},{5,9},{9,5},{13,1},{2,14},{6,10},... | collective-permute-start | bytes 589832 | tf_op jit(solution)/shard_map/ppermute | solution.py:38
  58.6 14.5 %collective-permute-start.16 = (bf16[256,128]{1,0:T(8,128)(2,1)S(1)}, bf16[256,128]{1,0:T(8,128)(2,1)S(1)}, u32[]{:S(2)}, u32[]{:S(2)}) collective-permute-start(bf16[256,128]{1,0:T(8,128)(2,1)S(1)} %get-tuple-element.234), channel_id=1, source_target_pairs={{0,4},{4,0},{8,12},{12,8},{1,5},{5,1},{9,13},{13,9},{2,6},{6,2},{1... | collective-permute-start | bytes 196616 | tf_op jit(solution)/shard_map/ppermute | solution.py:38
  69.4 9.9 %collective-permute-start.20 = (bf16[512,256]{1,0:T(8,128)(2,1)S(1)}, bf16[512,256]{1,0:T(8,128)(2,1)S(1)}, u32[]{:S(2)}, u32[]{:S(2)}) collective-permute-start(bf16[512,256]{1,0:T(8,128)(2,1)S(1)} %get-tuple-element.242.refs_4_.a_ref), channel_id=1, source_target_pairs={{0,1},{1,0},{2,3},{3,2},{4,5},{5,4},{6,7},{7,6},{8,9},{9,8},{10,11... | collective-permute-start | bytes 786440 | tf_op jit(solution)/shard_map/ppermute | solution.py:38
  69.4 9.9 %collective-permute-start.21 = (bf16[512,256]{1,0:T(8,128)(2,1)S(1)}, bf16[512,256]{1,0:T(8,128)(2,1)S(1)}, u32[]{:S(2)}, u32[]{:S(2)}) collective-permute-start(bf16[512,256]{1,0:T(8,128)(2,1)S(1)} %collective-permute-done.19.refs_5_.b_ref), channel_id=1, source_target_pairs={{0,1},{1,0},{2,3},{3,2},{4,5},{5,4},{6,7},{7,6},{8,9},{9,8},{10,11... | collective-permute-start | bytes 786440 | tf_op jit(solution)/shard_map/ppermute | solution.py:38
  69.9 8.4 %collective-permute-start.17 = (bf16[256,128]{1,0:T(8,128)(2,1)S(1)}, bf16[256,128]{1,0:T(8,128)(2,1)S(1)}, u32[]{:S(2)}, u32[]{:S(2)}) collective-permute-start(bf16[256,128]{1,0:T(8,128)(2,1)S(1)} %get-tuple-element.235), channel_id=1, source_target_pairs={{0,8},{4,12},{8,0},{12,4},{1,9},{5,13},{9,1},{13,5},{2,10},{6,14},... | collective-permute-start | bytes 196616 | tf_op jit(solution)/shard_map/ppermute | solution.py:38
  73.2 6.1 %collective-permute-start.18 = (bf16[256,128]{1,0:T(8,128)(2,1)S(1)}, bf16[256,128]{1,0:T(8,128)(2,1)S(1)}, u32[]{:S(2)}, u32[]{:S(2)}) collective-permute-start(bf16[256,128]{1,0:T(8,128)(2,1)S(1)} %get-tuple-element.236), channel_id=1, source_target_pairs={{0,12},{4,8},{8,4},{12,0},{1,13},{5,9},{9,5},{13,1},{2,14},{6,10},... | collective-permute-start | bytes 196616 | tf_op jit(solution)/shard_map/ppermute | solution.py:38
  78.3 18.1 %collective-permute-start.24 = (bf16[512,2048]{1,0:T(8,128)(2,1)S(1)}, bf16[512,2048]{1,0:T(8,128)(2,1)S(1)}, u32[]{:S(2)}, u32[]{:S(2)}) collective-permute-start(bf16[512,2048]{1,0:T(8,128)(2,1)S(1)} %get-tuple-element.252.a_ref), channel_id=1, source_target_pairs={{0,1},{1,0},{2,3},{3,2},{4,5},{5,4},{6,7},{7,6},{8,9},{9,8},{10,11... | collective-permute-start | bytes 6291464 | tf_op jit(solution)/shard_map/ppermute | solution.py:38
  80.3 16.1 %collective-permute-start.25 = (bf16[512,2048]{1,0:T(8,128)(2,1)S(1)}, bf16[512,2048]{1,0:T(8,128)(2,1)S(1)}, u32[]{:S(2)}, u32[]{:S(2)}) collective-permute-start(bf16[512,2048]{1,0:T(8,128)(2,1)S(1)} %collective-permute-done.23.b_ref), channel_id=1, source_target_pairs={{0,1},{1,0},{2,3},{3,2},{4,5},{5,4},{6,7},{7,6},{8,9},{9,8},{10,11... | collective-permute-start | bytes 6291464 | tf_op jit(solution)/shard_map/ppermute | solution.py:38
  80.4 16.0 %collective-permute-start.22 = (bf16[256,1024]{1,0:T(8,128)(2,1)S(1)}, bf16[256,1024]{1,0:T(8,128)(2,1)S(1)}, u32[]{:S(2)}, u32[]{:S(2)}) collective-permute-start(bf16[256,1024]{1,0:T(8,128)(2,1)S(1)} %get-tuple-element.251.mine_ref), channel_id=1, source_target_pairs={{0,2},{1,3},{2,0},{3,1},{4,6},{5,7},{6,4},{7,5},{8,10},{9,11},{10,... | collective-permute-start | bytes 1572872 | tf_op jit(solution)/shard_map/ppermute | solution.py:38
  81.9 6.7 %collective-permute-start.13 = (bf16[256,128]{1,0:T(8,128)(2,1)S(1)}, bf16[256,128]{1,0:T(8,128)(2,1)S(1)}, u32[]{:S(2)}, u32[]{:S(2)}) collective-permute-start(bf16[256,128]{1,0:T(8,128)(2,1)S(1)} %get-tuple-element.230), channel_id=1, source_target_pairs={{0,4},{4,0},{8,12},{12,8},{1,5},{5,1},{9,13},{13,9},{2,6},{6,2},{1... | collective-permute-start | bytes 196616 | tf_op jit(solution)/shard_map/ppermute | solution.py:38
  83.2 3.6 %collective-permute-start.9 = (f32[8,128]{1,0:T(8,128)S(1)}, f32[8,128]{1,0:T(8,128)S(1)}, u32[]{:S(2)}, u32[]{:S(2)}) collective-permute-start(f32[8,128]{1,0:T(8,128)S(1)} %add.37), channel_id=1, source_target_pairs={{0,16},{16,0},{1,17},{17,1},{2,18},{18,2},{3,19},{19,3},{4,20},{20... | collective-permute-start | bytes 12296 | tf_op jit(solution)/shard_map/ppermute | solution.py:38
  86.8 6.8 %collective-permute-start.14 = (bf16[256,128]{1,0:T(8,128)(2,1)S(1)}, bf16[256,128]{1,0:T(8,128)(2,1)S(1)}, u32[]{:S(2)}, u32[]{:S(2)}) collective-permute-start(bf16[256,128]{1,0:T(8,128)(2,1)S(1)} %get-tuple-element.231), channel_id=1, source_target_pairs={{0,8},{4,12},{8,0},{12,4},{1,9},{5,13},{9,1},{13,5},{2,10},{6,14},... | collective-permute-start | bytes 196616 | tf_op jit(solution)/shard_map/ppermute | solution.py:38
  88.6 6.2 %collective-permute-start.15 = (bf16[256,128]{1,0:T(8,128)(2,1)S(1)}, bf16[256,128]{1,0:T(8,128)(2,1)S(1)}, u32[]{:S(2)}, u32[]{:S(2)}) collective-permute-start(bf16[256,128]{1,0:T(8,128)(2,1)S(1)} %get-tuple-element.232), channel_id=1, source_target_pairs={{0,12},{4,8},{8,4},{12,0},{1,13},{5,9},{9,5},{13,1},{2,14},{6,10},... | collective-permute-start | bytes 196616 | tf_op jit(solution)/shard_map/ppermute | solution.py:38
  90.0 43.3 %copy-start.6 = (f32[8,128]{1,0:T(8,128)}, f32[8,128]{1,0:T(8,128)S(1)}, u32[]{:S(2)}) copy-start(f32[8,128]{1,0:T(8,128)S(1)} %add.38.count_ref) | copy-start | bytes 12292
  95.8 14.9 %collective-permute-start.26 = (bf16[256,1024]{1,0:T(8,128)(2,1)S(1)}, bf16[256,1024]{1,0:T(8,128)(2,1)S(1)}, u32[]{:S(2)}, u32[]{:S(2)}) collective-permute-start(bf16[256,1024]{1,0:T(8,128)(2,1)S(1)} %get-tuple-element.258.mine_ref), channel_id=1, source_target_pairs={{0,2},{1,3},{2,0},{3,1},{4,6},{5,7},{6,4},{7,5},{8,10},{9,11},{10,... | collective-permute-start | bytes 1572872 | tf_op jit(solution)/shard_map/ppermute | solution.py:38
  101.4 53.1 %copy-start.11 = (bf16[256,1024]{1,0:T(8,128)(2,1)}, bf16[256,1024]{1,0:T(8,128)(2,1)S(1)}, u32[]{:S(2)}) copy-start(bf16[256,1024]{1,0:T(8,128)(2,1)S(1)} %get-tuple-element.328.refs_0_) | copy-start | bytes 1572868
  101.5 20.5 %collective-permute-start.27 = (bf16[256,1024]{1,0:T(8,128)(2,1)S(1)}, bf16[256,1024]{1,0:T(8,128)(2,1)S(1)}, u32[]{:S(2)}, u32[]{:S(2)}) collective-permute-start(bf16[256,1024]{1,0:T(8,128)(2,1)S(1)} %get-tuple-element.261.mine_ref), channel_id=1, source_target_pairs={{0,2},{1,3},{2,0},{3,1},{4,6},{5,7},{6,4},{7,5},{8,10},{9,11},{10,... | collective-permute-start | bytes 1572872 | tf_op jit(solution)/shard_map/ppermute | solution.py:38
  116.0 17.2 %collective-permute-start.28 = (bf16[256,1024]{1,0:T(8,128)(2,1)S(1)}, bf16[256,1024]{1,0:T(8,128)(2,1)S(1)}, u32[]{:S(2)}, u32[]{:S(2)}) collective-permute-start(bf16[256,1024]{1,0:T(8,128)(2,1)S(1)} %get-tuple-element.268.mine_ref), channel_id=1, source_target_pairs={{0,2},{1,3},{2,0},{3,1},{4,6},{5,7},{6,4},{7,5},{8,10},{9,11},{10,... | collective-permute-start | bytes 1572872 | tf_op jit(solution)/shard_map/ppermute | solution.py:38
  128.9 12.5 %collective-permute-start.29 = (bf16[256,1024]{1,0:T(8,128)(2,1)S(1)}, bf16[256,1024]{1,0:T(8,128)(2,1)S(1)}, u32[]{:S(2)}, u32[]{:S(2)}) collective-permute-start(bf16[256,1024]{1,0:T(8,128)(2,1)S(1)} %get-tuple-element.275.mine_ref), channel_id=1, source_target_pairs={{0,2},{1,3},{2,0},{3,1},{4,6},{5,7},{6,4},{7,5},{8,10},{9,11},{10,... | collective-permute-start | bytes 1572872 | tf_op jit(solution)/shard_map/ppermute | solution.py:38
  146.5 7.2 %collective-permute-start.30 = (bf16[1024,2048]{1,0:T(8,128)(2,1)S(1)}, bf16[1024,2048]{1,0:T(8,128)(2,1)S(1)}, u32[]{:S(2)}, u32[]{:S(2)}) collective-permute-start(bf16[1024,2048]{1,0:T(8,128)(2,1)S(1)} %grad_core.2), channel_id=1, source_target_pairs={{0,1},{1,0},{2,3},{3,2},{4,5},{5,4},{6,7},{7,6},{8,9},{9,8},{10,11... | collective-permute-start | bytes 12582920 | tf_op jit(solution)/shard_map/ppermute | solution.py:38
  146.6 14.3 %collective-permute-start.31 = (bf16[256,1024]{1,0:T(8,128)(2,1)S(1)}, bf16[256,1024]{1,0:T(8,128)(2,1)S(1)}, u32[]{:S(2)}, u32[]{:S(2)}) collective-permute-start(bf16[256,1024]{1,0:T(8,128)(2,1)S(1)} %get-tuple-element.286.mine_ref), channel_id=1, source_target_pairs={{0,2},{1,3},{2,0},{3,1},{4,6},{5,7},{6,4},{7,5},{8,10},{9,11},{10,... | collective-permute-start | bytes 1572872 | tf_op jit(solution)/shard_map/ppermute | solution.py:38
  147.2 40.5 %collective-permute-start.38 = (bf16[2,256,1024]{2,1,0:T(8,128)(2,1)S(1)}, bf16[2,256,1024]{2,1,0:T(8,128)(2,1)S(1)}, u32[]{:S(2)}, u32[]{:S(2)}) collective-permute-start(bf16[2,256,1024]{2,1,0:T(8,128)(2,1)S(1)} %get-tuple-element.301.own_ref), channel_id=1, source_target_pairs={{0,1},{1,0},{2,3},{3,2},{4,5},{5,4},{6,7},{7,6},{8,9},{9,8},{10,11... | collective-permute-start | bytes 3145736 | tf_op jit(solution)/shard_map/ppermute | solution.py:38
  147.3 17.1 %collective-permute-start.35 = (bf16[256,128]{1,0:T(8,128)(2,1)S(1)}, bf16[256,128]{1,0:T(8,128)(2,1)S(1)}, u32[]{:S(2)}, u32[]{:S(2)}) collective-permute-start(bf16[256,128]{1,0:T(8,128)(2,1)S(1)} %get-tuple-element.292), channel_id=1, source_target_pairs={{0,4},{4,0},{8,12},{12,8},{1,5},{5,1},{9,13},{13,9},{2,6},{6,2},{1... | collective-permute-start | bytes 196616 | tf_op jit(solution)/shard_map/ppermute | solution.py:38
  148.2 16.3 %collective-permute-start.36 = (bf16[256,128]{1,0:T(8,128)(2,1)S(1)}, bf16[256,128]{1,0:T(8,128)(2,1)S(1)}, u32[]{:S(2)}, u32[]{:S(2)}) collective-permute-start(bf16[256,128]{1,0:T(8,128)(2,1)S(1)} %get-tuple-element.293), channel_id=1, source_target_pairs={{0,8},{4,12},{8,0},{12,4},{1,9},{5,13},{9,1},{13,5},{2,10},{6,14},... | collective-permute-start | bytes 196616 | tf_op jit(solution)/shard_map/ppermute | solution.py:38
  153.7 13.3 %collective-permute-start.37 = (bf16[256,128]{1,0:T(8,128)(2,1)S(1)}, bf16[256,128]{1,0:T(8,128)(2,1)S(1)}, u32[]{:S(2)}, u32[]{:S(2)}) collective-permute-start(bf16[256,128]{1,0:T(8,128)(2,1)S(1)} %get-tuple-element.294), channel_id=1, source_target_pairs={{0,12},{4,8},{8,4},{12,0},{1,13},{5,9},{9,5},{13,1},{2,14},{6,10},... | collective-permute-start | bytes 196616 | tf_op jit(solution)/shard_map/ppermute | solution.py:38
  160.9 51.8 %collective-permute-start.45 = (bf16[512,2048]{1,0:T(8,128)(2,1)}, bf16[512,2048]{1,0:T(8,128)(2,1)}, u32[]{:S(2)}, u32[]{:S(2)}) collective-permute-start(bf16[512,2048]{1,0:T(8,128)(2,1)} %grad_shard.2), channel_id=1, source_target_pairs={{0,16},{16,0},{1,17},{17,1},{2,18},{18,2},{3,19},{19,3},{4,20},{20... | collective-permute-start | bytes 6291464 | tf_op jit(solution)/shard_map/ppermute | solution.py:38
  164.4 11.5 %collective-permute-start.32 = (bf16[256,128]{1,0:T(8,128)(2,1)S(1)}, bf16[256,128]{1,0:T(8,128)(2,1)S(1)}, u32[]{:S(2)}, u32[]{:S(2)}) collective-permute-start(bf16[256,128]{1,0:T(8,128)(2,1)S(1)} %get-tuple-element.288), channel_id=1, source_target_pairs={{0,4},{4,0},{8,12},{12,8},{1,5},{5,1},{9,13},{13,9},{2,6},{6,2},{1... | collective-permute-start | bytes 196616 | tf_op jit(solution)/shard_map/ppermute | solution.py:38
  164.5 11.5 %collective-permute-start.33 = (bf16[256,128]{1,0:T(8,128)(2,1)S(1)}, bf16[256,128]{1,0:T(8,128)(2,1)S(1)}, u32[]{:S(2)}, u32[]{:S(2)}) collective-permute-start(bf16[256,128]{1,0:T(8,128)(2,1)S(1)} %get-tuple-element.289), channel_id=1, source_target_pairs={{0,8},{4,12},{8,0},{12,4},{1,9},{5,13},{9,1},{13,5},{2,10},{6,14},... | collective-permute-start | bytes 196616 | tf_op jit(solution)/shard_map/ppermute | solution.py:38
  167.0 11.5 %collective-permute-start.34 = (bf16[256,128]{1,0:T(8,128)(2,1)S(1)}, bf16[256,128]{1,0:T(8,128)(2,1)S(1)}, u32[]{:S(2)}, u32[]{:S(2)}) collective-permute-start(bf16[256,128]{1,0:T(8,128)(2,1)S(1)} %get-tuple-element.290), channel_id=1, source_target_pairs={{0,12},{4,8},{8,4},{12,0},{1,13},{5,9},{9,5},{13,1},{2,14},{6,10},... | collective-permute-start | bytes 196616 | tf_op jit(solution)/shard_map/ppermute | solution.py:38
  175.9 16.7 %collective-permute-start.42 = (bf16[256,384]{1,0:T(8,128)(2,1)S(1)}, bf16[256,384]{1,0:T(8,128)(2,1)S(1)}, u32[]{:S(2)}, u32[]{:S(2)}) collective-permute-start(bf16[256,384]{1,0:T(8,128)(2,1)S(1)} %get-tuple-element.306), channel_id=1, source_target_pairs={{0,4},{4,0},{8,12},{12,8},{1,5},{5,1},{9,13},{13,9},{2,6},{6,2},{1... | collective-permute-start | bytes 589832 | tf_op jit(solution)/shard_map/ppermute | solution.py:38
  176.0 19.1 %collective-permute-start.43 = (bf16[256,384]{1,0:T(8,128)(2,1)S(1)}, bf16[256,384]{1,0:T(8,128)(2,1)S(1)}, u32[]{:S(2)}, u32[]{:S(2)}) collective-permute-start(bf16[256,384]{1,0:T(8,128)(2,1)S(1)} %get-tuple-element.307), channel_id=1, source_target_pairs={{0,8},{4,12},{8,0},{12,4},{1,9},{5,13},{9,1},{13,5},{2,10},{6,14},... | collective-permute-start | bytes 589832 | tf_op jit(solution)/shard_map/ppermute | solution.py:38
  178.5 18.5 %collective-permute-start.44 = (bf16[256,384]{1,0:T(8,128)(2,1)S(1)}, bf16[256,384]{1,0:T(8,128)(2,1)S(1)}, u32[]{:S(2)}, u32[]{:S(2)}) collective-permute-start(bf16[256,384]{1,0:T(8,128)(2,1)S(1)} %get-tuple-element.308), channel_id=1, source_target_pairs={{0,12},{4,8},{8,4},{12,0},{1,13},{5,9},{9,5},{13,1},{2,14},{6,10},... | collective-permute-start | bytes 589832 | tf_op jit(solution)/shard_map/ppermute | solution.py:38
  187.6 12.4 %collective-permute-start.39 = (bf16[256,384]{1,0:T(8,128)(2,1)S(1)}, bf16[256,384]{1,0:T(8,128)(2,1)S(1)}, u32[]{:S(2)}, u32[]{:S(2)}) collective-permute-start(bf16[256,384]{1,0:T(8,128)(2,1)S(1)} %get-tuple-element.303), channel_id=1, source_target_pairs={{0,4},{4,0},{8,12},{12,8},{1,5},{5,1},{9,13},{13,9},{2,6},{6,2},{1... | collective-permute-start | bytes 589832 | tf_op jit(solution)/shard_map/ppermute | solution.py:38
  192.7 16.1 %collective-permute-start.40 = (bf16[256,384]{1,0:T(8,128)(2,1)S(1)}, bf16[256,384]{1,0:T(8,128)(2,1)S(1)}, u32[]{:S(2)}, u32[]{:S(2)}) collective-permute-start(bf16[256,384]{1,0:T(8,128)(2,1)S(1)} %get-tuple-element.304), channel_id=1, source_target_pairs={{0,8},{4,12},{8,0},{12,4},{1,9},{5,13},{9,1},{13,5},{2,10},{6,14},... | collective-permute-start | bytes 589832 | tf_op jit(solution)/shard_map/ppermute | solution.py:38
  195.1 13.6 %collective-permute-start.41 = (bf16[256,384]{1,0:T(8,128)(2,1)S(1)}, bf16[256,384]{1,0:T(8,128)(2,1)S(1)}, u32[]{:S(2)}, u32[]{:S(2)}) collective-permute-start(bf16[256,384]{1,0:T(8,128)(2,1)S(1)} %get-tuple-element.305), channel_id=1, source_target_pairs={{0,12},{4,8},{8,4},{12,0},{1,13},{5,9},{9,5},{13,1},{2,14},{6,10},... | collective-permute-start | bytes 589832 | tf_op jit(solution)/shard_map/ppermute | solution.py:38
  199.5 17.9 %collective-permute-start.49 = (bf16[256,1024]{1,0:T(8,128)(2,1)}, bf16[256,1024]{1,0:T(8,128)(2,1)}, u32[]{:S(2)}, u32[]{:S(2)}) collective-permute-start(bf16[256,1024]{1,0:T(8,128)(2,1)} %get-tuple-element.335.mine_ref), channel_id=1, source_target_pairs={{0,2},{1,3},{2,0},{3,1},{4,6},{5,7},{6,4},{7,5},{8,10},{9,11},{10,... | collective-permute-start | bytes 1572872 | tf_op jit(solution)/shard_map/ppermute | solution.py:38
  212.6 6.2 %collective-permute-start.50 = (bf16[1024,1024]{1,0:T(8,128)(2,1)S(1)}, bf16[1024,1024]{1,0:T(8,128)(2,1)S(1)}, u32[]{:S(2)}, u32[]{:S(2)}) collective-permute-start(bf16[1024,1024]{1,0:T(8,128)(2,1)S(1)} %grad_core.3), channel_id=1, source_target_pairs={{0,1},{1,0},{2,3},{3,2},{4,5},{5,4},{6,7},{7,6},{8,9},{9,8},{10,11... | collective-permute-start | bytes 6291464 | tf_op jit(solution)/shard_map/ppermute | solution.py:38
  219.8 44.6 %collective-permute-start.52 = (bf16[512,1024]{1,0:T(8,128)(2,1)S(1)}, bf16[512,1024]{1,0:T(8,128)(2,1)S(1)}, u32[]{:S(2)}, u32[]{:S(2)}) collective-permute-start(bf16[512,1024]{1,0:T(8,128)(2,1)S(1)} %grad_shard.3), channel_id=1, source_target_pairs={{0,16},{16,0},{1,17},{17,1},{2,18},{18,2},{3,19},{19,3},{4,20},{20... | collective-permute-start | bytes 3145736 | tf_op jit(solution)/shard_map/ppermute | solution.py:38
  220.8 12.9 %collective-permute-start.51 = (bf16[256,1024]{1,0:T(8,128)(2,1)S(1)}, bf16[256,1024]{1,0:T(8,128)(2,1)S(1)}, u32[]{:S(2)}, u32[]{:S(2)}) collective-permute-start(bf16[256,1024]{1,0:T(8,128)(2,1)S(1)} %get-tuple-element.339.mine_ref), channel_id=1, source_target_pairs={{0,2},{1,3},{2,0},{3,1},{4,6},{5,7},{6,4},{7,5},{8,10},{9,11},{10,... | collective-permute-start | bytes 1572872 | tf_op jit(solution)/shard_map/ppermute | solution.py:38
  221.3 38.5 %collective-permute-start.46 = (bf16[128,2048]{1,0:T(8,128)(2,1)S(1)}, bf16[128,2048]{1,0:T(8,128)(2,1)S(1)}, u32[]{:S(2)}, u32[]{:S(2)}) collective-permute-start(bf16[128,2048]{1,0:T(8,128)(2,1)S(1)} %get-tuple-element.330), channel_id=1, source_target_pairs={{0,4},{4,0},{8,12},{12,8},{1,5},{5,1},{9,13},{13,9},{2,6},{6,2},{1... | collective-permute-start | bytes 1572872 | tf_op jit(solution)/shard_map/ppermute | solution.py:38
  225.0 38.2 %collective-permute-start.47 = (bf16[128,2048]{1,0:T(8,128)(2,1)S(1)}, bf16[128,2048]{1,0:T(8,128)(2,1)S(1)}, u32[]{:S(2)}, u32[]{:S(2)}) collective-permute-start(bf16[128,2048]{1,0:T(8,128)(2,1)S(1)} %get-tuple-element.331), channel_id=1, source_target_pairs={{0,8},{4,12},{8,0},{12,4},{1,9},{5,13},{9,1},{13,5},{2,10},{6,14},... | collective-permute-start | bytes 1572872 | tf_op jit(solution)/shard_map/ppermute | solution.py:38
  225.4 37.8 %collective-permute-start.48 = (bf16[128,2048]{1,0:T(8,128)(2,1)S(1)}, bf16[128,2048]{1,0:T(8,128)(2,1)S(1)}, u32[]{:S(2)}, u32[]{:S(2)}) collective-permute-start(bf16[128,2048]{1,0:T(8,128)(2,1)S(1)} %get-tuple-element.332), channel_id=1, source_target_pairs={{0,12},{4,8},{8,4},{12,0},{1,13},{5,9},{9,5},{13,1},{2,14},{6,10},... | collective-permute-start | bytes 1572872 | tf_op jit(solution)/shard_map/ppermute | solution.py:38
  233.8 26.0 %collective-permute-start.54 = (f32[24,1024]{1,0:T(8,128)S(1)}, f32[24,1024]{1,0:T(8,128)S(1)}, u32[]{:S(2)}, u32[]{:S(2)}) collective-permute-start(f32[24,1024]{1,0:T(8,128)S(1)} %tally.1), channel_id=1, source_target_pairs={{0,4},{4,0},{8,12},{12,8},{1,5},{5,1},{9,13},{13,9},{2,6},{6,2},{1... | collective-permute-start | bytes 294920 | tf_op jit(solution)/shard_map/ppermute | solution.py:38
  259.8 29.2 %collective-permute-start.53 = (f32[2,256,1024]{2,1,0:T(8,128)S(1)}, f32[2,256,1024]{2,1,0:T(8,128)S(1)}, u32[]{:S(2)}, u32[]{:S(2)}) collective-permute-start(f32[2,256,1024]{2,1,0:T(8,128)S(1)} %last.3.own_ref), channel_id=1, source_target_pairs={{0,1},{1,0},{2,3},{3,2},{4,5},{5,4},{6,7},{7,6},{8,9},{9,8},{10,11... | collective-permute-start | bytes 6291464 | tf_op jit(solution)/shard_map/ppermute | solution.py:38
  259.9 21.2 %collective-permute-start.55 = (f32[24,1024]{1,0:T(8,128)S(1)}, f32[24,1024]{1,0:T(8,128)S(1)}, u32[]{:S(2)}, u32[]{:S(2)}) collective-permute-start(f32[24,1024]{1,0:T(8,128)S(1)} %add.39), channel_id=1, source_target_pairs={{0,8},{4,12},{8,0},{12,4},{1,9},{5,13},{9,1},{13,5},{2,10},{6,14},... | collective-permute-start | bytes 294920 | tf_op jit(solution)/shard_map/ppermute | solution.py:38
  266.0 30.6 %collective-permute-start.59 = (bf16[128,1024]{1,0:T(8,128)(2,1)S(1)}, bf16[128,1024]{1,0:T(8,128)(2,1)S(1)}, u32[]{:S(2)}, u32[]{:S(2)}) collective-permute-start(bf16[128,1024]{1,0:T(8,128)(2,1)S(1)} %get-tuple-element.352), channel_id=1, source_target_pairs={{0,4},{4,0},{8,12},{12,8},{1,5},{5,1},{9,13},{13,9},{2,6},{6,2},{1... | collective-permute-start | bytes 786440 | tf_op jit(solution)/shard_map/ppermute | solution.py:38
  278.6 19.3 %collective-permute-start.60 = (bf16[128,1024]{1,0:T(8,128)(2,1)S(1)}, bf16[128,1024]{1,0:T(8,128)(2,1)S(1)}, u32[]{:S(2)}, u32[]{:S(2)}) collective-permute-start(bf16[128,1024]{1,0:T(8,128)(2,1)S(1)} %get-tuple-element.353), channel_id=1, source_target_pairs={{0,8},{4,12},{8,0},{12,4},{1,9},{5,13},{9,1},{13,5},{2,10},{6,14},... | collective-permute-start | bytes 786440 | tf_op jit(solution)/shard_map/ppermute | solution.py:38
  279.1 18.8 %collective-permute-start.61 = (bf16[128,1024]{1,0:T(8,128)(2,1)S(1)}, bf16[128,1024]{1,0:T(8,128)(2,1)S(1)}, u32[]{:S(2)}, u32[]{:S(2)}) collective-permute-start(bf16[128,1024]{1,0:T(8,128)(2,1)S(1)} %get-tuple-element.354), channel_id=1, source_target_pairs={{0,12},{4,8},{8,4},{12,0},{1,13},{5,9},{9,5},{13,1},{2,14},{6,10},... | collective-permute-start | bytes 786440 | tf_op jit(solution)/shard_map/ppermute | solution.py:38
  281.1 1.4 collective-permute-start.56
  282.5 4.9 %collective-permute-start.57 = (f32[24,1024]{1,0:T(8,128)S(1)}, f32[24,1024]{1,0:T(8,128)S(1)}, u32[]{:S(2)}, u32[]{:S(2)}) collective-permute-start(f32[24,1024]{1,0:T(8,128)S(1)} %add.41), channel_id=1, source_target_pairs={{0,16},{16,0},{1,17},{17,1},{2,18},{18,2},{3,19},{19,3},{4,20},{20... | collective-permute-start | bytes 294920 | tf_op jit(solution)/shard_map/ppermute | solution.py:38
  287.4 6.6 %collective-permute-start.58 = (f32[8,1024]{1,0:T(8,128)S(1)}, f32[8,1024]{1,0:T(8,128)S(1)}, u32[]{:S(2)}, u32[]{:S(2)}) collective-permute-start(f32[8,1024]{1,0:T(8,128)S(1)} %slice.22), channel_id=1, source_target_pairs={{0,2},{1,3},{2,0},{3,1},{4,6},{5,7},{6,4},{7,5},{8,10},{9,11},{10,... | collective-permute-start | bytes 98312 | tf_op jit(solution)/shard_map/ppermute | solution.py:38
  (20 other events, 184.1 us)

commit v3 on v2

--- a/solution.py
+++ b/solution.py
@@ -23,7 +23,7 @@
 
 
 PINNED = False
-SCALES = {"project": 0.1, "attend": 1, "merge": 0.1, "feed": 0.1, "feed_back": 0.003, "split": 30, "attend_back": 1, "project_back": 100, "last": 10, "grad_core": 30, "grad_shard": 30, "grad_own": 30, "grad_sum": 30, "tally": 30, "leave": 30, "entry": 10, "own_rows": 1, "pack": 0.01, "pack_feed": 0.01}
+SCALES = {"project": 0.1, "attend": 1, "merge": 0.1, "feed": 0.1, "feed_back": 0.003, "split": 30, "attend_back": 1, "project_back": 100, "last": 10, "grad_core": 30, "grad_shard": 30, "grad_own": 100, "grad_sum": 30, "tally": 30, "leave": 30, "entry": 10, "own_rows": 10, "pack": 0.01, "pack_feed": 0.01}
 
 
 def cost(name, flops, nbytes):
@@ -1114,7 +1114,7 @@
             val.feed_weights[0] = (feed_mine, across, feed_side, side)
 
     def run_feed(c):
-        held, _ = order.hold(start[c], count)
+        (held,) = order.hold(start[c])
         first, normed, hidden, slope, mine = feed(
             held, *val.branch[c], vec, biases, val.feed_weights[0]
         )

time: 300 us -> 300 us (level)
  transfers between devices with their start and end apart: 62 -> 62, of which waited for: 21 -> 23; matrix products, arithmetic and copies ran while one was open for 2% -> 2% of each run, Pallas kernels for 32% -> 32%
where the time goes in v3:
time: 300 us; the launch traced here: 299 us
  Pallas kernels  104 us (35%)
  starting transfers between devices  97.7 us (33%)
  waiting for transfers between devices  88.6 us (30%)
  local copies, waits for them, and re-layouts  3.64 us (1%)
    ppermute x62, starting transfers between devices, swap(): return lax.ppermute(value, axis, [(i, i ^ bit) for i in range(size)])  97.7 us
    ppermute x62, waiting for transfers between devices, swap(): return lax.ppermute(value, axis, [(i, i ^ bit) for i in range(size)])  88.6 us
    pallas_call x28, Pallas kernels, call(): pl.pallas_call(kernel, in_specs=[pl.BlockSpec(memory_space=pltpu.SMEM)] *...  81.4 us
    pallas_call x6, Pallas kernels, grid_call(): pl.pallas_call(kernel, grid_spec=pltpu.PrefetchScalarGridSpec(num_scalar_...  22.5 us
  transfers between devices with their start and end apart: 62, of which 23 were waited for; matrix products, arithmetic and copies ran while one was open for 2% of the time, Pallas kernels for 32%

profile of v3, /device:TPU:0, one launch (start us, length us, event | category | flops | bytes accessed | tf_op | source)
XLA Modules:
  0.0 298.8 jit_solution(3655215573972134395)
XLA Ops:
  0.8 1.8 pack.1.a_ref.refs_4_
  2.5 3.0 %collective-permute-start.2 = (bf16[512,768]{1,0:T(8,128)(2,1)S(1)}, bf16[512,768]{1,0:T(8,128)(2,1)S(1)}, u32[]{:S(2)}, u32[]{:S(2)}) collective-permute-start(bf16[512,768]{1,0:T(8,128)(2,1)S(1)} %pack.1.a_ref.refs_4_), channel_id=1, source_target_pairs={{0,16},{16,0},{1,17},{17,1},{2,18},{18,2},{3,19},{19,3},{4,20},{20... | collective-permute-start | bytes 2359304 | tf_op jit(solution)/shard_map/ppermute | solution.py:38
  10.6 1.6 collective-permute-start
  12.2 2.0 collective-permute-done
  14.3 2.7 collective-permute-start.1
  16.9 4.1 %entry.1 = (bf16[256,1024]{1,0:T(8,128)(2,1)S(1)}, bf16[256,1024]{1,0:T(8,128)(2,1)S(1)}, f32[256,1024]{1,0:T(8,128)S(1)}, f32[256,1024]{1,0:T(8,128)S(1)}) custom-call(s32[4]{0:T(128)S(1)} %pad_add_fusion.place, bf16[256,4,1024]{2,1,0:T(4,128)(2,1)} %x_ref.2, f32[4,1024]{1,0:T(4,128)} %convolution_add_fusion.embed_ref), custom_call_target="tpu_custom_call" | custom-call | flops 41943040 | bytes 52592640 | tf_op jit(solution)/shard_map/entry/pallas_call | solution.py:80
  21.1 3.0 %pack_feed.1 = (bf16[512,256]{1,0:T(8,128)(2,1)S(1)}, bf16[512,2048]{1,0:T(8,128)(2,1)S(1)}) custom-call(s32[4]{0:T(128)S(1)} %pad_add_fusion.place, bf16[512,256]{1,0:T(8,128)(2,1)} %out_ref.1, bf16[512,1024]{1,0:T(8,128)(2,1)} %up_ref.1, bf16[512,1024]{1,0:T(8,128)(2,1)} %down_ref.1), custom_call_target="tpu_custom_call" | custom-call | bytes 47185 | tf_op jit(solution)/shard_map/pack_feed/pallas_call | solution.py:80
  26.4 2.4 project.2
  28.8 4.1 %collective-permute-done.18.refs_5_.b_ref = bf16[512,256]{1,0:T(8,128)(2,1)S(1)} collective-permute-done((bf16[512,256]{1,0:T(8,128)(2,1)S(1)}, bf16[512,256]{1,0:T(8,128)(2,1)S(1)}, u32[]{:S(2)}, u32[]{:S(2)}) %collective-permute-start.18) | collective-permute-done | bytes 262176 | tf_op jit(solution)/shard_map/ppermute | solution.py:38
  33.6 1.6 collective-permute-start.9
  35.1 2.6 collective-permute-start.10
  37.9 3.7 %own_rows.1 = (bf16[256,1024]{1,0:T(8,128)(2,1)S(1)}, bf16[256,1024]{1,0:T(8,128)(2,1)S(1)}) custom-call(s32[4]{0:T(128)S(1)} %pad_add_fusion.place, bf16[256,4,1024]{2,1,0:T(4,128)(2,1)} %x_ref.3), custom_call_target="tpu_custom_call" | custom-call | flops 20971520 | bytes 31457280 | tf_op jit(solution)/shard_map/own_rows/pallas_call | solution.py:80
  41.6 2.4 project.3
  44.7 3.5 %collective-permute-start.7 = (bf16[256,384]{1,0:T(8,128)(2,1)S(1)}, bf16[256,384]{1,0:T(8,128)(2,1)S(1)}, u32[]{:S(2)}, u32[]{:S(2)}) collective-permute-start(bf16[256,384]{1,0:T(8,128)(2,1)S(1)} %get-tuple-element.212), channel_id=1, source_target_pairs={{0,8},{4,12},{8,0},{12,4},{1,9},{5,13},{9,1},{13,5},{2,10},{6,14},... | collective-permute-start | bytes 589832 | tf_op jit(solution)/shard_map/ppermute | solution.py:38
  48.2 4.1 %collective-permute-done.10.refs_2_ = bf16[256,384]{1,0:T(8,128)(2,1)S(1)} collective-permute-done((bf16[256,384]{1,0:T(8,128)(2,1)S(1)}, bf16[256,384]{1,0:T(8,128)(2,1)S(1)}, u32[]{:S(2)}, u32[]{:S(2)}) %collective-permute-start.10) | collective-permute-done | bytes 196640 | tf_op jit(solution)/shard_map/ppermute | solution.py:38
  52.4 2.5 collective-permute-start.8
  54.9 3.7 %attend.2 = (bf16[256,128]{1,0:T(8,128)(2,1)S(1)}, bf16[256,128]{1,0:T(8,128)(2,1)S(1)}, bf16[256,128]{1,0:T(8,128)(2,1)S(1)}, bf16[256,128]{1,0:T(8,128)(2,1)S(1)}, f32[2,1024]{1,0:T(2,128)S(1)}) custom-call(bf16[256,384]{1,0:T(8,128)(2,1)S(1)} %get-tuple-element.219.refs_0_, bf16[256,384]{1,0:T(8,128)(2,1)S(1)} %collective-permute-done.9.refs_1_, ...), custom_call_target="tpu_custom_call" | custom-call | flops 2147483648 | bytes 1056768 | tf_op jit(solution)/shard_map/attend/pallas_call | solution.py:101
  58.6 10.7 %collective-permute-start.15 = (bf16[256,128]{1,0:T(8,128)(2,1)S(1)}, bf16[256,128]{1,0:T(8,128)(2,1)S(1)}, u32[]{:S(2)}, u32[]{:S(2)}) collective-permute-start(bf16[256,128]{1,0:T(8,128)(2,1)S(1)} %get-tuple-element.233), channel_id=1, source_target_pairs={{0,4},{4,0},{8,12},{12,8},{1,5},{5,1},{9,13},{13,9},{2,6},{6,2},{1... | collective-permute-start | bytes 196616 | tf_op jit(solution)/shard_map/ppermute | solution.py:38
  69.9 3.3 %collective-permute-start.16 = (bf16[256,128]{1,0:T(8,128)(2,1)S(1)}, bf16[256,128]{1,0:T(8,128)(2,1)S(1)}, u32[]{:S(2)}, u32[]{:S(2)}) collective-permute-start(bf16[256,128]{1,0:T(8,128)(2,1)S(1)} %get-tuple-element.234), channel_id=1, source_target_pairs={{0,8},{4,12},{8,0},{12,4},{1,9},{5,13},{9,1},{13,5},{2,10},{6,14},... | collective-permute-start | bytes 196616 | tf_op jit(solution)/shard_map/ppermute | solution.py:38
  74.5 3.7 %attend.3 = (bf16[256,128]{1,0:T(8,128)(2,1)S(1)}, bf16[256,128]{1,0:T(8,128)(2,1)S(1)}, bf16[256,128]{1,0:T(8,128)(2,1)S(1)}, bf16[256,128]{1,0:T(8,128)(2,1)S(1)}, f32[2,1024]{1,0:T(2,128)S(1)}) custom-call(bf16[256,384]{1,0:T(8,128)(2,1)S(1)} %get-tuple-element.224.refs_0_, bf16[256,384]{1,0:T(8,128)(2,1)S(1)} %collective-permute-done.6.refs_1_, ...), custom_call_target="tpu_custom_call" | custom-call | flops 2147483648 | bytes 1056768 | tf_op jit(solution)/shard_map/attend/pallas_call | solution.py:101
  80.4 1.6 collective-permute-start.21
  83.2 1.8 collective-permute-start.13
  86.2 3.2 %collective-permute-start.14 = (bf16[256,128]{1,0:T(8,128)(2,1)S(1)}, bf16[256,128]{1,0:T(8,128)(2,1)S(1)}, u32[]{:S(2)}, u32[]{:S(2)}) collective-permute-start(bf16[256,128]{1,0:T(8,128)(2,1)S(1)} %get-tuple-element.231), channel_id=1, source_target_pairs={{0,12},{4,8},{8,4},{12,0},{1,13},{5,9},{9,5},{13,1},{2,14},{6,10},... | collective-permute-start | bytes 196616 | tf_op jit(solution)/shard_map/ppermute | solution.py:38
  90.0 2.3 collective-permute-done.14.refs_3_
  95.2 5.0 %feed.2 = (f32[256,1024]{1,0:T(8,128)S(1)}, bf16[256,1024]{1,0:T(8,128)(2,1)S(1)}, bf16[256,2048]{1,0:T(8,128)(2,1)S(1)}, bf16[256,2048]{1,0:T(8,128)(2,1)S(1)}, bf16[256,1024]{1,0:T(8,128)(2,1)S(1)}) custom-call(f32[256,1024]{1,0:T(8,128)S(1)} %get-tuple-element.249.start_ref, bf16[256,1024]{1,0:T(8,128)(2,1)S(1)} %get-tuple-element.250.mine_ref, ...), custom_call_target="tpu_custom_call" | custom-call | flops 214748368 | bytes 1472512 | tf_op jit(solution)/shard_map/feed/pallas_call | solution.py:101
  100.2 1.6 collective-permute-start.26
  102.7 2.7 collective-permute-done.27
  105.4 2.8 collective-permute-done.25.theirs_ref
  108.2 5.2 %feed.3 = (f32[256,1024]{1,0:T(8,128)S(1)}, bf16[256,1024]{1,0:T(8,128)(2,1)S(1)}, bf16[256,2048]{1,0:T(8,128)(2,1)S(1)}, bf16[256,2048]{1,0:T(8,128)(2,1)S(1)}, bf16[256,1024]{1,0:T(8,128)(2,1)S(1)}) custom-call(f32[256,1024]{1,0:T(8,128)S(1)} %get-tuple-element.256.start_ref, bf16[256,1024]{1,0:T(8,128)(2,1)S(1)} %get-tuple-element.257.mine_ref, ...), custom_call_target="tpu_custom_call" | custom-call | flops 214748368 | bytes 1472512 | tf_op jit(solution)/shard_map/feed/pallas_call | solution.py:101
  114.1 5.4 %collective-permute-done.26.theirs_ref = bf16[256,1024]{1,0:T(8,128)(2,1)S(1)} collective-permute-done((bf16[256,1024]{1,0:T(8,128)(2,1)S(1)}, bf16[256,1024]{1,0:T(8,128)(2,1)S(1)}, u32[]{:S(2)}, u32[]{:S(2)}) %collective-permute-start.26) | collective-permute-done | bytes 524320 | tf_op jit(solution)/shard_map/ppermute | solution.py:38
  119.5 6.9 %feed_back.2 = (bf16[1,256,1024]{2,1,0:T(8,128)(2,1)S(1)}, f32[256,1024]{1,0:T(8,128)S(1)}, bf16[256,1024]{1,0:T(8,128)(2,1)S(1)}, bf16[256,2048]{1,0:T(8,128)(2...) custom-call(s32[4]{0:T(128)S(1)} %pad_add_fusion.place, ...), custom_call_target="tpu_custom_call" | custom-call | flops 6442450 | bytes 47529 | tf_op jit(solution)/shard_map/feed_back/pallas_call | solution.py:101
  127.0 3.7 %collective-permute-done.28.theirs_ref = bf16[256,1024]{1,0:T(8,128)(2,1)S(1)} collective-permute-done((bf16[256,1024]{1,0:T(8,128)(2,1)S(1)}, bf16[256,1024]{1,0:T(8,128)(2,1)S(1)}, u32[]{:S(2)}, u32[]{:S(2)}) %collective-permute-start.28) | collective-permute-done | bytes 524320 | tf_op jit(solution)/shard_map/ppermute | solution.py:38
  130.7 6.9 %feed_back.3 = (bf16[2,256,1024]{2,1,0:T(8,128)(2,1)S(1)}, f32[256,1024]{1,0:T(8,128)S(1)}, bf16[256,1024]{1,0:T(8,128)(2,1)S(1)}, bf16[256,2048]{1,0:T(8,128)(2...) custom-call(s32[4]{0:T(128)S(1)} %pad_add_fusion.place, ...), custom_call_target="tpu_custom_call" | custom-call | flops 6442450 | bytes 50577 | tf_op jit(solution)/shard_map/feed_back/pallas_call | solution.py:101
  137.6 2.1 collective-permute-done.29.theirs_ref
  139.6 2.4 split.2
  142.1 2.6 grad_core.2
  144.8 1.6 collective-permute-start.31
  147.8 1.8 collective-permute-start.36
  149.7 2.3 collective-permute-done.30.refs_8_
  151.9 2.6 collective-permute-start.37
  154.5 2.9 grad_shard.2
  157.4 1.7 collective-permute-done.31.theirs_ref
  159.8 2.5 split.3
  163.7 2.6 collective-permute-start.33
  166.7 7.0 %attend_back.2 = (bf16[256,384]{1,0:T(8,128)(2,1)S(1)}, bf16[256,384]{1,0:T(8,128)(2,1)S(1)}, bf16[256,384]{1,0:T(8,128)(2,1)S(1)}, bf16[256,384]{1,0:T(8,128)(2,1)S(1)}) custom-call(bf16[256,384]{1,0:T(8,128)(2,1)S(1)} %get-tuple-element.219.refs_0_, bf16[256,384]{1,0:T(8,128)(2,1)S(1)} %collective-permute-done.9.refs_1_, ...), custom_call_target="tpu_custom_call" | custom-call | flops 5368709120 | bytes 1843200 | tf_op jit(solution)/shard_map/attend_back/pallas_call | solution.py:101
  174.3 3.5 %collective-permute-start.43 = (bf16[256,384]{1,0:T(8,128)(2,1)S(1)}, bf16[256,384]{1,0:T(8,128)(2,1)S(1)}, u32[]{:S(2)}, u32[]{:S(2)}) collective-permute-start(bf16[256,384]{1,0:T(8,128)(2,1)S(1)} %get-tuple-element.307), channel_id=1, source_target_pairs={{0,8},{4,12},{8,0},{12,4},{1,9},{5,13},{9,1},{13,5},{2,10},{6,14},... | collective-permute-start | bytes 589832 | tf_op jit(solution)/shard_map/ppermute | solution.py:38
  178.2 7.2 %attend_back.3 = (bf16[256,384]{1,0:T(8,128)(2,1)S(1)}, bf16[256,384]{1,0:T(8,128)(2,1)S(1)}, bf16[256,384]{1,0:T(8,128)(2,1)S(1)}, bf16[256,384]{1,0:T(8,128)(2,1)S(1)}) custom-call(bf16[256,384]{1,0:T(8,128)(2,1)S(1)} %get-tuple-element.224.refs_0_, bf16[256,384]{1,0:T(8,128)(2,1)S(1)} %collective-permute-done.6.refs_1_, ...), custom_call_target="tpu_custom_call" | custom-call | flops 5368709120 | bytes 1843200 | tf_op jit(solution)/shard_map/attend_back/pallas_call | solution.py:101
  185.7 4.9 %leave.2 = bf16[256,4,1024]{2,1,0:T(4,128)(2,1)} custom-call(s32[4]{0:T(128)S(1)} %pad_add_fusion.place, bf16[2,256,1024]{2,1,0:T(8,128)(2,1)S(1)} %get-tuple-element.301.own_ref, bf16[2,256,1024]{2,1,0:T(8,128)(2,1)S(1)} %collective-permute-done.38.other_ref), custom_call_target="tpu_custom_call" | custom-call | flops 31457280 | bytes 125829120 | tf_op jit(solution)/shard_map/leave/pallas_call | solution.py:80
  190.7 3.8 %collective-permute-start.40 = (bf16[256,384]{1,0:T(8,128)(2,1)S(1)}, bf16[256,384]{1,0:T(8,128)(2,1)S(1)}, u32[]{:S(2)}, u32[]{:S(2)}) collective-permute-start(bf16[256,384]{1,0:T(8,128)(2,1)S(1)} %get-tuple-element.304), channel_id=1, source_target_pairs={{0,8},{4,12},{8,0},{12,4},{1,9},{5,13},{9,1},{13,5},{2,10},{6,14},... | collective-permute-start | bytes 589832 | tf_op jit(solution)/shard_map/ppermute | solution.py:38
  194.8 2.5 project_back.2
  198.8 8.6 %collective-permute-done.40.refs_2_ = bf16[256,384]{1,0:T(8,128)(2,1)S(1)} collective-permute-done((bf16[256,384]{1,0:T(8,128)(2,1)S(1)}, bf16[256,384]{1,0:T(8,128)(2,1)S(1)}, u32[]{:S(2)}, u32[]{:S(2)}) %collective-permute-start.40) | collective-permute-done | bytes 196640 | tf_op jit(solution)/shard_map/ppermute | solution.py:38
  207.5 1.7 project_back.3
  212.8 3.6 %grad_own.2 = (f32[128,2048]{1,0:T(8,128)S(1)}, bf16[128,2048]{1,0:T(8,128)(2,1)S(1)}, bf16[128,2048]{1,0:T(8,128)(2,1)S(1)}, bf16[128,2048]{1,0:T(8,128)(2,1)S(1)}) custom-call(s32[4]{0:T(128)S(1)} %pad_add_fusion.place, bf16[256,1024]{1,0:T(8,128)(2,1)S(1)} %copy-done.14, bf16[256,1024]{1,0:T(8,128)(2,1)S(1)} %copy-done.16, ...), custom_call_target="tpu_custom_call" | custom-call | flops 107374182400 | bytes 1520435200 | tf_op jit(solution)/shard_map/grad_own/pallas_call | solution.py:101
  219.4 3.7 %collective-permute-start.54 = (f32[24,1024]{1,0:T(8,128)S(1)}, f32[24,1024]{1,0:T(8,128)S(1)}, u32[]{:S(2)}, u32[]{:S(2)}) collective-permute-start(f32[24,1024]{1,0:T(8,128)S(1)} %tally.1), channel_id=1, source_target_pairs={{0,4},{4,0},{8,12},{12,8},{1,5},{5,1},{9,13},{13,9},{2,6},{6,2},{1... | collective-permute-start | bytes 294920 | tf_op jit(solution)/shard_map/ppermute | solution.py:38
  224.7 3.0 %collective-permute-start.47 = (bf16[128,2048]{1,0:T(8,128)(2,1)S(1)}, bf16[128,2048]{1,0:T(8,128)(2,1)S(1)}, u32[]{:S(2)}, u32[]{:S(2)}) collective-permute-start(bf16[128,2048]{1,0:T(8,128)(2,1)S(1)} %get-tuple-element.331), channel_id=1, source_target_pairs={{0,8},{4,12},{8,0},{12,4},{1,9},{5,13},{9,1},{13,5},{2,10},{6,14},... | collective-permute-start | bytes 1572872 | tf_op jit(solution)/shard_map/ppermute | solution.py:38
  229.1 6.5 %collective-permute-done.51.theirs_ref = bf16[256,1024]{1,0:T(8,128)(2,1)S(1)} collective-permute-done((bf16[256,1024]{1,0:T(8,128)(2,1)S(1)}, bf16[256,1024]{1,0:T(8,128)(2,1)S(1)}, u32[]{:S(2)}, u32[]{:S(2)}) %collective-permute-start.51) | collective-permute-done | bytes 524320 | tf_op jit(solution)/shard_map/ppermute | solution.py:38
  237.0 10.3 %collective-permute-done.46.refs_1_ = bf16[128,2048]{1,0:T(8,128)(2,1)S(1)} collective-permute-done((bf16[128,2048]{1,0:T(8,128)(2,1)S(1)}, bf16[128,2048]{1,0:T(8,128)(2,1)S(1)}, u32[]{:S(2)}, u32[]{:S(2)}) %collective-permute-start.46) | collective-permute-done | bytes 524320 | tf_op jit(solution)/shard_map/ppermute | solution.py:38
  247.3 17.8 %collective-permute-done.47.refs_2_ = bf16[128,2048]{1,0:T(8,128)(2,1)S(1)} collective-permute-done((bf16[128,2048]{1,0:T(8,128)(2,1)S(1)}, bf16[128,2048]{1,0:T(8,128)(2,1)S(1)}, u32[]{:S(2)}, u32[]{:S(2)}) %collective-permute-start.47) | collective-permute-done | bytes 524320 | tf_op jit(solution)/shard_map/ppermute | solution.py:38
  266.2 1.6 grad_own.3
  267.9 10.2 %collective-permute-start.59 = (bf16[128,1024]{1,0:T(8,128)(2,1)S(1)}, bf16[128,1024]{1,0:T(8,128)(2,1)S(1)}, u32[]{:S(2)}, u32[]{:S(2)}) collective-permute-start(bf16[128,1024]{1,0:T(8,128)(2,1)S(1)} %get-tuple-element.352), channel_id=1, source_target_pairs={{0,4},{4,0},{8,12},{12,8},{1,5},{5,1},{9,13},{13,9},{2,6},{6,2},{1... | collective-permute-start | bytes 786440 | tf_op jit(solution)/shard_map/ppermute | solution.py:38
  283.5 3.4 %collective-permute-done.57 = f32[24,1024]{1,0:T(8,128)S(1)} collective-permute-done((f32[24,1024]{1,0:T(8,128)S(1)}, f32[24,1024]{1,0:T(8,128)S(1)}, u32[]{:S(2)}, u32[]{:S(2)}) %collective-permute-start.57) | collective-permute-done | bytes 98336 | tf_op jit(solution)/shard_map/ppermute | solution.py:38
  287.5 5.0 %leave.3 = f32[256,4,1024]{2,1,0:T(4,128)} custom-call(s32[4]{0:T(128)S(1)} %pad_add_fusion.place, f32[2,256,1024]{2,1,0:T(8,128)S(1)} %last.3.own_ref, f32[2,256,1024]{2,1,0:T(8,128)S(1)} %collective-permute-done.53.other_ref), custom_call_target="tpu_custom_call" | custom-call | flops 31457280 | bytes 251658240 | tf_op jit(solution)/shard_map/leave/pallas_call | solution.py:80
  292.5 2.6 finish.1
  295.1 2.3 collective-permute-done.60.refs_2_
  (163 shorter events, 47.7 us)
Async XLA Ops:
  2.5 21.5 %collective-permute-start.2 = (bf16[512,768]{1,0:T(8,128)(2,1)S(1)}, bf16[512,768]{1,0:T(8,128)(2,1)S(1)}, u32[]{:S(2)}, u32[]{:S(2)}) collective-permute-start(bf16[512,768]{1,0:T(8,128)(2,1)S(1)} %pack.1.a_ref.refs_4_), channel_id=1, source_target_pairs={{0,16},{16,0},{1,17},{17,1},{2,18},{18,2},{3,19},{19,3},{4,20},{20... | collective-permute-start | bytes 2359304 | tf_op jit(solution)/shard_map/ppermute | solution.py:38
  10.6 3.7 %collective-permute-start = (f32[8,128]{1,0:T(8,128)S(1)}, f32[8,128]{1,0:T(8,128)S(1)}, u32[]{:S(2)}, u32[]{:S(2)}) collective-permute-start(f32[8,128]{1,0:T(8,128)S(1)} %broadcast_in_dim.10), channel_id=1, source_target_pairs={{0,4},{4,0},{8,12},{12,8},{1,5},{5,1},{9,13},{13,9},{2,6},{6,2},{1... | collective-permute-start | bytes 12296 | tf_op jit(solution)/shard_map/ppermute | solution.py:38
  12.2 14.2 %collective-permute-start.3 = (bf16[512,768]{1,0:T(8,128)(2,1)S(1)}, bf16[512,768]{1,0:T(8,128)(2,1)S(1)}, u32[]{:S(2)}, u32[]{:S(2)}) collective-permute-start(bf16[512,768]{1,0:T(8,128)(2,1)S(1)} %pack.1.a_ref.refs_4_), channel_id=1, source_target_pairs={{0,1},{1,0},{2,3},{3,2},{4,5},{5,4},{6,7},{7,6},{8,9},{9,8},{10,11... | collective-permute-start | bytes 2359304 | tf_op jit(solution)/shard_map/ppermute | solution.py:38
  14.3 6.8 %collective-permute-start.1 = (f32[8,128]{1,0:T(8,128)S(1)}, f32[8,128]{1,0:T(8,128)S(1)}, u32[]{:S(2)}, u32[]{:S(2)}) collective-permute-start(f32[8,128]{1,0:T(8,128)S(1)} %add.36), channel_id=1, source_target_pairs={{0,8},{4,12},{8,0},{12,4},{1,9},{5,13},{9,1},{13,5},{2,10},{6,14},... | collective-permute-start | bytes 12296 | tf_op jit(solution)/shard_map/ppermute | solution.py:38
  24.1 2.4 collective-permute-start.4
  24.2 8.7 %collective-permute-start.18 = (bf16[512,256]{1,0:T(8,128)(2,1)S(1)}, bf16[512,256]{1,0:T(8,128)(2,1)S(1)}, u32[]{:S(2)}, u32[]{:S(2)}) collective-permute-start(bf16[512,256]{1,0:T(8,128)(2,1)S(1)} %get-tuple-element.241.refs_4_.a_ref), channel_id=1, source_target_pairs={{0,16},{16,0},{1,17},{17,1},{2,18},{18,2},{3,19},{19,3},{4,20},{20... | collective-permute-start | bytes 786440 | tf_op jit(solution)/shard_map/ppermute | solution.py:38
  24.9 1.6 collective-permute-start.5
  32.9 47.4 %collective-permute-start.22 = (bf16[512,2048]{1,0:T(8,128)(2,1)S(1)}, bf16[512,2048]{1,0:T(8,128)(2,1)S(1)}, u32[]{:S(2)}, u32[]{:S(2)}) collective-permute-start(bf16[512,2048]{1,0:T(8,128)(2,1)S(1)} %get-tuple-element.251.a_ref), channel_id=1, source_target_pairs={{0,16},{16,0},{1,17},{17,1},{2,18},{18,2},{3,19},{19,3},{4,20},{20... | collective-permute-start | bytes 6291464 | tf_op jit(solution)/shard_map/ppermute | solution.py:38
  33.6 11.2 %collective-permute-start.9 = (bf16[256,384]{1,0:T(8,128)(2,1)S(1)}, bf16[256,384]{1,0:T(8,128)(2,1)S(1)}, u32[]{:S(2)}, u32[]{:S(2)}) collective-permute-start(bf16[256,384]{1,0:T(8,128)(2,1)S(1)} %get-tuple-element.216), channel_id=1, source_target_pairs={{0,4},{4,0},{8,12},{12,8},{1,5},{5,1},{9,13},{13,9},{2,6},{6,2},{1... | collective-permute-start | bytes 589832 | tf_op jit(solution)/shard_map/ppermute | solution.py:38
  35.1 17.2 %collective-permute-start.10 = (bf16[256,384]{1,0:T(8,128)(2,1)S(1)}, bf16[256,384]{1,0:T(8,128)(2,1)S(1)}, u32[]{:S(2)}, u32[]{:S(2)}) collective-permute-start(bf16[256,384]{1,0:T(8,128)(2,1)S(1)} %get-tuple-element.217), channel_id=1, source_target_pairs={{0,8},{4,12},{8,0},{12,4},{1,9},{5,13},{9,1},{13,5},{2,10},{6,14},... | collective-permute-start | bytes 589832 | tf_op jit(solution)/shard_map/ppermute | solution.py:38
  37.7 17.2 %collective-permute-start.11 = (bf16[256,384]{1,0:T(8,128)(2,1)S(1)}, bf16[256,384]{1,0:T(8,128)(2,1)S(1)}, u32[]{:S(2)}, u32[]{:S(2)}) collective-permute-start(bf16[256,384]{1,0:T(8,128)(2,1)S(1)} %get-tuple-element.218), channel_id=1, source_target_pairs={{0,12},{4,8},{8,4},{12,0},{1,13},{5,9},{9,5},{13,1},{2,14},{6,10},... | collective-permute-start | bytes 589832 | tf_op jit(solution)/shard_map/ppermute | solution.py:38
  44.0 25.4 %collective-permute-start.6 = (bf16[256,384]{1,0:T(8,128)(2,1)S(1)}, bf16[256,384]{1,0:T(8,128)(2,1)S(1)}, u32[]{:S(2)}, u32[]{:S(2)}) collective-permute-start(bf16[256,384]{1,0:T(8,128)(2,1)S(1)} %get-tuple-element.211), channel_id=1, source_target_pairs={{0,4},{4,0},{8,12},{12,8},{1,5},{5,1},{9,13},{13,9},{2,6},{6,2},{1... | collective-permute-start | bytes 589832 | tf_op jit(solution)/shard_map/ppermute | solution.py:38
  44.7 24.6 %collective-permute-start.7 = (bf16[256,384]{1,0:T(8,128)(2,1)S(1)}, bf16[256,384]{1,0:T(8,128)(2,1)S(1)}, u32[]{:S(2)}, u32[]{:S(2)}) collective-permute-start(bf16[256,384]{1,0:T(8,128)(2,1)S(1)} %get-tuple-element.212), channel_id=1, source_target_pairs={{0,8},{4,12},{8,0},{12,4},{1,9},{5,13},{9,1},{13,5},{2,10},{6,14},... | collective-permute-start | bytes 589832 | tf_op jit(solution)/shard_map/ppermute | solution.py:38
  52.4 17.5 %collective-permute-start.8 = (bf16[256,384]{1,0:T(8,128)(2,1)S(1)}, bf16[256,384]{1,0:T(8,128)(2,1)S(1)}, u32[]{:S(2)}, u32[]{:S(2)}) collective-permute-start(bf16[256,384]{1,0:T(8,128)(2,1)S(1)} %get-tuple-element.213), channel_id=1, source_target_pairs={{0,12},{4,8},{8,4},{12,0},{1,13},{5,9},{9,5},{13,1},{2,14},{6,10},... | collective-permute-start | bytes 589832 | tf_op jit(solution)/shard_map/ppermute | solution.py:38
  58.6 14.5 %collective-permute-start.15 = (bf16[256,128]{1,0:T(8,128)(2,1)S(1)}, bf16[256,128]{1,0:T(8,128)(2,1)S(1)}, u32[]{:S(2)}, u32[]{:S(2)}) collective-permute-start(bf16[256,128]{1,0:T(8,128)(2,1)S(1)} %get-tuple-element.233), channel_id=1, source_target_pairs={{0,4},{4,0},{8,12},{12,8},{1,5},{5,1},{9,13},{13,9},{2,6},{6,2},{1... | collective-permute-start | bytes 196616 | tf_op jit(solution)/shard_map/ppermute | solution.py:38
  69.4 9.9 %collective-permute-start.19 = (bf16[512,256]{1,0:T(8,128)(2,1)S(1)}, bf16[512,256]{1,0:T(8,128)(2,1)S(1)}, u32[]{:S(2)}, u32[]{:S(2)}) collective-permute-start(bf16[512,256]{1,0:T(8,128)(2,1)S(1)} %get-tuple-element.241.refs_4_.a_ref), channel_id=1, source_target_pairs={{0,1},{1,0},{2,3},{3,2},{4,5},{5,4},{6,7},{7,6},{8,9},{9,8},{10,11... | collective-permute-start | bytes 786440 | tf_op jit(solution)/shard_map/ppermute | solution.py:38
  69.4 9.9 %collective-permute-start.20 = (bf16[512,256]{1,0:T(8,128)(2,1)S(1)}, bf16[512,256]{1,0:T(8,128)(2,1)S(1)}, u32[]{:S(2)}, u32[]{:S(2)}) collective-permute-start(bf16[512,256]{1,0:T(8,128)(2,1)S(1)} %collective-permute-done.18.refs_5_.b_ref), channel_id=1, source_target_pairs={{0,1},{1,0},{2,3},{3,2},{4,5},{5,4},{6,7},{7,6},{8,9},{9,8},{10,11... | collective-permute-start | bytes 786440 | tf_op jit(solution)/shard_map/ppermute | solution.py:38
  69.9 8.4 %collective-permute-start.16 = (bf16[256,128]{1,0:T(8,128)(2,1)S(1)}, bf16[256,128]{1,0:T(8,128)(2,1)S(1)}, u32[]{:S(2)}, u32[]{:S(2)}) collective-permute-start(bf16[256,128]{1,0:T(8,128)(2,1)S(1)} %get-tuple-element.234), channel_id=1, source_target_pairs={{0,8},{4,12},{8,0},{12,4},{1,9},{5,13},{9,1},{13,5},{2,10},{6,14},... | collective-permute-start | bytes 196616 | tf_op jit(solution)/shard_map/ppermute | solution.py:38
  73.2 6.1 %collective-permute-start.17 = (bf16[256,128]{1,0:T(8,128)(2,1)S(1)}, bf16[256,128]{1,0:T(8,128)(2,1)S(1)}, u32[]{:S(2)}, u32[]{:S(2)}) collective-permute-start(bf16[256,128]{1,0:T(8,128)(2,1)S(1)} %get-tuple-element.235), channel_id=1, source_target_pairs={{0,12},{4,8},{8,4},{12,0},{1,13},{5,9},{9,5},{13,1},{2,14},{6,10},... | collective-permute-start | bytes 196616 | tf_op jit(solution)/shard_map/ppermute | solution.py:38
  78.3 15.6 %collective-permute-start.23 = (bf16[512,2048]{1,0:T(8,128)(2,1)S(1)}, bf16[512,2048]{1,0:T(8,128)(2,1)S(1)}, u32[]{:S(2)}, u32[]{:S(2)}) collective-permute-start(bf16[512,2048]{1,0:T(8,128)(2,1)S(1)} %get-tuple-element.251.a_ref), channel_id=1, source_target_pairs={{0,1},{1,0},{2,3},{3,2},{4,5},{5,4},{6,7},{7,6},{8,9},{9,8},{10,11... | collective-permute-start | bytes 6291464 | tf_op jit(solution)/shard_map/ppermute | solution.py:38
  80.3 14.9 %collective-permute-start.24 = (bf16[512,2048]{1,0:T(8,128)(2,1)S(1)}, bf16[512,2048]{1,0:T(8,128)(2,1)S(1)}, u32[]{:S(2)}, u32[]{:S(2)}) collective-permute-start(bf16[512,2048]{1,0:T(8,128)(2,1)S(1)} %collective-permute-done.22.b_ref), channel_id=1, source_target_pairs={{0,1},{1,0},{2,3},{3,2},{4,5},{5,4},{6,7},{7,6},{8,9},{9,8},{10,11... | collective-permute-start | bytes 6291464 | tf_op jit(solution)/shard_map/ppermute | solution.py:38
  80.4 14.8 %collective-permute-start.21 = (bf16[256,1024]{1,0:T(8,128)(2,1)S(1)}, bf16[256,1024]{1,0:T(8,128)(2,1)S(1)}, u32[]{:S(2)}, u32[]{:S(2)}) collective-permute-start(bf16[256,1024]{1,0:T(8,128)(2,1)S(1)} %get-tuple-element.250.mine_ref), channel_id=1, source_target_pairs={{0,2},{1,3},{2,0},{3,1},{4,6},{5,7},{6,4},{7,5},{8,10},{9,11},{10,... | collective-permute-start | bytes 1572872 | tf_op jit(solution)/shard_map/ppermute | solution.py:38
  81.9 4.3 %collective-permute-start.12 = (bf16[256,128]{1,0:T(8,128)(2,1)S(1)}, bf16[256,128]{1,0:T(8,128)(2,1)S(1)}, u32[]{:S(2)}, u32[]{:S(2)}) collective-permute-start(bf16[256,128]{1,0:T(8,128)(2,1)S(1)} %get-tuple-element.229), channel_id=1, source_target_pairs={{0,4},{4,0},{8,12},{12,8},{1,5},{5,1},{9,13},{13,9},{2,6},{6,2},{1... | collective-permute-start | bytes 196616 | tf_op jit(solution)/shard_map/ppermute | solution.py:38
  83.2 6.8 %collective-permute-start.13 = (bf16[256,128]{1,0:T(8,128)(2,1)S(1)}, bf16[256,128]{1,0:T(8,128)(2,1)S(1)}, u32[]{:S(2)}, u32[]{:S(2)}) collective-permute-start(bf16[256,128]{1,0:T(8,128)(2,1)S(1)} %get-tuple-element.230), channel_id=1, source_target_pairs={{0,8},{4,12},{8,0},{12,4},{1,9},{5,13},{9,1},{13,5},{2,10},{6,14},... | collective-permute-start | bytes 196616 | tf_op jit(solution)/shard_map/ppermute | solution.py:38
  86.2 6.1 %collective-permute-start.14 = (bf16[256,128]{1,0:T(8,128)(2,1)S(1)}, bf16[256,128]{1,0:T(8,128)(2,1)S(1)}, u32[]{:S(2)}, u32[]{:S(2)}) collective-permute-start(bf16[256,128]{1,0:T(8,128)(2,1)S(1)} %get-tuple-element.231), channel_id=1, source_target_pairs={{0,12},{4,8},{8,4},{12,0},{1,13},{5,9},{9,5},{13,1},{2,14},{6,10},... | collective-permute-start | bytes 196616 | tf_op jit(solution)/shard_map/ppermute | solution.py:38
  93.3 14.9 %collective-permute-start.25 = (bf16[256,1024]{1,0:T(8,128)(2,1)S(1)}, bf16[256,1024]{1,0:T(8,128)(2,1)S(1)}, u32[]{:S(2)}, u32[]{:S(2)}) collective-permute-start(bf16[256,1024]{1,0:T(8,128)(2,1)S(1)} %get-tuple-element.257.mine_ref), channel_id=1, source_target_pairs={{0,2},{1,3},{2,0},{3,1},{4,6},{5,7},{6,4},{7,5},{8,10},{9,11},{10,... | collective-permute-start | bytes 1572872 | tf_op jit(solution)/shard_map/ppermute | solution.py:38
  100.2 54.3 %copy-start.13 = (bf16[256,1024]{1,0:T(8,128)(2,1)}, bf16[256,1024]{1,0:T(8,128)(2,1)S(1)}, u32[]{:S(2)}) copy-start(bf16[256,1024]{1,0:T(8,128)(2,1)S(1)} %get-tuple-element.328.refs_0_) | copy-start | bytes 1572868
  100.2 19.2 %collective-permute-start.26 = (bf16[256,1024]{1,0:T(8,128)(2,1)S(1)}, bf16[256,1024]{1,0:T(8,128)(2,1)S(1)}, u32[]{:S(2)}, u32[]{:S(2)}) collective-permute-start(bf16[256,1024]{1,0:T(8,128)(2,1)S(1)} %get-tuple-element.260.mine_ref), channel_id=1, source_target_pairs={{0,2},{1,3},{2,0},{3,1},{4,6},{5,7},{6,4},{7,5},{8,10},{9,11},{10,... | collective-permute-start | bytes 1572872 | tf_op jit(solution)/shard_map/ppermute | solution.py:38
  101.8 3.6 %collective-permute-start.27 = (f32[8,128]{1,0:T(8,128)S(1)}, f32[8,128]{1,0:T(8,128)S(1)}, u32[]{:S(2)}, u32[]{:S(2)}) collective-permute-start(f32[8,128]{1,0:T(8,128)S(1)} %add.37), channel_id=1, source_target_pairs={{0,16},{16,0},{1,17},{17,1},{2,18},{18,2},{3,19},{19,3},{4,20},{20... | collective-permute-start | bytes 12296 | tf_op jit(solution)/shard_map/ppermute | solution.py:38
  113.5 41.0 %copy-start.11 = (bf16[256,2048]{1,0:T(8,128)(2,1)}, bf16[256,2048]{1,0:T(8,128)(2,1)S(1)}, u32[]{:S(2)}) copy-start(bf16[256,2048]{1,0:T(8,128)(2,1)S(1)} %get-tuple-element.283.refs_7_) | copy-start | bytes 3145732
  113.5 17.2 %collective-permute-start.28 = (bf16[256,1024]{1,0:T(8,128)(2,1)S(1)}, bf16[256,1024]{1,0:T(8,128)(2,1)S(1)}, u32[]{:S(2)}, u32[]{:S(2)}) collective-permute-start(bf16[256,1024]{1,0:T(8,128)(2,1)S(1)} %get-tuple-element.268.mine_ref), channel_id=1, source_target_pairs={{0,2},{1,3},{2,0},{3,1},{4,6},{5,7},{6,4},{7,5},{8,10},{9,11},{10,... | collective-permute-start | bytes 1572872 | tf_op jit(solution)/shard_map/ppermute | solution.py:38
  126.4 13.3 %collective-permute-start.29 = (bf16[256,1024]{1,0:T(8,128)(2,1)S(1)}, bf16[256,1024]{1,0:T(8,128)(2,1)S(1)}, u32[]{:S(2)}, u32[]{:S(2)}) collective-permute-start(bf16[256,1024]{1,0:T(8,128)(2,1)S(1)} %get-tuple-element.275.mine_ref), channel_id=1, source_target_pairs={{0,2},{1,3},{2,0},{3,1},{4,6},{5,7},{6,4},{7,5},{8,10},{9,11},{10,... | collective-permute-start | bytes 1572872 | tf_op jit(solution)/shard_map/ppermute | solution.py:38
  144.7 7.2 %collective-permute-start.30 = (bf16[1024,2048]{1,0:T(8,128)(2,1)S(1)}, bf16[1024,2048]{1,0:T(8,128)(2,1)S(1)}, u32[]{:S(2)}, u32[]{:S(2)}) collective-permute-start(bf16[1024,2048]{1,0:T(8,128)(2,1)S(1)} %grad_core.2), channel_id=1, source_target_pairs={{0,1},{1,0},{2,3},{3,2},{4,5},{5,4},{6,7},{7,6},{8,9},{9,8},{10,11... | collective-permute-start | bytes 12582920 | tf_op jit(solution)/shard_map/ppermute | solution.py:38
  144.8 14.3 %collective-permute-start.31 = (bf16[256,1024]{1,0:T(8,128)(2,1)S(1)}, bf16[256,1024]{1,0:T(8,128)(2,1)S(1)}, u32[]{:S(2)}, u32[]{:S(2)}) collective-permute-start(bf16[256,1024]{1,0:T(8,128)(2,1)S(1)} %get-tuple-element.286.mine_ref), channel_id=1, source_target_pairs={{0,2},{1,3},{2,0},{3,1},{4,6},{5,7},{6,4},{7,5},{8,10},{9,11},{10,... | collective-permute-start | bytes 1572872 | tf_op jit(solution)/shard_map/ppermute | solution.py:38
  146.4 39.0 %collective-permute-start.38 = (bf16[2,256,1024]{2,1,0:T(8,128)(2,1)S(1)}, bf16[2,256,1024]{2,1,0:T(8,128)(2,1)S(1)}, u32[]{:S(2)}, u32[]{:S(2)}) collective-permute-start(bf16[2,256,1024]{2,1,0:T(8,128)(2,1)S(1)} %get-tuple-element.301.own_ref), channel_id=1, source_target_pairs={{0,1},{1,0},{2,3},{3,2},{4,5},{5,4},{6,7},{7,6},{8,9},{9,8},{10,11... | collective-permute-start | bytes 3145736 | tf_op jit(solution)/shard_map/ppermute | solution.py:38
  146.6 15.7 %collective-permute-start.35 = (bf16[256,128]{1,0:T(8,128)(2,1)S(1)}, bf16[256,128]{1,0:T(8,128)(2,1)S(1)}, u32[]{:S(2)}, u32[]{:S(2)}) collective-permute-start(bf16[256,128]{1,0:T(8,128)(2,1)S(1)} %get-tuple-element.292), channel_id=1, source_target_pairs={{0,4},{4,0},{8,12},{12,8},{1,5},{5,1},{9,13},{13,9},{2,6},{6,2},{1... | collective-permute-start | bytes 196616 | tf_op jit(solution)/shard_map/ppermute | solution.py:38
  147.8 15.9 %collective-permute-start.36 = (bf16[256,128]{1,0:T(8,128)(2,1)S(1)}, bf16[256,128]{1,0:T(8,128)(2,1)S(1)}, u32[]{:S(2)}, u32[]{:S(2)}) collective-permute-start(bf16[256,128]{1,0:T(8,128)(2,1)S(1)} %get-tuple-element.293), channel_id=1, source_target_pairs={{0,8},{4,12},{8,0},{12,4},{1,9},{5,13},{9,1},{13,5},{2,10},{6,14},... | collective-permute-start | bytes 196616 | tf_op jit(solution)/shard_map/ppermute | solution.py:38
  151.9 14.4 %collective-permute-start.37 = (bf16[256,128]{1,0:T(8,128)(2,1)S(1)}, bf16[256,128]{1,0:T(8,128)(2,1)S(1)}, u32[]{:S(2)}, u32[]{:S(2)}) collective-permute-start(bf16[256,128]{1,0:T(8,128)(2,1)S(1)} %get-tuple-element.294), channel_id=1, source_target_pairs={{0,12},{4,8},{8,4},{12,0},{1,13},{5,9},{9,5},{13,1},{2,14},{6,10},... | collective-permute-start | bytes 196616 | tf_op jit(solution)/shard_map/ppermute | solution.py:38
  159.1 52.3 %collective-permute-start.45 = (bf16[512,2048]{1,0:T(8,128)(2,1)}, bf16[512,2048]{1,0:T(8,128)(2,1)}, u32[]{:S(2)}, u32[]{:S(2)}) collective-permute-start(bf16[512,2048]{1,0:T(8,128)(2,1)} %grad_shard.2), channel_id=1, source_target_pairs={{0,16},{16,0},{1,17},{17,1},{2,18},{18,2},{3,19},{19,3},{4,20},{20... | collective-permute-start | bytes 6291464 | tf_op jit(solution)/shard_map/ppermute | solution.py:38
  162.2 11.5 %collective-permute-start.32 = (bf16[256,128]{1,0:T(8,128)(2,1)S(1)}, bf16[256,128]{1,0:T(8,128)(2,1)S(1)}, u32[]{:S(2)}, u32[]{:S(2)}) collective-permute-start(bf16[256,128]{1,0:T(8,128)(2,1)S(1)} %get-tuple-element.288), channel_id=1, source_target_pairs={{0,4},{4,0},{8,12},{12,8},{1,5},{5,1},{9,13},{13,9},{2,6},{6,2},{1... | collective-permute-start | bytes 196616 | tf_op jit(solution)/shard_map/ppermute | solution.py:38
  163.7 10.6 %collective-permute-start.33 = (bf16[256,128]{1,0:T(8,128)(2,1)S(1)}, bf16[256,128]{1,0:T(8,128)(2,1)S(1)}, u32[]{:S(2)}, u32[]{:S(2)}) collective-permute-start(bf16[256,128]{1,0:T(8,128)(2,1)S(1)} %get-tuple-element.289), channel_id=1, source_target_pairs={{0,8},{4,12},{8,0},{12,4},{1,9},{5,13},{9,1},{13,5},{2,10},{6,14},... | collective-permute-start | bytes 196616 | tf_op jit(solution)/shard_map/ppermute | solution.py:38
  166.3 11.5 %collective-permute-start.34 = (bf16[256,128]{1,0:T(8,128)(2,1)S(1)}, bf16[256,128]{1,0:T(8,128)(2,1)S(1)}, u32[]{:S(2)}, u32[]{:S(2)}) collective-permute-start(bf16[256,128]{1,0:T(8,128)(2,1)S(1)} %get-tuple-element.290), channel_id=1, source_target_pairs={{0,12},{4,8},{8,4},{12,0},{1,13},{5,9},{9,5},{13,1},{2,14},{6,10},... | collective-permute-start | bytes 196616 | tf_op jit(solution)/shard_map/ppermute | solution.py:38
  173.7 17.0 %collective-permute-start.42 = (bf16[256,384]{1,0:T(8,128)(2,1)S(1)}, bf16[256,384]{1,0:T(8,128)(2,1)S(1)}, u32[]{:S(2)}, u32[]{:S(2)}) collective-permute-start(bf16[256,384]{1,0:T(8,128)(2,1)S(1)} %get-tuple-element.306), channel_id=1, source_target_pairs={{0,4},{4,0},{8,12},{12,8},{1,5},{5,1},{9,13},{13,9},{2,6},{6,2},{1... | collective-permute-start | bytes 589832 | tf_op jit(solution)/shard_map/ppermute | solution.py:38
  174.3 20.1 %collective-permute-start.43 = (bf16[256,384]{1,0:T(8,128)(2,1)S(1)}, bf16[256,384]{1,0:T(8,128)(2,1)S(1)}, u32[]{:S(2)}, u32[]{:S(2)}) collective-permute-start(bf16[256,384]{1,0:T(8,128)(2,1)S(1)} %get-tuple-element.307), channel_id=1, source_target_pairs={{0,8},{4,12},{8,0},{12,4},{1,9},{5,13},{9,1},{13,5},{2,10},{6,14},... | collective-permute-start | bytes 589832 | tf_op jit(solution)/shard_map/ppermute | solution.py:38
  177.8 17.0 %collective-permute-start.44 = (bf16[256,384]{1,0:T(8,128)(2,1)S(1)}, bf16[256,384]{1,0:T(8,128)(2,1)S(1)}, u32[]{:S(2)}, u32[]{:S(2)}) collective-permute-start(bf16[256,384]{1,0:T(8,128)(2,1)S(1)} %get-tuple-element.308), channel_id=1, source_target_pairs={{0,12},{4,8},{8,4},{12,0},{1,13},{5,9},{9,5},{13,1},{2,14},{6,10},... | collective-permute-start | bytes 589832 | tf_op jit(solution)/shard_map/ppermute | solution.py:38
  185.4 13.4 %collective-permute-start.39 = (bf16[256,384]{1,0:T(8,128)(2,1)S(1)}, bf16[256,384]{1,0:T(8,128)(2,1)S(1)}, u32[]{:S(2)}, u32[]{:S(2)}) collective-permute-start(bf16[256,384]{1,0:T(8,128)(2,1)S(1)} %get-tuple-element.303), channel_id=1, source_target_pairs={{0,4},{4,0},{8,12},{12,8},{1,5},{5,1},{9,13},{13,9},{2,6},{6,2},{1... | collective-permute-start | bytes 589832 | tf_op jit(solution)/shard_map/ppermute | solution.py:38
  190.7 16.8 %collective-permute-start.40 = (bf16[256,384]{1,0:T(8,128)(2,1)S(1)}, bf16[256,384]{1,0:T(8,128)(2,1)S(1)}, u32[]{:S(2)}, u32[]{:S(2)}) collective-permute-start(bf16[256,384]{1,0:T(8,128)(2,1)S(1)} %get-tuple-element.304), channel_id=1, source_target_pairs={{0,8},{4,12},{8,0},{12,4},{1,9},{5,13},{9,1},{13,5},{2,10},{6,14},... | collective-permute-start | bytes 589832 | tf_op jit(solution)/shard_map/ppermute | solution.py:38
  194.4 13.0 %collective-permute-start.41 = (bf16[256,384]{1,0:T(8,128)(2,1)S(1)}, bf16[256,384]{1,0:T(8,128)(2,1)S(1)}, u32[]{:S(2)}, u32[]{:S(2)}) collective-permute-start(bf16[256,384]{1,0:T(8,128)(2,1)S(1)} %get-tuple-element.305), channel_id=1, source_target_pairs={{0,12},{4,8},{8,4},{12,0},{1,13},{5,9},{9,5},{13,1},{2,14},{6,10},... | collective-permute-start | bytes 589832 | tf_op jit(solution)/shard_map/ppermute | solution.py:38
  197.3 19.1 %collective-permute-start.49 = (bf16[256,1024]{1,0:T(8,128)(2,1)}, bf16[256,1024]{1,0:T(8,128)(2,1)}, u32[]{:S(2)}, u32[]{:S(2)}) collective-permute-start(bf16[256,1024]{1,0:T(8,128)(2,1)} %get-tuple-element.335.mine_ref), channel_id=1, source_target_pairs={{0,2},{1,3},{2,0},{3,1},{4,6},{5,7},{6,4},{7,5},{8,10},{9,11},{10,... | collective-permute-start | bytes 1572872 | tf_op jit(solution)/shard_map/ppermute | solution.py:38
  211.3 6.5 %collective-permute-start.50 = (bf16[1024,1024]{1,0:T(8,128)(2,1)S(1)}, bf16[1024,1024]{1,0:T(8,128)(2,1)S(1)}, u32[]{:S(2)}, u32[]{:S(2)}) collective-permute-start(bf16[1024,1024]{1,0:T(8,128)(2,1)S(1)} %grad_core.3), channel_id=1, source_target_pairs={{0,1},{1,0},{2,3},{3,2},{4,5},{5,4},{6,7},{7,6},{8,9},{9,8},{10,11... | collective-permute-start | bytes 6291464 | tf_op jit(solution)/shard_map/ppermute | solution.py:38
  218.8 47.4 %collective-permute-start.52 = (bf16[512,1024]{1,0:T(8,128)(2,1)S(1)}, bf16[512,1024]{1,0:T(8,128)(2,1)S(1)}, u32[]{:S(2)}, u32[]{:S(2)}) collective-permute-start(bf16[512,1024]{1,0:T(8,128)(2,1)S(1)} %grad_shard.3), channel_id=1, source_target_pairs={{0,16},{16,0},{1,17},{17,1},{2,18},{18,2},{3,19},{19,3},{4,20},{20... | collective-permute-start | bytes 3145736 | tf_op jit(solution)/shard_map/ppermute | solution.py:38
  219.4 8.3 %collective-permute-start.54 = (f32[24,1024]{1,0:T(8,128)S(1)}, f32[24,1024]{1,0:T(8,128)S(1)}, u32[]{:S(2)}, u32[]{:S(2)}) collective-permute-start(f32[24,1024]{1,0:T(8,128)S(1)} %tally.1), channel_id=1, source_target_pairs={{0,4},{4,0},{8,12},{12,8},{1,5},{5,1},{9,13},{13,9},{2,6},{6,2},{1... | collective-permute-start | bytes 294920 | tf_op jit(solution)/shard_map/ppermute | solution.py:38
  223.1 12.4 %collective-permute-start.51 = (bf16[256,1024]{1,0:T(8,128)(2,1)S(1)}, bf16[256,1024]{1,0:T(8,128)(2,1)S(1)}, u32[]{:S(2)}, u32[]{:S(2)}) collective-permute-start(bf16[256,1024]{1,0:T(8,128)(2,1)S(1)} %get-tuple-element.339.mine_ref), channel_id=1, source_target_pairs={{0,2},{1,3},{2,0},{3,1},{4,6},{5,7},{6,4},{7,5},{8,10},{9,11},{10,... | collective-permute-start | bytes 1572872 | tf_op jit(solution)/shard_map/ppermute | solution.py:38
  224.6 22.6 %collective-permute-start.46 = (bf16[128,2048]{1,0:T(8,128)(2,1)S(1)}, bf16[128,2048]{1,0:T(8,128)(2,1)S(1)}, u32[]{:S(2)}, u32[]{:S(2)}) collective-permute-start(bf16[128,2048]{1,0:T(8,128)(2,1)S(1)} %get-tuple-element.330), channel_id=1, source_target_pairs={{0,4},{4,0},{8,12},{12,8},{1,5},{5,1},{9,13},{13,9},{2,6},{6,2},{1... | collective-permute-start | bytes 1572872 | tf_op jit(solution)/shard_map/ppermute | solution.py:38
  224.7 40.4 %collective-permute-start.47 = (bf16[128,2048]{1,0:T(8,128)(2,1)S(1)}, bf16[128,2048]{1,0:T(8,128)(2,1)S(1)}, u32[]{:S(2)}, u32[]{:S(2)}) collective-permute-start(bf16[128,2048]{1,0:T(8,128)(2,1)S(1)} %get-tuple-element.331), channel_id=1, source_target_pairs={{0,8},{4,12},{8,0},{12,4},{1,9},{5,13},{9,1},{13,5},{2,10},{6,14},... | collective-permute-start | bytes 1572872 | tf_op jit(solution)/shard_map/ppermute | solution.py:38
  227.7 37.4 %collective-permute-start.48 = (bf16[128,2048]{1,0:T(8,128)(2,1)S(1)}, bf16[128,2048]{1,0:T(8,128)(2,1)S(1)}, u32[]{:S(2)}, u32[]{:S(2)}) collective-permute-start(bf16[128,2048]{1,0:T(8,128)(2,1)S(1)} %get-tuple-element.332), channel_id=1, source_target_pairs={{0,12},{4,8},{8,4},{12,0},{1,13},{5,9},{9,5},{13,1},{2,14},{6,10},... | collective-permute-start | bytes 1572872 | tf_op jit(solution)/shard_map/ppermute | solution.py:38
  235.6 44.9 %collective-permute-start.55 = (f32[24,1024]{1,0:T(8,128)S(1)}, f32[24,1024]{1,0:T(8,128)S(1)}, u32[]{:S(2)}, u32[]{:S(2)}) collective-permute-start(f32[24,1024]{1,0:T(8,128)S(1)} %add.39), channel_id=1, source_target_pairs={{0,8},{4,12},{8,0},{12,4},{1,9},{5,13},{9,1},{13,5},{2,10},{6,14},... | collective-permute-start | bytes 294920 | tf_op jit(solution)/shard_map/ppermute | solution.py:38
  247.3 40.2 %collective-permute-start.53 = (f32[2,256,1024]{2,1,0:T(8,128)S(1)}, f32[2,256,1024]{2,1,0:T(8,128)S(1)}, u32[]{:S(2)}, u32[]{:S(2)}) collective-permute-start(f32[2,256,1024]{2,1,0:T(8,128)S(1)} %last.3.own_ref), channel_id=1, source_target_pairs={{0,1},{1,0},{2,3},{3,2},{4,5},{5,4},{6,7},{7,6},{8,9},{9,8},{10,11... | collective-permute-start | bytes 6291464 | tf_op jit(solution)/shard_map/ppermute | solution.py:38
  267.9 27.2 %collective-permute-start.59 = (bf16[128,1024]{1,0:T(8,128)(2,1)S(1)}, bf16[128,1024]{1,0:T(8,128)(2,1)S(1)}, u32[]{:S(2)}, u32[]{:S(2)}) collective-permute-start(bf16[128,1024]{1,0:T(8,128)(2,1)S(1)} %get-tuple-element.352), channel_id=1, source_target_pairs={{0,4},{4,0},{8,12},{12,8},{1,5},{5,1},{9,13},{13,9},{2,6},{6,2},{1... | collective-permute-start | bytes 786440 | tf_op jit(solution)/shard_map/ppermute | solution.py:38
  278.1 19.3 %collective-permute-start.60 = (bf16[128,1024]{1,0:T(8,128)(2,1)S(1)}, bf16[128,1024]{1,0:T(8,128)(2,1)S(1)}, u32[]{:S(2)}, u32[]{:S(2)}) collective-permute-start(bf16[128,1024]{1,0:T(8,128)(2,1)S(1)} %get-tuple-element.353), channel_id=1, source_target_pairs={{0,8},{4,12},{8,0},{12,4},{1,9},{5,13},{9,1},{13,5},{2,10},{6,14},... | collective-permute-start | bytes 786440 | tf_op jit(solution)/shard_map/ppermute | solution.py:38
  279.1 18.3 %collective-permute-start.61 = (bf16[128,1024]{1,0:T(8,128)(2,1)S(1)}, bf16[128,1024]{1,0:T(8,128)(2,1)S(1)}, u32[]{:S(2)}, u32[]{:S(2)}) collective-permute-start(bf16[128,1024]{1,0:T(8,128)(2,1)S(1)} %get-tuple-element.354), channel_id=1, source_target_pairs={{0,12},{4,8},{8,4},{12,0},{1,13},{5,9},{9,5},{13,1},{2,14},{6,10},... | collective-permute-start | bytes 786440 | tf_op jit(solution)/shard_map/ppermute | solution.py:38
  280.5 1.4 collective-permute-start.56
  281.9 4.9 %collective-permute-start.57 = (f32[24,1024]{1,0:T(8,128)S(1)}, f32[24,1024]{1,0:T(8,128)S(1)}, u32[]{:S(2)}, u32[]{:S(2)}) collective-permute-start(f32[24,1024]{1,0:T(8,128)S(1)} %add.41), channel_id=1, source_target_pairs={{0,16},{16,0},{1,17},{17,1},{2,18},{18,2},{3,19},{19,3},{4,20},{20... | collective-permute-start | bytes 294920 | tf_op jit(solution)/shard_map/ppermute | solution.py:38
  286.9 5.6 %collective-permute-start.58 = (f32[8,1024]{1,0:T(8,128)S(1)}, f32[8,1024]{1,0:T(8,128)S(1)}, u32[]{:S(2)}, u32[]{:S(2)}) collective-permute-start(f32[8,1024]{1,0:T(8,128)S(1)} %slice.22), channel_id=1, source_target_pairs={{0,2},{1,3},{2,0},{3,1},{4,6},{5,7},{6,4},{7,5},{8,10},{9,11},{10,... | collective-permute-start | bytes 98312 | tf_op jit(solution)/shard_map/ppermute | solution.py:38
  (22 other events, 223.3 us)

commit v4 on v3

--- a/solution.py
+++ b/solution.py
@@ -597,7 +597,7 @@
                 acc[:, k : k + half] += contract(pre_grad, weight[:, here], 1, 1)
             return carry
 
-        lax.fori_loop(0, each // size, step, 0)
+        lax.fori_loop(0, each // size, step, 0, unroll=True)
     out_ref[...] = acc[...].astype(BF)
 
 

time: 300 us -> 300 us (level)
  transfers between devices with their start and end apart: 62 -> 62, of which waited for: 23 -> 23; matrix products, arithmetic and copies ran while one was open for 2% -> 2% of each run, Pallas kernels for 32% -> 31%
where the time goes in v4:
time: 300 us; the launch traced here: 299 us
  Pallas kernels  103 us (34%)
  starting transfers between devices  97.5 us (32%)
  waiting for transfers between devices  90.4 us (30%)
  local copies, waits for them, and re-layouts  3.64 us (1%)
    ppermute x62, starting transfers between devices, swap(): return lax.ppermute(value, axis, [(i, i ^ bit) for i in range(size)])  97.5 us
    ppermute x62, waiting for transfers between devices, swap(): return lax.ppermute(value, axis, [(i, i ^ bit) for i in range(size)])  90.4 us
    pallas_call x28, Pallas kernels, call(): pl.pallas_call(kernel, in_specs=[pl.BlockSpec(memory_space=pltpu.SMEM)] *...  80 us
    pallas_call x6, Pallas kernels, grid_call(): pl.pallas_call(kernel, grid_spec=pltpu.PrefetchScalarGridSpec(num_scalar_...  22.5 us
  transfers between devices with their start and end apart: 62, of which 23 were waited for; matrix products, arithmetic and copies ran while one was open for 2% of the time, Pallas kernels for 31%

profile of v4, /device:TPU:0, one launch (start us, length us, event | category | flops | bytes accessed | tf_op | source)
XLA Modules:
  0.0 299.0 jit_solution(828877829550118091)
XLA Ops:
  0.8 1.8 pack.1.a_ref.refs_4_
  2.5 3.0 %collective-permute-start.2 = (bf16[512,768]{1,0:T(8,128)(2,1)S(1)}, bf16[512,768]{1,0:T(8,128)(2,1)S(1)}, u32[]{:S(2)}, u32[]{:S(2)}) collective-permute-start(bf16[512,768]{1,0:T(8,128)(2,1)S(1)} %pack.1.a_ref.refs_4_), channel_id=1, source_target_pairs={{0,16},{16,0},{1,17},{17,1},{2,18},{18,2},{3,19},{19,3},{4,20},{20... | collective-permute-start | bytes 2359304 | tf_op jit(solution)/shard_map/ppermute | solution.py:38
  10.6 1.6 collective-permute-start
  12.2 2.0 collective-permute-done
  14.3 2.7 collective-permute-start.1
  16.9 4.1 %entry.1 = (bf16[256,1024]{1,0:T(8,128)(2,1)S(1)}, bf16[256,1024]{1,0:T(8,128)(2,1)S(1)}, f32[256,1024]{1,0:T(8,128)S(1)}, f32[256,1024]{1,0:T(8,128)S(1)}) custom-call(s32[4]{0:T(128)S(1)} %pad_add_fusion.place, bf16[256,4,1024]{2,1,0:T(4,128)(2,1)} %x_ref.2, f32[4,1024]{1,0:T(4,128)} %convolution_add_fusion.embed_ref), custom_call_target="tpu_custom_call" | custom-call | flops 41943040 | bytes 52592640 | tf_op jit(solution)/shard_map/entry/pallas_call | solution.py:80
  21.1 3.0 %pack_feed.1 = (bf16[512,256]{1,0:T(8,128)(2,1)S(1)}, bf16[512,2048]{1,0:T(8,128)(2,1)S(1)}) custom-call(s32[4]{0:T(128)S(1)} %pad_add_fusion.place, bf16[512,256]{1,0:T(8,128)(2,1)} %out_ref.1, bf16[512,1024]{1,0:T(8,128)(2,1)} %up_ref.1, bf16[512,1024]{1,0:T(8,128)(2,1)} %down_ref.1), custom_call_target="tpu_custom_call" | custom-call | bytes 47185 | tf_op jit(solution)/shard_map/pack_feed/pallas_call | solution.py:80
  26.4 2.4 project.2
  28.8 4.1 %collective-permute-done.18.refs_5_.b_ref = bf16[512,256]{1,0:T(8,128)(2,1)S(1)} collective-permute-done((bf16[512,256]{1,0:T(8,128)(2,1)S(1)}, bf16[512,256]{1,0:T(8,128)(2,1)S(1)}, u32[]{:S(2)}, u32[]{:S(2)}) %collective-permute-start.18) | collective-permute-done | bytes 262176 | tf_op jit(solution)/shard_map/ppermute | solution.py:38
  33.6 1.6 collective-permute-start.9
  35.1 2.6 collective-permute-start.10
  37.9 3.7 %own_rows.1 = (bf16[256,1024]{1,0:T(8,128)(2,1)S(1)}, bf16[256,1024]{1,0:T(8,128)(2,1)S(1)}) custom-call(s32[4]{0:T(128)S(1)} %pad_add_fusion.place, bf16[256,4,1024]{2,1,0:T(4,128)(2,1)} %x_ref.3), custom_call_target="tpu_custom_call" | custom-call | flops 20971520 | bytes 31457280 | tf_op jit(solution)/shard_map/own_rows/pallas_call | solution.py:80
  41.6 2.4 project.3
  44.7 3.5 %collective-permute-start.7 = (bf16[256,384]{1,0:T(8,128)(2,1)S(1)}, bf16[256,384]{1,0:T(8,128)(2,1)S(1)}, u32[]{:S(2)}, u32[]{:S(2)}) collective-permute-start(bf16[256,384]{1,0:T(8,128)(2,1)S(1)} %get-tuple-element.212), channel_id=1, source_target_pairs={{0,8},{4,12},{8,0},{12,4},{1,9},{5,13},{9,1},{13,5},{2,10},{6,14},... | collective-permute-start | bytes 589832 | tf_op jit(solution)/shard_map/ppermute | solution.py:38
  48.2 4.1 %collective-permute-done.10.refs_2_ = bf16[256,384]{1,0:T(8,128)(2,1)S(1)} collective-permute-done((bf16[256,384]{1,0:T(8,128)(2,1)S(1)}, bf16[256,384]{1,0:T(8,128)(2,1)S(1)}, u32[]{:S(2)}, u32[]{:S(2)}) %collective-permute-start.10) | collective-permute-done | bytes 196640 | tf_op jit(solution)/shard_map/ppermute | solution.py:38
  52.4 2.5 collective-permute-start.8
  54.9 3.7 %attend.2 = (bf16[256,128]{1,0:T(8,128)(2,1)S(1)}, bf16[256,128]{1,0:T(8,128)(2,1)S(1)}, bf16[256,128]{1,0:T(8,128)(2,1)S(1)}, bf16[256,128]{1,0:T(8,128)(2,1)S(1)}, f32[2,1024]{1,0:T(2,128)S(1)}) custom-call(bf16[256,384]{1,0:T(8,128)(2,1)S(1)} %get-tuple-element.219.refs_0_, bf16[256,384]{1,0:T(8,128)(2,1)S(1)} %collective-permute-done.9.refs_1_, ...), custom_call_target="tpu_custom_call" | custom-call | flops 2147483648 | bytes 1056768 | tf_op jit(solution)/shard_map/attend/pallas_call | solution.py:101
  58.6 10.7 %collective-permute-start.15 = (bf16[256,128]{1,0:T(8,128)(2,1)S(1)}, bf16[256,128]{1,0:T(8,128)(2,1)S(1)}, u32[]{:S(2)}, u32[]{:S(2)}) collective-permute-start(bf16[256,128]{1,0:T(8,128)(2,1)S(1)} %get-tuple-element.233), channel_id=1, source_target_pairs={{0,4},{4,0},{8,12},{12,8},{1,5},{5,1},{9,13},{13,9},{2,6},{6,2},{1... | collective-permute-start | bytes 196616 | tf_op jit(solution)/shard_map/ppermute | solution.py:38
  69.9 3.3 %collective-permute-start.16 = (bf16[256,128]{1,0:T(8,128)(2,1)S(1)}, bf16[256,128]{1,0:T(8,128)(2,1)S(1)}, u32[]{:S(2)}, u32[]{:S(2)}) collective-permute-start(bf16[256,128]{1,0:T(8,128)(2,1)S(1)} %get-tuple-element.234), channel_id=1, source_target_pairs={{0,8},{4,12},{8,0},{12,4},{1,9},{5,13},{9,1},{13,5},{2,10},{6,14},... | collective-permute-start | bytes 196616 | tf_op jit(solution)/shard_map/ppermute | solution.py:38
  74.5 3.7 %attend.3 = (bf16[256,128]{1,0:T(8,128)(2,1)S(1)}, bf16[256,128]{1,0:T(8,128)(2,1)S(1)}, bf16[256,128]{1,0:T(8,128)(2,1)S(1)}, bf16[256,128]{1,0:T(8,128)(2,1)S(1)}, f32[2,1024]{1,0:T(2,128)S(1)}) custom-call(bf16[256,384]{1,0:T(8,128)(2,1)S(1)} %get-tuple-element.224.refs_0_, bf16[256,384]{1,0:T(8,128)(2,1)S(1)} %collective-permute-done.6.refs_1_, ...), custom_call_target="tpu_custom_call" | custom-call | flops 2147483648 | bytes 1056768 | tf_op jit(solution)/shard_map/attend/pallas_call | solution.py:101
  80.4 1.6 collective-permute-start.21
  83.2 1.8 collective-permute-start.13
  86.2 3.2 %collective-permute-start.14 = (bf16[256,128]{1,0:T(8,128)(2,1)S(1)}, bf16[256,128]{1,0:T(8,128)(2,1)S(1)}, u32[]{:S(2)}, u32[]{:S(2)}) collective-permute-start(bf16[256,128]{1,0:T(8,128)(2,1)S(1)} %get-tuple-element.231), channel_id=1, source_target_pairs={{0,12},{4,8},{8,4},{12,0},{1,13},{5,9},{9,5},{13,1},{2,14},{6,10},... | collective-permute-start | bytes 196616 | tf_op jit(solution)/shard_map/ppermute | solution.py:38
  90.0 2.3 collective-permute-done.14.refs_3_
  95.2 5.0 %feed.2 = (f32[256,1024]{1,0:T(8,128)S(1)}, bf16[256,1024]{1,0:T(8,128)(2,1)S(1)}, bf16[256,2048]{1,0:T(8,128)(2,1)S(1)}, bf16[256,2048]{1,0:T(8,128)(2,1)S(1)}, bf16[256,1024]{1,0:T(8,128)(2,1)S(1)}) custom-call(f32[256,1024]{1,0:T(8,128)S(1)} %get-tuple-element.249.start_ref, bf16[256,1024]{1,0:T(8,128)(2,1)S(1)} %get-tuple-element.250.mine_ref, ...), custom_call_target="tpu_custom_call" | custom-call | flops 214748368 | bytes 1472512 | tf_op jit(solution)/shard_map/feed/pallas_call | solution.py:101
  100.2 1.6 collective-permute-start.26
  102.7 2.7 collective-permute-done.27
  105.4 2.8 collective-permute-done.25.theirs_ref
  108.2 5.2 %feed.3 = (f32[256,1024]{1,0:T(8,128)S(1)}, bf16[256,1024]{1,0:T(8,128)(2,1)S(1)}, bf16[256,2048]{1,0:T(8,128)(2,1)S(1)}, bf16[256,2048]{1,0:T(8,128)(2,1)S(1)}, bf16[256,1024]{1,0:T(8,128)(2,1)S(1)}) custom-call(f32[256,1024]{1,0:T(8,128)S(1)} %get-tuple-element.256.start_ref, bf16[256,1024]{1,0:T(8,128)(2,1)S(1)} %get-tuple-element.257.mine_ref, ...), custom_call_target="tpu_custom_call" | custom-call | flops 214748368 | bytes 1472512 | tf_op jit(solution)/shard_map/feed/pallas_call | solution.py:101
  114.1 5.4 %collective-permute-done.26.theirs_ref = bf16[256,1024]{1,0:T(8,128)(2,1)S(1)} collective-permute-done((bf16[256,1024]{1,0:T(8,128)(2,1)S(1)}, bf16[256,1024]{1,0:T(8,128)(2,1)S(1)}, u32[]{:S(2)}, u32[]{:S(2)}) %collective-permute-start.26) | collective-permute-done | bytes 524320 | tf_op jit(solution)/shard_map/ppermute | solution.py:38
  119.5 6.2 %feed_back.2 = (bf16[1,256,1024]{2,1,0:T(8,128)(2,1)S(1)}, f32[256,1024]{1,0:T(8,128)S(1)}, bf16[256,1024]{1,0:T(8,128)(2,1)S(1)}, bf16[256,2048]{1,0:T(8,128)(2...) custom-call(s32[4]{0:T(128)S(1)} %pad_add_fusion.place, ...), custom_call_target="tpu_custom_call" | custom-call | flops 6442450 | bytes 47529 | tf_op jit(solution)/shard_map/feed_back/pallas_call | solution.py:101
  126.3 4.4 %collective-permute-done.28.theirs_ref = bf16[256,1024]{1,0:T(8,128)(2,1)S(1)} collective-permute-done((bf16[256,1024]{1,0:T(8,128)(2,1)S(1)}, bf16[256,1024]{1,0:T(8,128)(2,1)S(1)}, u32[]{:S(2)}, u32[]{:S(2)}) %collective-permute-start.28) | collective-permute-done | bytes 524320 | tf_op jit(solution)/shard_map/ppermute | solution.py:38
  130.7 6.2 %feed_back.3 = (bf16[2,256,1024]{2,1,0:T(8,128)(2,1)S(1)}, f32[256,1024]{1,0:T(8,128)S(1)}, bf16[256,1024]{1,0:T(8,128)(2,1)S(1)}, bf16[256,2048]{1,0:T(8,128)(2...) custom-call(s32[4]{0:T(128)S(1)} %pad_add_fusion.place, ...), custom_call_target="tpu_custom_call" | custom-call | flops 6442450 | bytes 50577 | tf_op jit(solution)/shard_map/feed_back/pallas_call | solution.py:101
  136.9 2.7 collective-permute-done.29.theirs_ref
  139.6 2.4 split.2
  142.1 2.6 grad_core.2
  144.8 1.6 collective-permute-start.31
  147.8 1.8 collective-permute-start.36
  149.7 2.3 collective-permute-done.30.refs_8_
  151.9 2.6 collective-permute-start.37
  154.5 2.9 grad_shard.2
  157.4 1.7 collective-permute-done.31.theirs_ref
  159.8 2.5 split.3
  163.7 2.6 collective-permute-start.33
  166.7 7.2 %attend_back.2 = (bf16[256,384]{1,0:T(8,128)(2,1)S(1)}, bf16[256,384]{1,0:T(8,128)(2,1)S(1)}, bf16[256,384]{1,0:T(8,128)(2,1)S(1)}, bf16[256,384]{1,0:T(8,128)(2,1)S(1)}) custom-call(bf16[256,384]{1,0:T(8,128)(2,1)S(1)} %get-tuple-element.219.refs_0_, bf16[256,384]{1,0:T(8,128)(2,1)S(1)} %collective-permute-done.9.refs_1_, ...), custom_call_target="tpu_custom_call" | custom-call | flops 5368709120 | bytes 1843200 | tf_op jit(solution)/shard_map/attend_back/pallas_call | solution.py:101
  174.5 3.5 %collective-permute-start.43 = (bf16[256,384]{1,0:T(8,128)(2,1)S(1)}, bf16[256,384]{1,0:T(8,128)(2,1)S(1)}, u32[]{:S(2)}, u32[]{:S(2)}) collective-permute-start(bf16[256,384]{1,0:T(8,128)(2,1)S(1)} %get-tuple-element.307), channel_id=1, source_target_pairs={{0,8},{4,12},{8,0},{12,4},{1,9},{5,13},{9,1},{13,5},{2,10},{6,14},... | collective-permute-start | bytes 589832 | tf_op jit(solution)/shard_map/ppermute | solution.py:38
  178.4 7.0 %attend_back.3 = (bf16[256,384]{1,0:T(8,128)(2,1)S(1)}, bf16[256,384]{1,0:T(8,128)(2,1)S(1)}, bf16[256,384]{1,0:T(8,128)(2,1)S(1)}, bf16[256,384]{1,0:T(8,128)(2,1)S(1)}) custom-call(bf16[256,384]{1,0:T(8,128)(2,1)S(1)} %get-tuple-element.224.refs_0_, bf16[256,384]{1,0:T(8,128)(2,1)S(1)} %collective-permute-done.6.refs_1_, ...), custom_call_target="tpu_custom_call" | custom-call | flops 5368709120 | bytes 1843200 | tf_op jit(solution)/shard_map/attend_back/pallas_call | solution.py:101
  185.7 4.9 %leave.2 = bf16[256,4,1024]{2,1,0:T(4,128)(2,1)} custom-call(s32[4]{0:T(128)S(1)} %pad_add_fusion.place, bf16[2,256,1024]{2,1,0:T(8,128)(2,1)S(1)} %get-tuple-element.301.own_ref, bf16[2,256,1024]{2,1,0:T(8,128)(2,1)S(1)} %collective-permute-done.38.other_ref), custom_call_target="tpu_custom_call" | custom-call | flops 31457280 | bytes 125829120 | tf_op jit(solution)/shard_map/leave/pallas_call | solution.py:80
  190.7 3.8 %collective-permute-start.40 = (bf16[256,384]{1,0:T(8,128)(2,1)S(1)}, bf16[256,384]{1,0:T(8,128)(2,1)S(1)}, u32[]{:S(2)}, u32[]{:S(2)}) collective-permute-start(bf16[256,384]{1,0:T(8,128)(2,1)S(1)} %get-tuple-element.304), channel_id=1, source_target_pairs={{0,8},{4,12},{8,0},{12,4},{1,9},{5,13},{9,1},{13,5},{2,10},{6,14},... | collective-permute-start | bytes 589832 | tf_op jit(solution)/shard_map/ppermute | solution.py:38
  194.8 2.5 project_back.2
  198.8 9.1 %collective-permute-done.40.refs_2_ = bf16[256,384]{1,0:T(8,128)(2,1)S(1)} collective-permute-done((bf16[256,384]{1,0:T(8,128)(2,1)S(1)}, bf16[256,384]{1,0:T(8,128)(2,1)S(1)}, u32[]{:S(2)}, u32[]{:S(2)}) %collective-permute-start.40) | collective-permute-done | bytes 196640 | tf_op jit(solution)/shard_map/ppermute | solution.py:38
  207.9 1.7 project_back.3
  213.3 3.6 %grad_own.2 = (f32[128,2048]{1,0:T(8,128)S(1)}, bf16[128,2048]{1,0:T(8,128)(2,1)S(1)}, bf16[128,2048]{1,0:T(8,128)(2,1)S(1)}, bf16[128,2048]{1,0:T(8,128)(2,1)S(1)}) custom-call(s32[4]{0:T(128)S(1)} %pad_add_fusion.place, bf16[256,1024]{1,0:T(8,128)(2,1)S(1)} %copy-done.14, bf16[256,1024]{1,0:T(8,128)(2,1)S(1)} %copy-done.16, ...), custom_call_target="tpu_custom_call" | custom-call | flops 107374182400 | bytes 1520435200 | tf_op jit(solution)/shard_map/grad_own/pallas_call | solution.py:101
  219.8 3.5 %collective-permute-start.54 = (f32[24,1024]{1,0:T(8,128)S(1)}, f32[24,1024]{1,0:T(8,128)S(1)}, u32[]{:S(2)}, u32[]{:S(2)}) collective-permute-start(f32[24,1024]{1,0:T(8,128)S(1)} %tally.1), channel_id=1, source_target_pairs={{0,4},{4,0},{8,12},{12,8},{1,5},{5,1},{9,13},{13,9},{2,6},{6,2},{1... | collective-permute-start | bytes 294920 | tf_op jit(solution)/shard_map/ppermute | solution.py:38
  224.9 3.0 %collective-permute-start.47 = (bf16[128,2048]{1,0:T(8,128)(2,1)S(1)}, bf16[128,2048]{1,0:T(8,128)(2,1)S(1)}, u32[]{:S(2)}, u32[]{:S(2)}) collective-permute-start(bf16[128,2048]{1,0:T(8,128)(2,1)S(1)} %get-tuple-element.331), channel_id=1, source_target_pairs={{0,8},{4,12},{8,0},{12,4},{1,9},{5,13},{9,1},{13,5},{2,10},{6,14},... | collective-permute-start | bytes 1572872 | tf_op jit(solution)/shard_map/ppermute | solution.py:38
  229.3 6.5 %collective-permute-done.51.theirs_ref = bf16[256,1024]{1,0:T(8,128)(2,1)S(1)} collective-permute-done((bf16[256,1024]{1,0:T(8,128)(2,1)S(1)}, bf16[256,1024]{1,0:T(8,128)(2,1)S(1)}, u32[]{:S(2)}, u32[]{:S(2)}) %collective-permute-start.51) | collective-permute-done | bytes 524320 | tf_op jit(solution)/shard_map/ppermute | solution.py:38
  237.2 10.2 %collective-permute-done.46.refs_1_ = bf16[128,2048]{1,0:T(8,128)(2,1)S(1)} collective-permute-done((bf16[128,2048]{1,0:T(8,128)(2,1)S(1)}, bf16[128,2048]{1,0:T(8,128)(2,1)S(1)}, u32[]{:S(2)}, u32[]{:S(2)}) %collective-permute-start.46) | collective-permute-done | bytes 524320 | tf_op jit(solution)/shard_map/ppermute | solution.py:38
  247.5 17.8 %collective-permute-done.47.refs_2_ = bf16[128,2048]{1,0:T(8,128)(2,1)S(1)} collective-permute-done((bf16[128,2048]{1,0:T(8,128)(2,1)S(1)}, bf16[128,2048]{1,0:T(8,128)(2,1)S(1)}, u32[]{:S(2)}, u32[]{:S(2)}) %collective-permute-start.47) | collective-permute-done | bytes 524320 | tf_op jit(solution)/shard_map/ppermute | solution.py:38
  266.4 1.6 grad_own.3
  268.1 10.2 %collective-permute-start.59 = (bf16[128,1024]{1,0:T(8,128)(2,1)S(1)}, bf16[128,1024]{1,0:T(8,128)(2,1)S(1)}, u32[]{:S(2)}, u32[]{:S(2)}) collective-permute-start(bf16[128,1024]{1,0:T(8,128)(2,1)S(1)} %get-tuple-element.352), channel_id=1, source_target_pairs={{0,4},{4,0},{8,12},{12,8},{1,5},{5,1},{9,13},{13,9},{2,6},{6,2},{1... | collective-permute-start | bytes 786440 | tf_op jit(solution)/shard_map/ppermute | solution.py:38
  283.7 3.3 %collective-permute-done.57 = f32[24,1024]{1,0:T(8,128)S(1)} collective-permute-done((f32[24,1024]{1,0:T(8,128)S(1)}, f32[24,1024]{1,0:T(8,128)S(1)}, u32[]{:S(2)}, u32[]{:S(2)}) %collective-permute-start.57) | collective-permute-done | bytes 98336 | tf_op jit(solution)/shard_map/ppermute | solution.py:38
  287.7 5.0 %leave.3 = f32[256,4,1024]{2,1,0:T(4,128)} custom-call(s32[4]{0:T(128)S(1)} %pad_add_fusion.place, f32[2,256,1024]{2,1,0:T(8,128)S(1)} %last.3.own_ref, f32[2,256,1024]{2,1,0:T(8,128)S(1)} %collective-permute-done.53.other_ref), custom_call_target="tpu_custom_call" | custom-call | flops 31457280 | bytes 251658240 | tf_op jit(solution)/shard_map/leave/pallas_call | solution.py:80
  292.7 2.6 finish.1
  295.3 2.3 collective-permute-done.60.refs_2_
  (163 shorter events, 47.8 us)
Async XLA Ops:
  2.5 21.5 %collective-permute-start.2 = (bf16[512,768]{1,0:T(8,128)(2,1)S(1)}, bf16[512,768]{1,0:T(8,128)(2,1)S(1)}, u32[]{:S(2)}, u32[]{:S(2)}) collective-permute-start(bf16[512,768]{1,0:T(8,128)(2,1)S(1)} %pack.1.a_ref.refs_4_), channel_id=1, source_target_pairs={{0,16},{16,0},{1,17},{17,1},{2,18},{18,2},{3,19},{19,3},{4,20},{20... | collective-permute-start | bytes 2359304 | tf_op jit(solution)/shard_map/ppermute | solution.py:38
  10.6 3.7 %collective-permute-start = (f32[8,128]{1,0:T(8,128)S(1)}, f32[8,128]{1,0:T(8,128)S(1)}, u32[]{:S(2)}, u32[]{:S(2)}) collective-permute-start(f32[8,128]{1,0:T(8,128)S(1)} %broadcast_in_dim.10), channel_id=1, source_target_pairs={{0,4},{4,0},{8,12},{12,8},{1,5},{5,1},{9,13},{13,9},{2,6},{6,2},{1... | collective-permute-start | bytes 12296 | tf_op jit(solution)/shard_map/ppermute | solution.py:38
  12.2 14.2 %collective-permute-start.3 = (bf16[512,768]{1,0:T(8,128)(2,1)S(1)}, bf16[512,768]{1,0:T(8,128)(2,1)S(1)}, u32[]{:S(2)}, u32[]{:S(2)}) collective-permute-start(bf16[512,768]{1,0:T(8,128)(2,1)S(1)} %pack.1.a_ref.refs_4_), channel_id=1, source_target_pairs={{0,1},{1,0},{2,3},{3,2},{4,5},{5,4},{6,7},{7,6},{8,9},{9,8},{10,11... | collective-permute-start | bytes 2359304 | tf_op jit(solution)/shard_map/ppermute | solution.py:38
  14.3 6.8 %collective-permute-start.1 = (f32[8,128]{1,0:T(8,128)S(1)}, f32[8,128]{1,0:T(8,128)S(1)}, u32[]{:S(2)}, u32[]{:S(2)}) collective-permute-start(f32[8,128]{1,0:T(8,128)S(1)} %add.36), channel_id=1, source_target_pairs={{0,8},{4,12},{8,0},{12,4},{1,9},{5,13},{9,1},{13,5},{2,10},{6,14},... | collective-permute-start | bytes 12296 | tf_op jit(solution)/shard_map/ppermute | solution.py:38
  24.1 2.4 collective-permute-start.4
  24.2 8.7 %collective-permute-start.18 = (bf16[512,256]{1,0:T(8,128)(2,1)S(1)}, bf16[512,256]{1,0:T(8,128)(2,1)S(1)}, u32[]{:S(2)}, u32[]{:S(2)}) collective-permute-start(bf16[512,256]{1,0:T(8,128)(2,1)S(1)} %get-tuple-element.241.refs_4_.a_ref), channel_id=1, source_target_pairs={{0,16},{16,0},{1,17},{17,1},{2,18},{18,2},{3,19},{19,3},{4,20},{20... | collective-permute-start | bytes 786440 | tf_op jit(solution)/shard_map/ppermute | solution.py:38
  24.9 1.6 collective-permute-start.5
  32.9 47.4 %collective-permute-start.22 = (bf16[512,2048]{1,0:T(8,128)(2,1)S(1)}, bf16[512,2048]{1,0:T(8,128)(2,1)S(1)}, u32[]{:S(2)}, u32[]{:S(2)}) collective-permute-start(bf16[512,2048]{1,0:T(8,128)(2,1)S(1)} %get-tuple-element.251.a_ref), channel_id=1, source_target_pairs={{0,16},{16,0},{1,17},{17,1},{2,18},{18,2},{3,19},{19,3},{4,20},{20... | collective-permute-start | bytes 6291464 | tf_op jit(solution)/shard_map/ppermute | solution.py:38
  33.6 11.2 %collective-permute-start.9 = (bf16[256,384]{1,0:T(8,128)(2,1)S(1)}, bf16[256,384]{1,0:T(8,128)(2,1)S(1)}, u32[]{:S(2)}, u32[]{:S(2)}) collective-permute-start(bf16[256,384]{1,0:T(8,128)(2,1)S(1)} %get-tuple-element.216), channel_id=1, source_target_pairs={{0,4},{4,0},{8,12},{12,8},{1,5},{5,1},{9,13},{13,9},{2,6},{6,2},{1... | collective-permute-start | bytes 589832 | tf_op jit(solution)/shard_map/ppermute | solution.py:38
  35.1 17.2 %collective-permute-start.10 = (bf16[256,384]{1,0:T(8,128)(2,1)S(1)}, bf16[256,384]{1,0:T(8,128)(2,1)S(1)}, u32[]{:S(2)}, u32[]{:S(2)}) collective-permute-start(bf16[256,384]{1,0:T(8,128)(2,1)S(1)} %get-tuple-element.217), channel_id=1, source_target_pairs={{0,8},{4,12},{8,0},{12,4},{1,9},{5,13},{9,1},{13,5},{2,10},{6,14},... | collective-permute-start | bytes 589832 | tf_op jit(solution)/shard_map/ppermute | solution.py:38
  37.7 17.2 %collective-permute-start.11 = (bf16[256,384]{1,0:T(8,128)(2,1)S(1)}, bf16[256,384]{1,0:T(8,128)(2,1)S(1)}, u32[]{:S(2)}, u32[]{:S(2)}) collective-permute-start(bf16[256,384]{1,0:T(8,128)(2,1)S(1)} %get-tuple-element.218), channel_id=1, source_target_pairs={{0,12},{4,8},{8,4},{12,0},{1,13},{5,9},{9,5},{13,1},{2,14},{6,10},... | collective-permute-start | bytes 589832 | tf_op jit(solution)/shard_map/ppermute | solution.py:38
  44.0 25.4 %collective-permute-start.6 = (bf16[256,384]{1,0:T(8,128)(2,1)S(1)}, bf16[256,384]{1,0:T(8,128)(2,1)S(1)}, u32[]{:S(2)}, u32[]{:S(2)}) collective-permute-start(bf16[256,384]{1,0:T(8,128)(2,1)S(1)} %get-tuple-element.211), channel_id=1, source_target_pairs={{0,4},{4,0},{8,12},{12,8},{1,5},{5,1},{9,13},{13,9},{2,6},{6,2},{1... | collective-permute-start | bytes 589832 | tf_op jit(solution)/shard_map/ppermute | solution.py:38
  44.7 24.6 %collective-permute-start.7 = (bf16[256,384]{1,0:T(8,128)(2,1)S(1)}, bf16[256,384]{1,0:T(8,128)(2,1)S(1)}, u32[]{:S(2)}, u32[]{:S(2)}) collective-permute-start(bf16[256,384]{1,0:T(8,128)(2,1)S(1)} %get-tuple-element.212), channel_id=1, source_target_pairs={{0,8},{4,12},{8,0},{12,4},{1,9},{5,13},{9,1},{13,5},{2,10},{6,14},... | collective-permute-start | bytes 589832 | tf_op jit(solution)/shard_map/ppermute | solution.py:38
  52.4 17.5 %collective-permute-start.8 = (bf16[256,384]{1,0:T(8,128)(2,1)S(1)}, bf16[256,384]{1,0:T(8,128)(2,1)S(1)}, u32[]{:S(2)}, u32[]{:S(2)}) collective-permute-start(bf16[256,384]{1,0:T(8,128)(2,1)S(1)} %get-tuple-element.213), channel_id=1, source_target_pairs={{0,12},{4,8},{8,4},{12,0},{1,13},{5,9},{9,5},{13,1},{2,14},{6,10},... | collective-permute-start | bytes 589832 | tf_op jit(solution)/shard_map/ppermute | solution.py:38
  58.6 14.5 %collective-permute-start.15 = (bf16[256,128]{1,0:T(8,128)(2,1)S(1)}, bf16[256,128]{1,0:T(8,128)(2,1)S(1)}, u32[]{:S(2)}, u32[]{:S(2)}) collective-permute-start(bf16[256,128]{1,0:T(8,128)(2,1)S(1)} %get-tuple-element.233), channel_id=1, source_target_pairs={{0,4},{4,0},{8,12},{12,8},{1,5},{5,1},{9,13},{13,9},{2,6},{6,2},{1... | collective-permute-start | bytes 196616 | tf_op jit(solution)/shard_map/ppermute | solution.py:38
  69.4 9.9 %collective-permute-start.19 = (bf16[512,256]{1,0:T(8,128)(2,1)S(1)}, bf16[512,256]{1,0:T(8,128)(2,1)S(1)}, u32[]{:S(2)}, u32[]{:S(2)}) collective-permute-start(bf16[512,256]{1,0:T(8,128)(2,1)S(1)} %get-tuple-element.241.refs_4_.a_ref), channel_id=1, source_target_pairs={{0,1},{1,0},{2,3},{3,2},{4,5},{5,4},{6,7},{7,6},{8,9},{9,8},{10,11... | collective-permute-start | bytes 786440 | tf_op jit(solution)/shard_map/ppermute | solution.py:38
  69.4 9.9 %collective-permute-start.20 = (bf16[512,256]{1,0:T(8,128)(2,1)S(1)}, bf16[512,256]{1,0:T(8,128)(2,1)S(1)}, u32[]{:S(2)}, u32[]{:S(2)}) collective-permute-start(bf16[512,256]{1,0:T(8,128)(2,1)S(1)} %collective-permute-done.18.refs_5_.b_ref), channel_id=1, source_target_pairs={{0,1},{1,0},{2,3},{3,2},{4,5},{5,4},{6,7},{7,6},{8,9},{9,8},{10,11... | collective-permute-start | bytes 786440 | tf_op jit(solution)/shard_map/ppermute | solution.py:38
  69.9 8.4 %collective-permute-start.16 = (bf16[256,128]{1,0:T(8,128)(2,1)S(1)}, bf16[256,128]{1,0:T(8,128)(2,1)S(1)}, u32[]{:S(2)}, u32[]{:S(2)}) collective-permute-start(bf16[256,128]{1,0:T(8,128)(2,1)S(1)} %get-tuple-element.234), channel_id=1, source_target_pairs={{0,8},{4,12},{8,0},{12,4},{1,9},{5,13},{9,1},{13,5},{2,10},{6,14},... | collective-permute-start | bytes 196616 | tf_op jit(solution)/shard_map/ppermute | solution.py:38
  73.2 6.1 %collective-permute-start.17 = (bf16[256,128]{1,0:T(8,128)(2,1)S(1)}, bf16[256,128]{1,0:T(8,128)(2,1)S(1)}, u32[]{:S(2)}, u32[]{:S(2)}) collective-permute-start(bf16[256,128]{1,0:T(8,128)(2,1)S(1)} %get-tuple-element.235), channel_id=1, source_target_pairs={{0,12},{4,8},{8,4},{12,0},{1,13},{5,9},{9,5},{13,1},{2,14},{6,10},... | collective-permute-start | bytes 196616 | tf_op jit(solution)/shard_map/ppermute | solution.py:38
  78.3 15.6 %collective-permute-start.23 = (bf16[512,2048]{1,0:T(8,128)(2,1)S(1)}, bf16[512,2048]{1,0:T(8,128)(2,1)S(1)}, u32[]{:S(2)}, u32[]{:S(2)}) collective-permute-start(bf16[512,2048]{1,0:T(8,128)(2,1)S(1)} %get-tuple-element.251.a_ref), channel_id=1, source_target_pairs={{0,1},{1,0},{2,3},{3,2},{4,5},{5,4},{6,7},{7,6},{8,9},{9,8},{10,11... | collective-permute-start | bytes 6291464 | tf_op jit(solution)/shard_map/ppermute | solution.py:38
  80.3 14.9 %collective-permute-start.24 = (bf16[512,2048]{1,0:T(8,128)(2,1)S(1)}, bf16[512,2048]{1,0:T(8,128)(2,1)S(1)}, u32[]{:S(2)}, u32[]{:S(2)}) collective-permute-start(bf16[512,2048]{1,0:T(8,128)(2,1)S(1)} %collective-permute-done.22.b_ref), channel_id=1, source_target_pairs={{0,1},{1,0},{2,3},{3,2},{4,5},{5,4},{6,7},{7,6},{8,9},{9,8},{10,11... | collective-permute-start | bytes 6291464 | tf_op jit(solution)/shard_map/ppermute | solution.py:38
  80.4 14.8 %collective-permute-start.21 = (bf16[256,1024]{1,0:T(8,128)(2,1)S(1)}, bf16[256,1024]{1,0:T(8,128)(2,1)S(1)}, u32[]{:S(2)}, u32[]{:S(2)}) collective-permute-start(bf16[256,1024]{1,0:T(8,128)(2,1)S(1)} %get-tuple-element.250.mine_ref), channel_id=1, source_target_pairs={{0,2},{1,3},{2,0},{3,1},{4,6},{5,7},{6,4},{7,5},{8,10},{9,11},{10,... | collective-permute-start | bytes 1572872 | tf_op jit(solution)/shard_map/ppermute | solution.py:38
  81.9 4.3 %collective-permute-start.12 = (bf16[256,128]{1,0:T(8,128)(2,1)S(1)}, bf16[256,128]{1,0:T(8,128)(2,1)S(1)}, u32[]{:S(2)}, u32[]{:S(2)}) collective-permute-start(bf16[256,128]{1,0:T(8,128)(2,1)S(1)} %get-tuple-element.229), channel_id=1, source_target_pairs={{0,4},{4,0},{8,12},{12,8},{1,5},{5,1},{9,13},{13,9},{2,6},{6,2},{1... | collective-permute-start | bytes 196616 | tf_op jit(solution)/shard_map/ppermute | solution.py:38
  83.2 6.8 %collective-permute-start.13 = (bf16[256,128]{1,0:T(8,128)(2,1)S(1)}, bf16[256,128]{1,0:T(8,128)(2,1)S(1)}, u32[]{:S(2)}, u32[]{:S(2)}) collective-permute-start(bf16[256,128]{1,0:T(8,128)(2,1)S(1)} %get-tuple-element.230), channel_id=1, source_target_pairs={{0,8},{4,12},{8,0},{12,4},{1,9},{5,13},{9,1},{13,5},{2,10},{6,14},... | collective-permute-start | bytes 196616 | tf_op jit(solution)/shard_map/ppermute | solution.py:38
  86.2 6.1 %collective-permute-start.14 = (bf16[256,128]{1,0:T(8,128)(2,1)S(1)}, bf16[256,128]{1,0:T(8,128)(2,1)S(1)}, u32[]{:S(2)}, u32[]{:S(2)}) collective-permute-start(bf16[256,128]{1,0:T(8,128)(2,1)S(1)} %get-tuple-element.231), channel_id=1, source_target_pairs={{0,12},{4,8},{8,4},{12,0},{1,13},{5,9},{9,5},{13,1},{2,14},{6,10},... | collective-permute-start | bytes 196616 | tf_op jit(solution)/shard_map/ppermute | solution.py:38
  93.3 14.9 %collective-permute-start.25 = (bf16[256,1024]{1,0:T(8,128)(2,1)S(1)}, bf16[256,1024]{1,0:T(8,128)(2,1)S(1)}, u32[]{:S(2)}, u32[]{:S(2)}) collective-permute-start(bf16[256,1024]{1,0:T(8,128)(2,1)S(1)} %get-tuple-element.257.mine_ref), channel_id=1, source_target_pairs={{0,2},{1,3},{2,0},{3,1},{4,6},{5,7},{6,4},{7,5},{8,10},{9,11},{10,... | collective-permute-start | bytes 1572872 | tf_op jit(solution)/shard_map/ppermute | solution.py:38
  100.2 54.3 %copy-start.13 = (bf16[256,1024]{1,0:T(8,128)(2,1)}, bf16[256,1024]{1,0:T(8,128)(2,1)S(1)}, u32[]{:S(2)}) copy-start(bf16[256,1024]{1,0:T(8,128)(2,1)S(1)} %get-tuple-element.328.refs_0_) | copy-start | bytes 1572868
  100.2 19.2 %collective-permute-start.26 = (bf16[256,1024]{1,0:T(8,128)(2,1)S(1)}, bf16[256,1024]{1,0:T(8,128)(2,1)S(1)}, u32[]{:S(2)}, u32[]{:S(2)}) collective-permute-start(bf16[256,1024]{1,0:T(8,128)(2,1)S(1)} %get-tuple-element.260.mine_ref), channel_id=1, source_target_pairs={{0,2},{1,3},{2,0},{3,1},{4,6},{5,7},{6,4},{7,5},{8,10},{9,11},{10,... | collective-permute-start | bytes 1572872 | tf_op jit(solution)/shard_map/ppermute | solution.py:38
  101.8 3.6 %collective-permute-start.27 = (f32[8,128]{1,0:T(8,128)S(1)}, f32[8,128]{1,0:T(8,128)S(1)}, u32[]{:S(2)}, u32[]{:S(2)}) collective-permute-start(f32[8,128]{1,0:T(8,128)S(1)} %add.37), channel_id=1, source_target_pairs={{0,16},{16,0},{1,17},{17,1},{2,18},{18,2},{3,19},{19,3},{4,20},{20... | collective-permute-start | bytes 12296 | tf_op jit(solution)/shard_map/ppermute | solution.py:38
  113.5 41.0 %copy-start.11 = (bf16[256,2048]{1,0:T(8,128)(2,1)}, bf16[256,2048]{1,0:T(8,128)(2,1)S(1)}, u32[]{:S(2)}) copy-start(bf16[256,2048]{1,0:T(8,128)(2,1)S(1)} %get-tuple-element.283.refs_7_) | copy-start | bytes 3145732
  113.5 17.2 %collective-permute-start.28 = (bf16[256,1024]{1,0:T(8,128)(2,1)S(1)}, bf16[256,1024]{1,0:T(8,128)(2,1)S(1)}, u32[]{:S(2)}, u32[]{:S(2)}) collective-permute-start(bf16[256,1024]{1,0:T(8,128)(2,1)S(1)} %get-tuple-element.268.mine_ref), channel_id=1, source_target_pairs={{0,2},{1,3},{2,0},{3,1},{4,6},{5,7},{6,4},{7,5},{8,10},{9,11},{10,... | collective-permute-start | bytes 1572872 | tf_op jit(solution)/shard_map/ppermute | solution.py:38
  125.7 14.0 %collective-permute-start.29 = (bf16[256,1024]{1,0:T(8,128)(2,1)S(1)}, bf16[256,1024]{1,0:T(8,128)(2,1)S(1)}, u32[]{:S(2)}, u32[]{:S(2)}) collective-permute-start(bf16[256,1024]{1,0:T(8,128)(2,1)S(1)} %get-tuple-element.275.mine_ref), channel_id=1, source_target_pairs={{0,2},{1,3},{2,0},{3,1},{4,6},{5,7},{6,4},{7,5},{8,10},{9,11},{10,... | collective-permute-start | bytes 1572872 | tf_op jit(solution)/shard_map/ppermute | solution.py:38
  144.7 7.2 %collective-permute-start.30 = (bf16[1024,2048]{1,0:T(8,128)(2,1)S(1)}, bf16[1024,2048]{1,0:T(8,128)(2,1)S(1)}, u32[]{:S(2)}, u32[]{:S(2)}) collective-permute-start(bf16[1024,2048]{1,0:T(8,128)(2,1)S(1)} %grad_core.2), channel_id=1, source_target_pairs={{0,1},{1,0},{2,3},{3,2},{4,5},{5,4},{6,7},{7,6},{8,9},{9,8},{10,11... | collective-permute-start | bytes 12582920 | tf_op jit(solution)/shard_map/ppermute | solution.py:38
  144.8 14.3 %collective-permute-start.31 = (bf16[256,1024]{1,0:T(8,128)(2,1)S(1)}, bf16[256,1024]{1,0:T(8,128)(2,1)S(1)}, u32[]{:S(2)}, u32[]{:S(2)}) collective-permute-start(bf16[256,1024]{1,0:T(8,128)(2,1)S(1)} %get-tuple-element.286.mine_ref), channel_id=1, source_target_pairs={{0,2},{1,3},{2,0},{3,1},{4,6},{5,7},{6,4},{7,5},{8,10},{9,11},{10,... | collective-permute-start | bytes 1572872 | tf_op jit(solution)/shard_map/ppermute | solution.py:38
  146.4 39.0 %collective-permute-start.38 = (bf16[2,256,1024]{2,1,0:T(8,128)(2,1)S(1)}, bf16[2,256,1024]{2,1,0:T(8,128)(2,1)S(1)}, u32[]{:S(2)}, u32[]{:S(2)}) collective-permute-start(bf16[2,256,1024]{2,1,0:T(8,128)(2,1)S(1)} %get-tuple-element.301.own_ref), channel_id=1, source_target_pairs={{0,1},{1,0},{2,3},{3,2},{4,5},{5,4},{6,7},{7,6},{8,9},{9,8},{10,11... | collective-permute-start | bytes 3145736 | tf_op jit(solution)/shard_map/ppermute | solution.py:38
  146.6 15.7 %collective-permute-start.35 = (bf16[256,128]{1,0:T(8,128)(2,1)S(1)}, bf16[256,128]{1,0:T(8,128)(2,1)S(1)}, u32[]{:S(2)}, u32[]{:S(2)}) collective-permute-start(bf16[256,128]{1,0:T(8,128)(2,1)S(1)} %get-tuple-element.292), channel_id=1, source_target_pairs={{0,4},{4,0},{8,12},{12,8},{1,5},{5,1},{9,13},{13,9},{2,6},{6,2},{1... | collective-permute-start | bytes 196616 | tf_op jit(solution)/shard_map/ppermute | solution.py:38
  147.8 15.9 %collective-permute-start.36 = (bf16[256,128]{1,0:T(8,128)(2,1)S(1)}, bf16[256,128]{1,0:T(8,128)(2,1)S(1)}, u32[]{:S(2)}, u32[]{:S(2)}) collective-permute-start(bf16[256,128]{1,0:T(8,128)(2,1)S(1)} %get-tuple-element.293), channel_id=1, source_target_pairs={{0,8},{4,12},{8,0},{12,4},{1,9},{5,13},{9,1},{13,5},{2,10},{6,14},... | collective-permute-start | bytes 196616 | tf_op jit(solution)/shard_map/ppermute | solution.py:38
  151.9 14.4 %collective-permute-start.37 = (bf16[256,128]{1,0:T(8,128)(2,1)S(1)}, bf16[256,128]{1,0:T(8,128)(2,1)S(1)}, u32[]{:S(2)}, u32[]{:S(2)}) collective-permute-start(bf16[256,128]{1,0:T(8,128)(2,1)S(1)} %get-tuple-element.294), channel_id=1, source_target_pairs={{0,12},{4,8},{8,4},{12,0},{1,13},{5,9},{9,5},{13,1},{2,14},{6,10},... | collective-permute-start | bytes 196616 | tf_op jit(solution)/shard_map/ppermute | solution.py:38
  159.1 52.7 %collective-permute-start.45 = (bf16[512,2048]{1,0:T(8,128)(2,1)}, bf16[512,2048]{1,0:T(8,128)(2,1)}, u32[]{:S(2)}, u32[]{:S(2)}) collective-permute-start(bf16[512,2048]{1,0:T(8,128)(2,1)} %grad_shard.2), channel_id=1, source_target_pairs={{0,16},{16,0},{1,17},{17,1},{2,18},{18,2},{3,19},{19,3},{4,20},{20... | collective-permute-start | bytes 6291464 | tf_op jit(solution)/shard_map/ppermute | solution.py:38
  162.2 11.7 %collective-permute-start.32 = (bf16[256,128]{1,0:T(8,128)(2,1)S(1)}, bf16[256,128]{1,0:T(8,128)(2,1)S(1)}, u32[]{:S(2)}, u32[]{:S(2)}) collective-permute-start(bf16[256,128]{1,0:T(8,128)(2,1)S(1)} %get-tuple-element.288), channel_id=1, source_target_pairs={{0,4},{4,0},{8,12},{12,8},{1,5},{5,1},{9,13},{13,9},{2,6},{6,2},{1... | collective-permute-start | bytes 196616 | tf_op jit(solution)/shard_map/ppermute | solution.py:38
  163.7 10.8 %collective-permute-start.33 = (bf16[256,128]{1,0:T(8,128)(2,1)S(1)}, bf16[256,128]{1,0:T(8,128)(2,1)S(1)}, u32[]{:S(2)}, u32[]{:S(2)}) collective-permute-start(bf16[256,128]{1,0:T(8,128)(2,1)S(1)} %get-tuple-element.289), channel_id=1, source_target_pairs={{0,8},{4,12},{8,0},{12,4},{1,9},{5,13},{9,1},{13,5},{2,10},{6,14},... | collective-permute-start | bytes 196616 | tf_op jit(solution)/shard_map/ppermute | solution.py:38
  166.3 11.7 %collective-permute-start.34 = (bf16[256,128]{1,0:T(8,128)(2,1)S(1)}, bf16[256,128]{1,0:T(8,128)(2,1)S(1)}, u32[]{:S(2)}, u32[]{:S(2)}) collective-permute-start(bf16[256,128]{1,0:T(8,128)(2,1)S(1)} %get-tuple-element.290), channel_id=1, source_target_pairs={{0,12},{4,8},{8,4},{12,0},{1,13},{5,9},{9,5},{13,1},{2,14},{6,10},... | collective-permute-start | bytes 196616 | tf_op jit(solution)/shard_map/ppermute | solution.py:38
  173.9 16.7 %collective-permute-start.42 = (bf16[256,384]{1,0:T(8,128)(2,1)S(1)}, bf16[256,384]{1,0:T(8,128)(2,1)S(1)}, u32[]{:S(2)}, u32[]{:S(2)}) collective-permute-start(bf16[256,384]{1,0:T(8,128)(2,1)S(1)} %get-tuple-element.306), channel_id=1, source_target_pairs={{0,4},{4,0},{8,12},{12,8},{1,5},{5,1},{9,13},{13,9},{2,6},{6,2},{1... | collective-permute-start | bytes 589832 | tf_op jit(solution)/shard_map/ppermute | solution.py:38
  174.5 19.9 %collective-permute-start.43 = (bf16[256,384]{1,0:T(8,128)(2,1)S(1)}, bf16[256,384]{1,0:T(8,128)(2,1)S(1)}, u32[]{:S(2)}, u32[]{:S(2)}) collective-permute-start(bf16[256,384]{1,0:T(8,128)(2,1)S(1)} %get-tuple-element.307), channel_id=1, source_target_pairs={{0,8},{4,12},{8,0},{12,4},{1,9},{5,13},{9,1},{13,5},{2,10},{6,14},... | collective-permute-start | bytes 589832 | tf_op jit(solution)/shard_map/ppermute | solution.py:38
  178.0 16.8 %collective-permute-start.44 = (bf16[256,384]{1,0:T(8,128)(2,1)S(1)}, bf16[256,384]{1,0:T(8,128)(2,1)S(1)}, u32[]{:S(2)}, u32[]{:S(2)}) collective-permute-start(bf16[256,384]{1,0:T(8,128)(2,1)S(1)} %get-tuple-element.308), channel_id=1, source_target_pairs={{0,12},{4,8},{8,4},{12,0},{1,13},{5,9},{9,5},{13,1},{2,14},{6,10},... | collective-permute-start | bytes 589832 | tf_op jit(solution)/shard_map/ppermute | solution.py:38
  185.4 13.4 %collective-permute-start.39 = (bf16[256,384]{1,0:T(8,128)(2,1)S(1)}, bf16[256,384]{1,0:T(8,128)(2,1)S(1)}, u32[]{:S(2)}, u32[]{:S(2)}) collective-permute-start(bf16[256,384]{1,0:T(8,128)(2,1)S(1)} %get-tuple-element.303), channel_id=1, source_target_pairs={{0,4},{4,0},{8,12},{12,8},{1,5},{5,1},{9,13},{13,9},{2,6},{6,2},{1... | collective-permute-start | bytes 589832 | tf_op jit(solution)/shard_map/ppermute | solution.py:38
  190.7 17.2 %collective-permute-start.40 = (bf16[256,384]{1,0:T(8,128)(2,1)S(1)}, bf16[256,384]{1,0:T(8,128)(2,1)S(1)}, u32[]{:S(2)}, u32[]{:S(2)}) collective-permute-start(bf16[256,384]{1,0:T(8,128)(2,1)S(1)} %get-tuple-element.304), channel_id=1, source_target_pairs={{0,8},{4,12},{8,0},{12,4},{1,9},{5,13},{9,1},{13,5},{2,10},{6,14},... | collective-permute-start | bytes 589832 | tf_op jit(solution)/shard_map/ppermute | solution.py:38
  194.4 13.5 %collective-permute-start.41 = (bf16[256,384]{1,0:T(8,128)(2,1)S(1)}, bf16[256,384]{1,0:T(8,128)(2,1)S(1)}, u32[]{:S(2)}, u32[]{:S(2)}) collective-permute-start(bf16[256,384]{1,0:T(8,128)(2,1)S(1)} %get-tuple-element.305), channel_id=1, source_target_pairs={{0,12},{4,8},{8,4},{12,0},{1,13},{5,9},{9,5},{13,1},{2,14},{6,10},... | collective-permute-start | bytes 589832 | tf_op jit(solution)/shard_map/ppermute | solution.py:38
  197.3 19.6 %collective-permute-start.49 = (bf16[256,1024]{1,0:T(8,128)(2,1)}, bf16[256,1024]{1,0:T(8,128)(2,1)}, u32[]{:S(2)}, u32[]{:S(2)}) collective-permute-start(bf16[256,1024]{1,0:T(8,128)(2,1)} %get-tuple-element.335.mine_ref), channel_id=1, source_target_pairs={{0,2},{1,3},{2,0},{3,1},{4,6},{5,7},{6,4},{7,5},{8,10},{9,11},{10,... | collective-permute-start | bytes 1572872 | tf_op jit(solution)/shard_map/ppermute | solution.py:38
  211.8 6.5 %collective-permute-start.50 = (bf16[1024,1024]{1,0:T(8,128)(2,1)S(1)}, bf16[1024,1024]{1,0:T(8,128)(2,1)S(1)}, u32[]{:S(2)}, u32[]{:S(2)}) collective-permute-start(bf16[1024,1024]{1,0:T(8,128)(2,1)S(1)} %grad_core.3), channel_id=1, source_target_pairs={{0,1},{1,0},{2,3},{3,2},{4,5},{5,4},{6,7},{7,6},{8,9},{9,8},{10,11... | collective-permute-start | bytes 6291464 | tf_op jit(solution)/shard_map/ppermute | solution.py:38
  219.2 47.2 %collective-permute-start.52 = (bf16[512,1024]{1,0:T(8,128)(2,1)S(1)}, bf16[512,1024]{1,0:T(8,128)(2,1)S(1)}, u32[]{:S(2)}, u32[]{:S(2)}) collective-permute-start(bf16[512,1024]{1,0:T(8,128)(2,1)S(1)} %grad_shard.3), channel_id=1, source_target_pairs={{0,16},{16,0},{1,17},{17,1},{2,18},{18,2},{3,19},{19,3},{4,20},{20... | collective-permute-start | bytes 3145736 | tf_op jit(solution)/shard_map/ppermute | solution.py:38
  219.8 8.1 %collective-permute-start.54 = (f32[24,1024]{1,0:T(8,128)S(1)}, f32[24,1024]{1,0:T(8,128)S(1)}, u32[]{:S(2)}, u32[]{:S(2)}) collective-permute-start(f32[24,1024]{1,0:T(8,128)S(1)} %tally.1), channel_id=1, source_target_pairs={{0,4},{4,0},{8,12},{12,8},{1,5},{5,1},{9,13},{13,9},{2,6},{6,2},{1... | collective-permute-start | bytes 294920 | tf_op jit(solution)/shard_map/ppermute | solution.py:38
  223.3 12.4 %collective-permute-start.51 = (bf16[256,1024]{1,0:T(8,128)(2,1)S(1)}, bf16[256,1024]{1,0:T(8,128)(2,1)S(1)}, u32[]{:S(2)}, u32[]{:S(2)}) collective-permute-start(bf16[256,1024]{1,0:T(8,128)(2,1)S(1)} %get-tuple-element.339.mine_ref), channel_id=1, source_target_pairs={{0,2},{1,3},{2,0},{3,1},{4,6},{5,7},{6,4},{7,5},{8,10},{9,11},{10,... | collective-permute-start | bytes 1572872 | tf_op jit(solution)/shard_map/ppermute | solution.py:38
  224.9 22.6 %collective-permute-start.46 = (bf16[128,2048]{1,0:T(8,128)(2,1)S(1)}, bf16[128,2048]{1,0:T(8,128)(2,1)S(1)}, u32[]{:S(2)}, u32[]{:S(2)}) collective-permute-start(bf16[128,2048]{1,0:T(8,128)(2,1)S(1)} %get-tuple-element.330), channel_id=1, source_target_pairs={{0,4},{4,0},{8,12},{12,8},{1,5},{5,1},{9,13},{13,9},{2,6},{6,2},{1... | collective-permute-start | bytes 1572872 | tf_op jit(solution)/shard_map/ppermute | solution.py:38
  224.9 40.4 %collective-permute-start.47 = (bf16[128,2048]{1,0:T(8,128)(2,1)S(1)}, bf16[128,2048]{1,0:T(8,128)(2,1)S(1)}, u32[]{:S(2)}, u32[]{:S(2)}) collective-permute-start(bf16[128,2048]{1,0:T(8,128)(2,1)S(1)} %get-tuple-element.331), channel_id=1, source_target_pairs={{0,8},{4,12},{8,0},{12,4},{1,9},{5,13},{9,1},{13,5},{2,10},{6,14},... | collective-permute-start | bytes 1572872 | tf_op jit(solution)/shard_map/ppermute | solution.py:38
  227.9 37.4 %collective-permute-start.48 = (bf16[128,2048]{1,0:T(8,128)(2,1)S(1)}, bf16[128,2048]{1,0:T(8,128)(2,1)S(1)}, u32[]{:S(2)}, u32[]{:S(2)}) collective-permute-start(bf16[128,2048]{1,0:T(8,128)(2,1)S(1)} %get-tuple-element.332), channel_id=1, source_target_pairs={{0,12},{4,8},{8,4},{12,0},{1,13},{5,9},{9,5},{13,1},{2,14},{6,10},... | collective-permute-start | bytes 1572872 | tf_op jit(solution)/shard_map/ppermute | solution.py:38
  235.8 45.0 %collective-permute-start.55 = (f32[24,1024]{1,0:T(8,128)S(1)}, f32[24,1024]{1,0:T(8,128)S(1)}, u32[]{:S(2)}, u32[]{:S(2)}) collective-permute-start(f32[24,1024]{1,0:T(8,128)S(1)} %add.39), channel_id=1, source_target_pairs={{0,8},{4,12},{8,0},{12,4},{1,9},{5,13},{9,1},{13,5},{2,10},{6,14},... | collective-permute-start | bytes 294920 | tf_op jit(solution)/shard_map/ppermute | solution.py:38
  247.5 40.2 %collective-permute-start.53 = (f32[2,256,1024]{2,1,0:T(8,128)S(1)}, f32[2,256,1024]{2,1,0:T(8,128)S(1)}, u32[]{:S(2)}, u32[]{:S(2)}) collective-permute-start(f32[2,256,1024]{2,1,0:T(8,128)S(1)} %last.3.own_ref), channel_id=1, source_target_pairs={{0,1},{1,0},{2,3},{3,2},{4,5},{5,4},{6,7},{7,6},{8,9},{9,8},{10,11... | collective-permute-start | bytes 6291464 | tf_op jit(solution)/shard_map/ppermute | solution.py:38
  268.1 27.2 %collective-permute-start.59 = (bf16[128,1024]{1,0:T(8,128)(2,1)S(1)}, bf16[128,1024]{1,0:T(8,128)(2,1)S(1)}, u32[]{:S(2)}, u32[]{:S(2)}) collective-permute-start(bf16[128,1024]{1,0:T(8,128)(2,1)S(1)} %get-tuple-element.352), channel_id=1, source_target_pairs={{0,4},{4,0},{8,12},{12,8},{1,5},{5,1},{9,13},{13,9},{2,6},{6,2},{1... | collective-permute-start | bytes 786440 | tf_op jit(solution)/shard_map/ppermute | solution.py:38
  278.3 19.3 %collective-permute-start.60 = (bf16[128,1024]{1,0:T(8,128)(2,1)S(1)}, bf16[128,1024]{1,0:T(8,128)(2,1)S(1)}, u32[]{:S(2)}, u32[]{:S(2)}) collective-permute-start(bf16[128,1024]{1,0:T(8,128)(2,1)S(1)} %get-tuple-element.353), channel_id=1, source_target_pairs={{0,8},{4,12},{8,0},{12,4},{1,9},{5,13},{9,1},{13,5},{2,10},{6,14},... | collective-permute-start | bytes 786440 | tf_op jit(solution)/shard_map/ppermute | solution.py:38
  279.3 18.3 %collective-permute-start.61 = (bf16[128,1024]{1,0:T(8,128)(2,1)S(1)}, bf16[128,1024]{1,0:T(8,128)(2,1)S(1)}, u32[]{:S(2)}, u32[]{:S(2)}) collective-permute-start(bf16[128,1024]{1,0:T(8,128)(2,1)S(1)} %get-tuple-element.354), channel_id=1, source_target_pairs={{0,12},{4,8},{8,4},{12,0},{1,13},{5,9},{9,5},{13,1},{2,14},{6,10},... | collective-permute-start | bytes 786440 | tf_op jit(solution)/shard_map/ppermute | solution.py:38
  280.8 1.4 collective-permute-start.56
  282.1 4.9 %collective-permute-start.57 = (f32[24,1024]{1,0:T(8,128)S(1)}, f32[24,1024]{1,0:T(8,128)S(1)}, u32[]{:S(2)}, u32[]{:S(2)}) collective-permute-start(f32[24,1024]{1,0:T(8,128)S(1)} %add.41), channel_id=1, source_target_pairs={{0,16},{16,0},{1,17},{17,1},{2,18},{18,2},{3,19},{19,3},{4,20},{20... | collective-permute-start | bytes 294920 | tf_op jit(solution)/shard_map/ppermute | solution.py:38
  287.1 5.6 %collective-permute-start.58 = (f32[8,1024]{1,0:T(8,128)S(1)}, f32[8,1024]{1,0:T(8,128)S(1)}, u32[]{:S(2)}, u32[]{:S(2)}) collective-permute-start(f32[8,1024]{1,0:T(8,128)S(1)} %slice.22), channel_id=1, source_target_pairs={{0,2},{1,3},{2,0},{3,1},{4,6},{5,7},{6,4},{7,5},{8,10},{9,11},{10,... | collective-permute-start | bytes 98312 | tf_op jit(solution)/shard_map/ppermute | solution.py:38
  (22 other events, 224.7 us)
